TPU v7x, 32 devices: a whole 2x2x4 slice. The times are simulated.
32 devices in a mesh: groups: 2 (over y), area: 8 (over z, x), unit: 2 (over core).
Axes of the slice: x: 2, y: 2, z: 4, core: 2. Of those that a mesh axis runs over, the one named last changes fastest.
Arguments:
- state_start: float32 [64, 65536], P(None, ('groups', 'area', 'unit')), parts along dimension 1, may hold values from -6 to 6
- history: bfloat16 [6, 64, 12288], P(None, None, ('groups', 'area', 'unit')), parts along dimension 2, may hold values from -0.8984375 to 0.8984375
- external: float32 [64, 65536], P(None, ('groups', 'area', 'unit')), parts along dimension 1, may hold values from -4 to 4
- leak: float32 [65536], P(('groups', 'area', 'unit')), parts along dimension 0, may hold values from 0.05 to 0.6
- w_rec: bfloat16 [4096, 65536], P(None, ('groups', 'area', 'unit')), parts along dimension 1, may hold values from -0.09375 to 0.09375
- w_in: bfloat16 [768, 65536], P(None, ('groups', 'area', 'unit')), parts along dimension 1, may hold values from -0.21875 to 0.21875
- sources: int32 [16, 6], P('groups'), parts along dimension 0, may hold values from -1 to 7, as said below
- delays: int32 [16, 6], P('groups'), parts along dimension 0, may hold values from 3 to 6
- gains: float32 [16, 6], P('groups'), parts along dimension 0, may hold values from 0.3 to 1.5
- proj_units: int32 [12288], P(('groups', 'area', 'unit')), parts along dimension 0, may hold values from 0 to 4095, as said below
Outputs:
- state_end: float32 [64, 65536], P(None, ('groups', 'area', 'unit')), parts along dimension 1
- produced: bfloat16 [6, 64, 12288], P(None, None, ('groups', 'area', 'unit')), parts along dimension 2
There are 2 independent parts, one for each index of `groups`. A program takes and returns all parts, laid end to end along the dimension named above; each array names one. Nothing has to cross between parts.
Inputs may be any that keep to these rules, and one draw needn't show every extreme that they name: Row a names, in its first 2 to 6 entries, distinct source areas other than a; its other entries are -1. Some row has 6 sources and some row 2, at rows drawn from the seed. `proj_units`: the 768 entries of one area are distinct units of that area.
All inputs are finite; a program needn't handle non-finite values.
Results may differ from a plain program's by a relative error of at most 0.0023.
Values may be sent and summed in bfloat16 or wider, within the bound.
No kernel may reach another device: no remote copies, remote signals or barrier semaphores. Data moves between devices by JAX's collectives and lax.ppermute only.
A program may use at most 64 MiB of HBM per device.

v0:
```python
import functools

import jax
import jax.numpy as jnp
from jax import lax
from jax.experimental import pallas as pl
from jax.experimental.pallas import tpu as pltpu
from jax.sharding import PartitionSpec as P

MAXSRC = 6
WIN = 3
WINDOWS = 2
STEPS = WIN * WINDOWS
BF16 = jnp.bfloat16
F32 = jnp.float32
VM = pl.BlockSpec(memory_space=pltpu.VMEM)
SM = pl.BlockSpec(memory_space=pltpu.SMEM)
HB = pl.BlockSpec(memory_space=pltpu.MemorySpace.HBM)
LAGS = range(WIN, 2 * WIN + 1)
MIB = 1 << 20
CODE = 8192.0


def swapped(value, axis, stride):
    mask = 2**stride
    return crossed(value, axis, mask)


def crossed(value, axis, mask):
    pairs = [(source, source ^ mask) for source in range(lax.axis_size(axis))]
    return lax.ppermute(value, axis, pairs)


def shaped(shape, kind):
    return jax.ShapeDtypeStruct(shape, kind)


def params(limit=8):
    return pltpu.CompilerParams(vmem_limit_bytes=limit * MIB)


def columns_of(width):
    size = 256 if width % 256 == 0 else width
    return [slice(start, start + size) for start in range(0, width, size)]


def matmul(left, right):
    return jnp.dot(left, right, preferred_element_type=F32)


def far(array):
    return pltpu.with_memory_space_constraint(array, pltpu.MemorySpace.HBM)


def half_of(unit, count):
    return pl.ds(pl.multiple_of(unit * count, count), count)


def started(moves, sems):
    found = []
    for index, (source, target) in enumerate(moves):
        found.append(pltpu.make_async_copy(source, target, sems.at[index]))
        found[-1].start()
    return found


def stage_kernel(
    lines,
    area_ref,
    unit_ref,
    src_ref,
    delay_ref,
    gain_ref,
    units_ref,
    history_far,
    rec_far,
    in_far,
    history_ref,
    rec_ref,
    in_own_ref,
    in_other_ref,
    own_ref,
    other_ref,
    coef_ref,
    sems,
):
    area, unit = area_ref[0], unit_ref[0]
    count = rec_ref.shape[0]
    part = in_own_ref.shape[0]
    moves = started(
        [
            (history_far, history_ref),
            (rec_far.at[half_of(unit, count), :], rec_ref),
            (in_far.at[half_of(unit, part), :], in_own_ref),
            (in_far.at[half_of(1 - unit, part), :], in_other_ref),
        ],
        sems,
    )
    width = coef_ref.shape[1]
    row = 0
    for line in range(lines):
        target = area ^ (2 * line)
        for who in range(2):
            source = area ^ who
            delay, gain = jnp.int32(0), jnp.float32(0.0)
            for slot in range(MAXSRC):
                match = src_ref[target, slot] == source
                delay += jnp.where(match, delay_ref[target, slot], 0)
                gain += jnp.where(match, gain_ref[target, slot], 0.0)
            for lag in LAGS:
                value = jnp.where(delay == lag, gain, 0.0)
                coef_ref[row : row + 1, :] = jnp.full((1, width), value, F32)
                row += 1
    units = units_ref[...].reshape(1, width)
    for half, ref in ((unit, own_ref), (1 - unit, other_ref)):
        block = 256 if count % 256 == 0 else count
        for start in range(0, count, block):
            ids = lax.broadcasted_iota(jnp.int32, (block, width), 0) + (start + half * count)
            ref[start : start + block, :] = jnp.where(ids == units, 1.0, 0.0).astype(BF16)
    for move in moves:
        move.wait()


def stage(area, unit, tables, units, history, w_rec, w_in, lines):
    part = units.shape[0]
    count = w_rec.shape[0] // 2
    return pl.pallas_call(
        functools.partial(stage_kernel, lines),
        out_shape=(
            pltpu.VMEM(history.shape, BF16),
            pltpu.VMEM((count, w_rec.shape[1]), BF16),
            pltpu.VMEM((w_in.shape[0] // 2, w_in.shape[1]), BF16),
            pltpu.VMEM((w_in.shape[0] // 2, w_in.shape[1]), BF16),
            pltpu.VMEM((count, part), BF16),
            pltpu.VMEM((count, part), BF16),
            pltpu.VMEM((lines * 2 * len(LAGS), part), F32),
        ),
        in_specs=[SM] * 5 + [VM] + [HB] * 3,
        out_specs=(VM,) * 7,
        scratch_shapes=[pltpu.SemaphoreType.DMA((4,))],
        compiler_params=params(),
        name="stage",
    )(area, unit, *[far(table) for table in tables], far(units), far(history), far(w_rec), far(w_in))


def opening_kernel(
    unit_ref,
    rates_ref,
    facing_ref,
    own_ref,
    pick_own_ref,
    pick_other_ref,
    rec_far,
    extra_far,
    state_far,
    leak_far,
    other_ref,
    extra_ref,
    state_ref,
    leak_ref,
    out_ref,
    pick_ref,
    sems,
):
    unit = unit_ref[0]
    count = other_ref.shape[0]
    size = count // 2 if count % 512 == 0 else count
    spans = [slice(start, start + size) for start in range(0, count, size)]
    moves = [
        (rec_far.at[pl.ds(pl.multiple_of((1 - unit) * count + span.start, size), size), :], other_ref.at[span, :])
        for span in spans
    ]
    moves += [
        (extra_far, extra_ref),
        (state_far, state_ref),
        (leak_far, leak_ref),
    ]
    moves = started(moves, sems)
    for cols in columns_of(out_ref.shape[1]):
        out_ref[:, cols] = matmul(rates_ref[...], own_ref[:, cols])
    picked = matmul(rates_ref[...], pick_own_ref[...])
    picked += matmul(facing_ref[...], pick_other_ref[...])
    pick_ref[...] = picked.astype(BF16)
    for move, span in zip(moves, spans):
        move.wait()
        for cols in columns_of(out_ref.shape[1]):
            out_ref[:, cols] += matmul(facing_ref[:, span], other_ref[span, cols])
    for move in moves[len(spans) :]:
        move.wait()
    out_ref[...] += extra_ref[...]


def opening(unit, rates, facing, own, selects, w_rec, extra, state, leak):
    part = selects[0].shape[1]
    return pl.pallas_call(
        opening_kernel,
        out_shape=(
            pltpu.VMEM(own.shape, BF16),
            pltpu.VMEM(extra.shape, F32),
            pltpu.VMEM(state.shape, F32),
            pltpu.VMEM(leak.shape, F32),
            pltpu.VMEM(extra.shape, F32),
            pltpu.VMEM((rates.shape[0], part), BF16),
        ),
        in_specs=[SM] + [VM] * 5 + [HB] * 4,
        out_specs=(VM,) * 6,
        scratch_shapes=[pltpu.SemaphoreType.DMA((5,))],
        compiler_params=params(),
        name="opening",
    )(unit, rates, facing, own, *selects, *[far(array) for array in (w_rec, extra, state, leak)])


def pick_kernel(count, *refs):
    owns, others, (pick_own_ref, pick_other_ref, out_ref) = refs[:count], refs[count : 2 * count], refs[2 * count :]
    left = jnp.concatenate([ref[...] for ref in owns], axis=0)
    right = jnp.concatenate([ref[...] for ref in others], axis=0)
    picked = matmul(left, pick_own_ref[...]) + matmul(right, pick_other_ref[...])
    out_ref[...] = picked.astype(BF16).reshape(out_ref.shape)


def pick(pairs, selects):
    owns, others = zip(*pairs)
    return pl.pallas_call(
        functools.partial(pick_kernel, len(pairs)),
        out_shape=shaped((len(pairs), owns[0].shape[0], selects[0].shape[1]), BF16),
        in_specs=[VM] * (2 * len(pairs) + 2),
        out_specs=VM,
        compiler_params=params(),
        name="pick",
    )(*owns, *others, *selects)


def own_kernel(rates_ref, weight_ref, extra_ref, out_ref):
    for cols in columns_of(out_ref.shape[1]):
        out_ref[:, cols] = extra_ref[:, cols] + matmul(rates_ref[...], weight_ref[:, cols])


def own_part(rates, weight, extra):
    return pl.pallas_call(
        own_kernel,
        out_shape=shaped(extra.shape, F32),
        in_specs=[VM] * 3,
        out_specs=VM,
        compiler_params=params(),
        name="own_part",
    )(rates, weight, extra)


def renewed(cols, total, state_ref, leak_ref):
    state = state_ref[:, cols]
    return state + leak_ref[:, cols] * (total - state)


def step_kernel(flow, drives, last, sum_ref, state_ref, leak_ref, *refs):
    refs = list(refs)
    rates_ref, weight_ref = (refs.pop(0), refs.pop(0)) if flow else (None, None)
    if drives:
        d0_ref, d1_ref, i0_ref, i1_ref = (refs.pop(0) for _ in range(4))
    else:
        kept_ref = refs.pop(0)
    trials = state_ref.shape[0]
    moves = []

    def send(source, target):
        moves.append(pltpu.make_async_copy(source, target, sems.at[len(moves)]))
        moves[-1].start()

    if last:
        sems, state_buf, fresh, new_ref, all_ref = (refs.pop(index) for index in (-1, -1, -1, -2, -1))
        pick_own_ref, pick_other_ref, first_ref, second_ref = (refs.pop(0) for _ in range(4))
        count = len(refs) // 2
        old = 0
        for ref in (first_ref, second_ref):
            send(ref, all_ref.at[pl.ds(old, ref.shape[0])])
            old += ref.shape[0]
        left = jnp.concatenate([ref[...] for ref in refs[:count]], axis=0)
        right = jnp.concatenate([ref[...] for ref in refs[count:]], axis=0)
        picked = matmul(left, pick_own_ref[...]) + matmul(right, pick_other_ref[...])
        fresh[...] = picked.astype(BF16).reshape(fresh.shape)
        send(fresh, all_ref.at[pl.ds(old, fresh.shape[0])])
    else:
        state_buf, next_ref = refs[:2]
    for cols in columns_of(state_buf.shape[1]):
        total = sum_ref[:, cols]
        if flow:
            total += matmul(rates_ref[...], weight_ref[:, cols])
        if drives:
            current = matmul(d0_ref[...], i0_ref[:, cols]) + matmul(d1_ref[...], i1_ref[:, cols])
            refs[2][:, cols] = current[trials:, :]
            total += current[:trials, :]
        else:
            total += kept_ref[:, cols]
        state = renewed(cols, total, state_ref, leak_ref)
        state_buf[:, cols] = state
        if last:
            send(state_buf.at[:, cols], new_ref.at[:, cols])
        else:
            next_ref[:, cols] = jnp.tanh(state).astype(BF16)
    for move in moves:
        move.wait()


def step(total, state, leak, flow, drives, kept):
    outs = [shaped(state.shape, F32), shaped(state.shape, BF16)]
    given = list(flow or ())
    if drives:
        given += drives
        outs.append(shaped(state.shape, F32))
    else:
        given.append(kept)
    return pl.pallas_call(
        functools.partial(step_kernel, flow is not None, drives is not None, False),
        out_shape=tuple(outs),
        in_specs=[VM] * (3 + len(given)),
        out_specs=(VM,) * len(outs),
        compiler_params=params(),
        name="step",
    )(total, state, leak, *given)


def last_step(total, state, leak, flow, kept, selects, old, pairs):
    owns, others = zip(*pairs)
    trials, part = old[0].shape[1:]
    first = sum(value.shape[0] for value in old)
    given = [*flow, kept, *selects, *old, *owns, *others]
    return pl.pallas_call(
        functools.partial(step_kernel, True, False, True),
        out_shape=(shaped(state.shape, F32), shaped((first + len(pairs), trials, part), BF16)),
        in_specs=[VM] * (3 + len(given)),
        out_specs=(HB, HB),
        scratch_shapes=[
            pltpu.VMEM((len(pairs), trials, part), BF16),
            pltpu.VMEM(state.shape, F32),
            pltpu.SemaphoreType.DMA((len(old) + 1 + len(columns_of(state.shape[1])),)),
        ],
        compiler_params=params(),
        name="last_step",
    )(total, state, leak, *given)


def coded(value):
    return jnp.round(value * CODE).astype(jnp.int32).astype(jnp.int16)


def decoded(value):
    return value.astype(jnp.int32).astype(F32) * (1.0 / CODE)


def partial_kernel(times, lines, slots, coef_ref, *refs):
    fields, outs = refs[: len(slots)], refs[len(slots) :]
    trials = fields[0].shape[-2]
    size = 16 if trials % 16 == 0 else trials
    spans = {}
    for ref, (who, first) in zip(fields, slots):
        for pos in range(ref.shape[0]):
            spans[who, first + pos] = (ref, pos)
    for start in range(0, trials, size):
        band = slice(start, start + size)
        for index, time in enumerate(times):
            totals = [None] * lines
            for who in range(2):
                for lag in LAGS:
                    ref, pos = spans[who, time - lag]
                    value = ref[pos, band, :].astype(F32)
                    for line in range(lines):
                        row = (line * 2 + who) * len(LAGS) + lag - WIN
                        term = coef_ref[row : row + 1, :] * value
                        totals[line] = term if totals[line] is None else totals[line] + term
            for line in range(lines):
                outs[line][index, band, :] = totals[line] if line == 0 else coded(totals[line])


def partials(coef, times, lines, fields):
    shape = (len(times),) + fields[0][2].shape[1:]
    outs = [shaped(shape, F32)] + [shaped(shape, jnp.int16)] * (lines - 1)
    return pl.pallas_call(
        functools.partial(partial_kernel, times, lines, [field[:2] for field in fields]),
        out_shape=tuple(outs),
        in_specs=[VM] * (1 + len(fields)),
        out_specs=(VM,) * len(outs),
        compiler_params=params(),
        name="partials",
    )(coef, *[field[2] for field in fields])


def drive_kernel(own_ref, *refs):
    total = own_ref[...]
    for ref in refs[:-1]:
        total += decoded(ref[...])
    refs[-1][...] = total.astype(BF16).reshape(refs[-1].shape)


def drive_of(own, arrived):
    span, trials, part = own.shape
    return pl.pallas_call(
        drive_kernel,
        out_shape=shaped((span * trials, part), BF16),
        in_specs=[VM] * (1 + len(arrived)),
        out_specs=VM,
        compiler_params=params(),
        name="drive",
    )(own, *arrived)


def body(*args):
    return narrow_body(*args)


def narrow_body(state_start, history, external, leak, w_rec, w_in, sources, delays, gains, proj_units):
    area = lax.axis_index("area").astype(jnp.int32).reshape(1)
    unit = lax.axis_index("unit").astype(jnp.int32).reshape(1)
    lines = lax.axis_size("area") // 2
    leak_row = leak.reshape(1, -1)

    facing = crossed(history, "area", 1)
    rates = jnp.tanh(state_start).astype(BF16)
    other = crossed(rates, "unit", 1)
    history, rec_own, in_own, in_other, select_own, select_other, coef = stage(
        area, unit, (sources, delays, gains), proj_units, history, w_rec, w_in, lines
    )
    selects = (select_own, select_other)
    known = [(0, -2 * WIN, history), (1, -2 * WIN, facing)]

    def send(times):
        sums = partials(coef, times, lines, known)
        arrived = []
        for line in range(1, lines):
            arrived.append(crossed(sums[line], "area", 2 * line))
        return sums[0], arrived

    def drive_pair(group):
        own = drive_of(*group)
        return [own, crossed(own, "unit", 1), in_own, in_other]

    def share(value, first):
        return [(0, first, value), (1, first, crossed(value, "area", 1))]

    sent = send((0, 1))
    rec_other, external, state, leak_row, total, fresh = opening(
        unit, rates, other, rec_own, selects, w_rec, external, state_start, leak_row
    )
    known += share(fresh[None], 0)
    old, pairs, flow, kept = [fresh[None]], [], None, None
    for time in range(STEPS):
        if time > 0:
            other = crossed(rates, "unit", 1)
            pairs.append((rates, other))
            flow = (other, rec_other)
            if time == 2:
                fresh = pick(pairs, selects)
                old.append(fresh)
                pairs = []
                known += share(fresh, 1)
            total = own_part(rates, rec_own, external)
        if time == STEPS - 1:
            return last_step(total, state, leak_row, flow, kept, selects, old, pairs)
        drives = drive_pair(sent) if time % 2 == 0 else None
        if time in (0, 2):
            sent = send((time + 2, time + 3))
        state, rates, *more = step(total, state, leak_row, flow, drives, kept)
        kept = more[0] if more else None


def wide_body(state_start, history, external, leak, w_rec, w_in, sources, delays, gains, proj_units):
    area_count = lax.axis_size("area")
    area_index = lax.axis_index("area")
    area_total = sources.shape[0]
    share = area_count // area_total
    own_area = area_index // share
    own_src = lax.dynamic_slice_in_dim(sources, own_area, 1, 0)[0]
    own_delay = lax.dynamic_slice_in_dim(delays, own_area, 1, 0)[0]
    own_gain = lax.dynamic_slice_in_dim(gains, own_area, 1, 0)[0]
    own_valid = own_src >= 0
    trial_count = state_start.shape[0]
    proj_part = proj_units.shape[0]
    unit_full = w_rec.shape[0]
    proj_full = w_in.shape[0]
    bit_count = share.bit_length() - 1
    select = (jnp.arange(unit_full, dtype=jnp.int32)[:, None] == proj_units[None, :]).astype(BF16)
    state_now = state_start
    received = []
    outgoing = history
    produced = []
    for window_idx in range(WINDOWS):
        move_span_len = outgoing.shape[0]
        flat = outgoing.reshape(1, -1)
        wanted = (own_src[:, None] * share + jnp.arange(share, dtype=jnp.int32)[None, :]).reshape(-1)
        piece = lax.all_gather(flat, "area", axis=0, tiled=True)
        count = piece.shape[0]
        match = wanted[:, None] == jnp.arange(count, dtype=jnp.int32)[None, :]
        total = jnp.dot(match.astype(BF16), piece, preferred_element_type=F32)
        received.append(
            total.astype(BF16).reshape(MAXSRC, share, move_span_len, trial_count, proj_part)
        )
        known = jnp.concatenate(received, axis=2)
        span_len = known.shape[2]
        times = window_idx * WIN + jnp.arange(WIN, dtype=jnp.int32)
        target_idx = times[:, None] - own_delay[None, :] + 2 * WIN
        columns = jnp.arange(span_len, dtype=jnp.int32)
        chosen_steps = (columns[None, None, :] == target_idx[:, :, None]) & own_valid[None, :, None]
        weight = jnp.where(chosen_steps, own_gain[None, :, None], jnp.float32(0.0))
        summed = jnp.einsum(
            "ikj,kqjbp->ibqp", weight, known.astype(F32), precision=lax.Precision.HIGHEST
        )
        drive_part = summed.astype(BF16)
        drive_full = lax.all_gather(drive_part[:, :, :, None, :], "unit", axis=3, tiled=True)
        current = jnp.dot(
            drive_full.reshape(WIN * trial_count, proj_full), w_in, preferred_element_type=F32
        )
        current = current.reshape(WIN, trial_count, -1)
        fresh = []
        for inner_step in range(WIN):
            rate_rows = jnp.tanh(state_now).astype(BF16)
            joined = lax.all_gather(rate_rows, "unit", axis=1, tiled=True)
            for bit in range(bit_count):
                other = swapped(joined, "area", bit)
                upper = area_index // (1 << bit) % 2 == 1
                joined = jnp.where(
                    upper,
                    jnp.concatenate([other, joined], axis=1),
                    jnp.concatenate([joined, other], axis=1),
                )
            recur = jnp.dot(joined, w_rec, preferred_element_type=F32)
            picked = jnp.dot(joined, select, preferred_element_type=F32)
            fresh.append(picked.astype(BF16))
            state_now = state_now + leak[None, :] * (
                -state_now + recur + current[inner_step] + external
            )
        outgoing = jnp.stack(fresh)
        produced.append(outgoing)
    return (state_now, jnp.concatenate(produced, axis=0))


def solution(mesh):
    split = P(None, ("groups", "area", "unit"))
    placed = (
        split,
        P(None, None, ("groups", "area", "unit")),
        split,
        P(("groups", "area", "unit")),
        split,
        split,
        P("groups", None),
        P("groups", None),
        P("groups", None),
        P(("groups", "area", "unit")),
    )

    def chosen(*args):
        areas = lax.axis_size("area")
        narrow = args[6].shape[0] == areas and lax.axis_size("unit") == 2 and areas & (areas - 1) == 0
        return (body if narrow else wide_body)(*args)

    return jax.shard_map(
        chosen,
        mesh=mesh,
        in_specs=placed,
        out_specs=(split, P(None, None, ("groups", "area", "unit"))),
        check_vma=False,
    )
```

profile of v0, /device:TPU:0, one launch (start us, length us, event | category | flops | bytes accessed | tf_op | source)
XLA Modules:
  0.0 81.0 jit_solution(14006578466219369027)
XLA Ops:
  0.6 3.0 %collective-permute-start.1 = (bf16[6,64,384]{2,1,0:T(8,128)(2,1)}, bf16[6,64,384]{2,1,0:T(8,128)(2,1)S(1)}, u32[]{:S(2)}, u32[]{:S(2)}) collective-permute-start(bf16[6,64,384]{2,1,0:T(8,128)(2,1)} %history_far.1), channel_id=1, source_target_pairs={{0,2},{2,0},{4,6},{6,4},{8,10},{10,8},{12,14},{14,12},{1,3},{3,1},... | collective-permute-start | bytes 884744 | tf_op jit(solution)/shard_map/ppermute | solution.py:31
  3.7 1.1 %tanh_convert_fusion.rates_ref = bf16[64,2048]{1,0:T(8,128)(2,1)S(1)} fusion(f32[64,2048]{1,0:T(8,128)} %state_far.1), kind=kLoop, calls=%fused_computation | loop fusion | flops 131072 | bytes 786432 | tf_op jit(solution)/shard_map/convert_element_type | solution.py:416
  4.8 0.1 collective-permute-start
  4.9 5.3 %stage.1 = (bf16[6,64,384]{2,1,0:T(8,128)(2,1)S(1)}, bf16[2048,2048]{1,0:T(8,128)(2,1)S(1)}, bf16[384,2048]{1,0:T(8,128)(2,1)S(1)}, bf16[384,2048]{1,0:T(8,128)(...) custom-call(s32[1]{0:T(128)} %bitcast.1.area_ref, s32[1]{0:T(128)} %bitcast.unit_ref, ...), custom_call_target="tpu_custom_call" | custom-call | tf_op jit(solution)/shard_map/stage/pallas_call | solution.py:127
  10.1 0.8 collective-permute-done.1.refs_1_
  10.9 0.6 partials.3
  11.5 1.9 %collective-permute-start.2 = (s16[2,64,384]{2,1,0:T(8,128)(2,1)S(1)}, s16[2,64,384]{2,1,0:T(8,128)(2,1)S(1)}, u32[]{:S(2)}, u32[]{:S(2)}) collective-permute-start(s16[2,64,384]{2,1,0:T(8,128)(2,1)S(1)} %get-tuple-element.49), channel_id=1, source_target_pairs={{0,4},{2,6},{4,0},{6,2},{8,12},{10,14},{12,8},{14,10},{1,5},{3,7},... | collective-permute-start | bytes 294920 | tf_op jit(solution)/shard_map/ppermute | solution.py:31
  13.4 2.6 %collective-permute-start.3 = (s16[2,64,384]{2,1,0:T(8,128)(2,1)S(1)}, s16[2,64,384]{2,1,0:T(8,128)(2,1)S(1)}, u32[]{:S(2)}, u32[]{:S(2)}) collective-permute-start(s16[2,64,384]{2,1,0:T(8,128)(2,1)S(1)} %get-tuple-element.50), channel_id=1, source_target_pairs={{0,8},{2,10},{4,12},{6,14},{8,0},{10,2},{12,4},{14,6},{1,9},{3,11}... | collective-permute-start | bytes 294920 | tf_op jit(solution)/shard_map/ppermute | solution.py:31
  16.0 0.2 collective-permute-done.2.refs_0_
  16.2 7.3 %collective-permute-done.3.refs_1_ = s16[2,64,384]{2,1,0:T(8,128)(2,1)S(1)} collective-permute-done((s16[2,64,384]{2,1,0:T(8,128)(2,1)S(1)}, s16[2,64,384]{2,1,0:T(8,128)(2,1)S(1)}, u32[]{:S(2)}, u32[]{:S(2)}) %collective-permute-start.3) | collective-permute-done | bytes 98336 | tf_op jit(solution)/shard_map/ppermute | solution.py:31
  23.5 0.1 drive.3.refs_0_
  23.5 0.1 collective-permute-start.5
  23.6 5.1 %opening.1 = (bf16[2048,2048]{1,0:T(8,128)(2,1)S(1)}, f32[64,2048]{1,0:T(8,128)S(1)}, f32[64,2048]{1,0:T(8,128)S(1)}, f32[1,2048]{1,0:T(1,128)S(1)}, f32[64,2048...) custom-call(s32[1]{0:T(128)} %bitcast.unit_ref, bf16[64,2048]{1,0:T(8,128)(2,1)S(1)} %tanh_convert_fusion.rates_ref, ...), custom_call_target="tpu_custom_call" | custom-call | tf_op jit(solution)/shard_map/opening/pallas_call | solution.py:195
  28.7 0.7 step.5
  29.5 0.5 collective-permute-start.6
  30.0 1.6 %own_part.5.sum_ref = f32[64,2048]{1,0:T(8,128)S(1)} custom-call(bf16[64,2048]{1,0:T(8,128)(2,1)S(1)} %get-tuple-element.54.rates_ref.refs_0_, bf16[2048,2048]{1,0:T(8,128)(2,1)S(1)} %get-tuple-element.40.own_ref.weight_ref, f32[64,2048]{1,0:T(8,128)S(1)} %get-tuple-element.55.extra_ref), custom_call_target="tpu_custom_call" | custom-call | tf_op jit(solution)/shard_map/own_part/pallas_call | solution.py:239
  31.6 1.7 %step.6 = (f32[64,2048]{1,0:T(8,128)S(1)}, bf16[64,2048]{1,0:T(8,128)(2,1)S(1)}) custom-call(f32[64,2048]{1,0:T(8,128)S(1)} %own_part.5.sum_ref, f32[64,2048]{1,0:T(8,128)S(1)} %get-tuple-element.56.state_ref, f32[1,2048]{1,0:T(1,128)S(1)} %get-tuple-element.45.leak_ref, bf16[64,2048]{1,0:T(8,128)(2,1)S(1)} %collective-permute-done.6.refs_0_.refs_2_, ...), custom_call_target="tpu_custom_call" | custom-call | tf_op jit(solution)/shard_map/step/pallas_call | solution.py:311
  33.3 0.1 collective-permute-start.7
  33.4 1.0 %collective-permute-start.8 = (bf16[1,64,384]{2,1,0:T(8,128)(2,1)S(1)}, bf16[1,64,384]{2,1,0:T(8,128)(2,1)S(1)}, u32[]{:S(2)}, u32[]{:S(2)}) collective-permute-start(bf16[1,64,384]{2,1,0:T(8,128)(2,1)S(1)} %bitcast.4), channel_id=1, source_target_pairs={{0,2},{2,0},{4,6},{6,4},{8,10},{10,8},{12,14},{14,12},{1,3},{3,1},... | collective-permute-start | bytes 147464 | tf_op jit(solution)/shard_map/ppermute | solution.py:31
  34.4 3.1 %collective-permute-done.8.refs_3_ = bf16[1,64,384]{2,1,0:T(8,128)(2,1)S(1)} collective-permute-done((bf16[1,64,384]{2,1,0:T(8,128)(2,1)S(1)}, bf16[1,64,384]{2,1,0:T(8,128)(2,1)S(1)}, u32[]{:S(2)}, u32[]{:S(2)}) %collective-permute-start.8) | collective-permute-done | bytes 49184 | tf_op jit(solution)/shard_map/ppermute | solution.py:31
  37.5 0.6 partials.4
  38.1 2.7 %collective-permute-start.10 = (s16[2,64,384]{2,1,0:T(8,128)(2,1)S(1)}, s16[2,64,384]{2,1,0:T(8,128)(2,1)S(1)}, u32[]{:S(2)}, u32[]{:S(2)}) collective-permute-start(s16[2,64,384]{2,1,0:T(8,128)(2,1)S(1)} %get-tuple-element.64), channel_id=1, source_target_pairs={{0,8},{2,10},{4,12},{6,14},{8,0},{10,2},{12,4},{14,6},{1,9},{3,11}... | collective-permute-start | bytes 294920 | tf_op jit(solution)/shard_map/ppermute | solution.py:31
  40.8 1.3 %collective-permute-start.11 = (s16[2,64,384]{2,1,0:T(8,128)(2,1)S(1)}, s16[2,64,384]{2,1,0:T(8,128)(2,1)S(1)}, u32[]{:S(2)}, u32[]{:S(2)}) collective-permute-start(s16[2,64,384]{2,1,0:T(8,128)(2,1)S(1)} %get-tuple-element.65), channel_id=1, source_target_pairs={{0,12},{2,14},{4,8},{6,10},{8,4},{10,6},{12,0},{14,2},{1,13},{3,15... | collective-permute-start | bytes 294920 | tf_op jit(solution)/shard_map/ppermute | solution.py:31
  42.2 6.2 %collective-permute-done.10.refs_1_ = s16[2,64,384]{2,1,0:T(8,128)(2,1)S(1)} collective-permute-done((s16[2,64,384]{2,1,0:T(8,128)(2,1)S(1)}, s16[2,64,384]{2,1,0:T(8,128)(2,1)S(1)}, u32[]{:S(2)}, u32[]{:S(2)}) %collective-permute-start.10) | collective-permute-done | bytes 98336 | tf_op jit(solution)/shard_map/ppermute | solution.py:31
  48.4 0.4 collective-permute-done.9.refs_0_
  48.7 0.1 drive.4.refs_2_
  48.8 0.1 collective-permute-start.12
  48.9 1.6 %own_part.6.sum_ref = f32[64,2048]{1,0:T(8,128)S(1)} custom-call(bf16[64,2048]{1,0:T(8,128)(2,1)S(1)} %get-tuple-element.59.rates_ref.refs_1_, bf16[2048,2048]{1,0:T(8,128)(2,1)S(1)} %get-tuple-element.40.own_ref.weight_ref, f32[64,2048]{1,0:T(8,128)S(1)} %get-tuple-element.55.extra_ref), custom_call_target="tpu_custom_call" | custom-call | tf_op jit(solution)/shard_map/own_part/pallas_call | solution.py:239
  50.5 2.3 %step.7 = (f32[64,2048]{1,0:T(8,128)S(1)}, bf16[64,2048]{1,0:T(8,128)(2,1)S(1)}, f32[64,2048]{1,0:T(8,128)S(1)}) custom-call(f32[64,2048]{1,0:T(8,128)S(1)} %own_part.6.sum_ref, f32[64,2048]{1,0:T(8,128)S(1)} %get-tuple-element.60.state_ref, f32[1,2048]{1,0:T(1,128)S(1)} %get-tuple-element.45.leak_ref, ...), custom_call_target="tpu_custom_call" | custom-call | tf_op jit(solution)/shard_map/step/pallas_call | solution.py:311
  52.8 0.6 collective-permute-start.13
  53.4 0.9 %pick.1.refs_4_.refs_6_ = bf16[2,64,384]{2,1,0:T(8,128)(2,1)S(1)} custom-call(bf16[64,2048]{1,0:T(8,128)(2,1)S(1)} %get-tuple-element.54.rates_ref.refs_0_, bf16[64,2048]{1,0:T(8,128)(2,1)S(1)} %get-tuple-element.59.rates_ref.refs_1_, bf16[64,2048]{1,0:T(8,128)(2,1)S(1)} %collective-permute-done.6.refs_0_.refs_2_, ...), custom_call_target="tpu_custom_call" | custom-call | tf_op jit(solution)/shard_map/pick/pallas_call | solution.py:223
  54.3 1.0 %collective-permute-start.15 = (bf16[2,64,384]{2,1,0:T(8,128)(2,1)S(1)}, bf16[2,64,384]{2,1,0:T(8,128)(2,1)S(1)}, u32[]{:S(2)}, u32[]{:S(2)}) collective-permute-start(bf16[2,64,384]{2,1,0:T(8,128)(2,1)S(1)} %pick.1.refs_4_.refs_6_), channel_id=1, source_target_pairs={{0,2},{2,0},{4,6},{6,4},{8,10},{10,8},{12,14},{14,12},{1,3},{3,1},... | collective-permute-start | bytes 294920 | tf_op jit(solution)/shard_map/ppermute | solution.py:31
  55.3 1.6 %own_part.7.sum_ref = f32[64,2048]{1,0:T(8,128)S(1)} custom-call(bf16[64,2048]{1,0:T(8,128)(2,1)S(1)} %get-tuple-element.66.rates_ref.refs_7_, bf16[2048,2048]{1,0:T(8,128)(2,1)S(1)} %get-tuple-element.40.own_ref.weight_ref, f32[64,2048]{1,0:T(8,128)S(1)} %get-tuple-element.55.extra_ref), custom_call_target="tpu_custom_call" | custom-call | tf_op jit(solution)/shard_map/own_part/pallas_call | solution.py:239
  56.9 1.7 %step.8 = (f32[64,2048]{1,0:T(8,128)S(1)}, bf16[64,2048]{1,0:T(8,128)(2,1)S(1)}) custom-call(f32[64,2048]{1,0:T(8,128)S(1)} %own_part.7.sum_ref, f32[64,2048]{1,0:T(8,128)S(1)} %get-tuple-element.67.state_ref, f32[1,2048]{1,0:T(1,128)S(1)} %get-tuple-element.45.leak_ref, bf16[64,2048]{1,0:T(8,128)(2,1)S(1)} %collective-permute-done.13.refs_0_.refs_10_, ...), custom_call_target="tpu_custom_call" | custom-call | tf_op jit(solution)/shard_map/step/pallas_call | solution.py:311
  58.6 0.1 collective-permute-start.14
  58.7 0.4 collective-permute-done.15.refs_5_
  59.1 0.6 partials.5
  59.7 1.3 %collective-permute-start.16 = (s16[2,64,384]{2,1,0:T(8,128)(2,1)S(1)}, s16[2,64,384]{2,1,0:T(8,128)(2,1)S(1)}, u32[]{:S(2)}, u32[]{:S(2)}) collective-permute-start(s16[2,64,384]{2,1,0:T(8,128)(2,1)S(1)} %get-tuple-element.72), channel_id=1, source_target_pairs={{0,4},{2,6},{4,0},{6,2},{8,12},{10,14},{12,8},{14,10},{1,5},{3,7},... | collective-permute-start | bytes 294920 | tf_op jit(solution)/shard_map/ppermute | solution.py:31
  61.0 1.7 %collective-permute-start.17 = (s16[2,64,384]{2,1,0:T(8,128)(2,1)S(1)}, s16[2,64,384]{2,1,0:T(8,128)(2,1)S(1)}, u32[]{:S(2)}, u32[]{:S(2)}) collective-permute-start(s16[2,64,384]{2,1,0:T(8,128)(2,1)S(1)} %get-tuple-element.73), channel_id=1, source_target_pairs={{0,8},{2,10},{4,12},{6,14},{8,0},{10,2},{12,4},{14,6},{1,9},{3,11}... | collective-permute-start | bytes 294920 | tf_op jit(solution)/shard_map/ppermute | solution.py:31
  62.7 1.4 %collective-permute-start.18 = (s16[2,64,384]{2,1,0:T(8,128)(2,1)S(1)}, s16[2,64,384]{2,1,0:T(8,128)(2,1)S(1)}, u32[]{:S(2)}, u32[]{:S(2)}) collective-permute-start(s16[2,64,384]{2,1,0:T(8,128)(2,1)S(1)} %get-tuple-element.74), channel_id=1, source_target_pairs={{0,12},{2,14},{4,8},{6,10},{8,4},{10,6},{12,0},{14,2},{1,13},{3,15... | collective-permute-start | bytes 294920 | tf_op jit(solution)/shard_map/ppermute | solution.py:31
  64.1 1.6 %collective-permute-done.16.refs_0_ = s16[2,64,384]{2,1,0:T(8,128)(2,1)S(1)} collective-permute-done((s16[2,64,384]{2,1,0:T(8,128)(2,1)S(1)}, s16[2,64,384]{2,1,0:T(8,128)(2,1)S(1)}, u32[]{:S(2)}, u32[]{:S(2)}) %collective-permute-start.16) | collective-permute-done | bytes 98336 | tf_op jit(solution)/shard_map/ppermute | solution.py:31
  65.7 6.0 %collective-permute-done.17.refs_1_ = s16[2,64,384]{2,1,0:T(8,128)(2,1)S(1)} collective-permute-done((s16[2,64,384]{2,1,0:T(8,128)(2,1)S(1)}, s16[2,64,384]{2,1,0:T(8,128)(2,1)S(1)}, u32[]{:S(2)}, u32[]{:S(2)}) %collective-permute-start.17) | collective-permute-done | bytes 98336 | tf_op jit(solution)/shard_map/ppermute | solution.py:31
  71.7 0.1 drive.5.refs_2_
  71.9 1.6 %own_part.8.sum_ref = f32[64,2048]{1,0:T(8,128)S(1)} custom-call(bf16[64,2048]{1,0:T(8,128)(2,1)S(1)} %get-tuple-element.69.rates_ref.refs_8_, bf16[2048,2048]{1,0:T(8,128)(2,1)S(1)} %get-tuple-element.40.own_ref.weight_ref, f32[64,2048]{1,0:T(8,128)S(1)} %get-tuple-element.55.extra_ref), custom_call_target="tpu_custom_call" | custom-call | tf_op jit(solution)/shard_map/own_part/pallas_call | solution.py:239
  73.5 2.3 %step.9 = (f32[64,2048]{1,0:T(8,128)S(1)}, bf16[64,2048]{1,0:T(8,128)(2,1)S(1)}, f32[64,2048]{1,0:T(8,128)S(1)}) custom-call(f32[64,2048]{1,0:T(8,128)S(1)} %own_part.8.sum_ref, f32[64,2048]{1,0:T(8,128)S(1)} %get-tuple-element.70.state_ref, f32[1,2048]{1,0:T(1,128)S(1)} %get-tuple-element.45.leak_ref, ...), custom_call_target="tpu_custom_call" | custom-call | tf_op jit(solution)/shard_map/step/pallas_call | solution.py:311
  75.8 0.6 collective-permute-start.20
  76.3 1.6 %own_part.9.sum_ref = f32[64,2048]{1,0:T(8,128)S(1)} custom-call(bf16[64,2048]{1,0:T(8,128)(2,1)S(1)} %get-tuple-element.75.rates_ref.refs_9_, bf16[2048,2048]{1,0:T(8,128)(2,1)S(1)} %get-tuple-element.40.own_ref.weight_ref, f32[64,2048]{1,0:T(8,128)S(1)} %get-tuple-element.55.extra_ref), custom_call_target="tpu_custom_call" | custom-call | tf_op jit(solution)/shard_map/own_part/pallas_call | solution.py:239
  77.9 2.9 %last_step.1 = (f32[64,2048]{1,0:T(8,128)}, bf16[6,64,384]{2,1,0:T(8,128)(2,1)}) custom-call(f32[64,2048]{1,0:T(8,128)S(1)} %own_part.9.sum_ref, f32[64,2048]{1,0:T(8,128)S(1)} %get-tuple-element.76.state_ref, f32[1,2048]{1,0:T(1,128)S(1)} %get-tuple-element.45.leak_ref, bf16[64,2048]{1,0:T(8,128)(2,1)S(1)} %collective-permute-done.20.refs_0_.refs_12_, ...), custom_call_target="tpu_custom_call" | custom-call | tf_op jit(solution)/shard_map/last_step/pallas_call | solution.py:326
  (15 shorter events, 0.1 us)
Async XLA Ops:
  0.6 10.3 %collective-permute-start.1 = (bf16[6,64,384]{2,1,0:T(8,128)(2,1)}, bf16[6,64,384]{2,1,0:T(8,128)(2,1)S(1)}, u32[]{:S(2)}, u32[]{:S(2)}) collective-permute-start(bf16[6,64,384]{2,1,0:T(8,128)(2,1)} %history_far.1), channel_id=1, source_target_pairs={{0,2},{2,0},{4,6},{6,4},{8,10},{10,8},{12,14},{14,12},{1,3},{3,1},... | collective-permute-start | bytes 884744 | tf_op jit(solution)/shard_map/ppermute | solution.py:31
  4.8 18.8 %collective-permute-start = (bf16[64,2048]{1,0:T(8,128)(2,1)S(1)}, bf16[64,2048]{1,0:T(8,128)(2,1)S(1)}, u32[]{:S(2)}, u32[]{:S(2)}) collective-permute-start(bf16[64,2048]{1,0:T(8,128)(2,1)S(1)} %tanh_convert_fusion.rates_ref), channel_id=1, source_target_pairs={{0,1},{1,0},{2,3},{3,2},{4,5},{5,4},{6,7},{7,6},{8,9},{9,8},{10,11... | collective-permute-start | bytes 786440 | tf_op jit(solution)/shard_map/ppermute | solution.py:31
  11.5 4.7 %collective-permute-start.2 = (s16[2,64,384]{2,1,0:T(8,128)(2,1)S(1)}, s16[2,64,384]{2,1,0:T(8,128)(2,1)S(1)}, u32[]{:S(2)}, u32[]{:S(2)}) collective-permute-start(s16[2,64,384]{2,1,0:T(8,128)(2,1)S(1)} %get-tuple-element.49), channel_id=1, source_target_pairs={{0,4},{2,6},{4,0},{6,2},{8,12},{10,14},{12,8},{14,10},{1,5},{3,7},... | collective-permute-start | bytes 294920 | tf_op jit(solution)/shard_map/ppermute | solution.py:31
  13.4 10.1 %collective-permute-start.3 = (s16[2,64,384]{2,1,0:T(8,128)(2,1)S(1)}, s16[2,64,384]{2,1,0:T(8,128)(2,1)S(1)}, u32[]{:S(2)}, u32[]{:S(2)}) collective-permute-start(s16[2,64,384]{2,1,0:T(8,128)(2,1)S(1)} %get-tuple-element.50), channel_id=1, source_target_pairs={{0,8},{2,10},{4,12},{6,14},{8,0},{10,2},{12,4},{14,6},{1,9},{3,11}... | collective-permute-start | bytes 294920 | tf_op jit(solution)/shard_map/ppermute | solution.py:31
  16.0 7.5 %collective-permute-start.4 = (s16[2,64,384]{2,1,0:T(8,128)(2,1)S(1)}, s16[2,64,384]{2,1,0:T(8,128)(2,1)S(1)}, u32[]{:S(2)}, u32[]{:S(2)}) collective-permute-start(s16[2,64,384]{2,1,0:T(8,128)(2,1)S(1)} %get-tuple-element.51), channel_id=1, source_target_pairs={{0,12},{2,14},{4,8},{6,10},{8,4},{10,6},{12,0},{14,2},{1,13},{3,15... | collective-permute-start | bytes 294920 | tf_op jit(solution)/shard_map/ppermute | solution.py:31
  23.5 5.2 %collective-permute-start.5 = (bf16[128,384]{1,0:T(8,128)(2,1)S(1)}, bf16[128,384]{1,0:T(8,128)(2,1)S(1)}, u32[]{:S(2)}, u32[]{:S(2)}) collective-permute-start(bf16[128,384]{1,0:T(8,128)(2,1)S(1)} %drive.3.refs_0_), channel_id=1, source_target_pairs={{0,1},{1,0},{2,3},{3,2},{4,5},{5,4},{6,7},{7,6},{8,9},{9,8},{10,11... | collective-permute-start | bytes 294920 | tf_op jit(solution)/shard_map/ppermute | solution.py:31
  29.5 2.1 %collective-permute-start.6 = (bf16[64,2048]{1,0:T(8,128)(2,1)S(1)}, bf16[64,2048]{1,0:T(8,128)(2,1)S(1)}, u32[]{:S(2)}, u32[]{:S(2)}) collective-permute-start(bf16[64,2048]{1,0:T(8,128)(2,1)S(1)} %get-tuple-element.54.rates_ref.refs_0_), channel_id=1, source_target_pairs={{0,1},{1,0},{2,3},{3,2},{4,5},{5,4},{6,7},{7,6},{8,9},{9,8},{10,11... | collective-permute-start | bytes 786440 | tf_op jit(solution)/shard_map/ppermute | solution.py:31
  33.3 17.2 %collective-permute-start.7 = (bf16[64,2048]{1,0:T(8,128)(2,1)S(1)}, bf16[64,2048]{1,0:T(8,128)(2,1)S(1)}, u32[]{:S(2)}, u32[]{:S(2)}) collective-permute-start(bf16[64,2048]{1,0:T(8,128)(2,1)S(1)} %get-tuple-element.59.rates_ref.refs_1_), channel_id=1, source_target_pairs={{0,1},{1,0},{2,3},{3,2},{4,5},{5,4},{6,7},{7,6},{8,9},{9,8},{10,11... | collective-permute-start | bytes 786440 | tf_op jit(solution)/shard_map/ppermute | solution.py:31
  33.4 4.1 %collective-permute-start.8 = (bf16[1,64,384]{2,1,0:T(8,128)(2,1)S(1)}, bf16[1,64,384]{2,1,0:T(8,128)(2,1)S(1)}, u32[]{:S(2)}, u32[]{:S(2)}) collective-permute-start(bf16[1,64,384]{2,1,0:T(8,128)(2,1)S(1)} %bitcast.4), channel_id=1, source_target_pairs={{0,2},{2,0},{4,6},{6,4},{8,10},{10,8},{12,14},{14,12},{1,3},{3,1},... | collective-permute-start | bytes 147464 | tf_op jit(solution)/shard_map/ppermute | solution.py:31
  38.1 10.2 %collective-permute-start.10 = (s16[2,64,384]{2,1,0:T(8,128)(2,1)S(1)}, s16[2,64,384]{2,1,0:T(8,128)(2,1)S(1)}, u32[]{:S(2)}, u32[]{:S(2)}) collective-permute-start(s16[2,64,384]{2,1,0:T(8,128)(2,1)S(1)} %get-tuple-element.64), channel_id=1, source_target_pairs={{0,8},{2,10},{4,12},{6,14},{8,0},{10,2},{12,4},{14,6},{1,9},{3,11}... | collective-permute-start | bytes 294920 | tf_op jit(solution)/shard_map/ppermute | solution.py:31
  40.8 7.5 %collective-permute-start.11 = (s16[2,64,384]{2,1,0:T(8,128)(2,1)S(1)}, s16[2,64,384]{2,1,0:T(8,128)(2,1)S(1)}, u32[]{:S(2)}, u32[]{:S(2)}) collective-permute-start(s16[2,64,384]{2,1,0:T(8,128)(2,1)S(1)} %get-tuple-element.65), channel_id=1, source_target_pairs={{0,12},{2,14},{4,8},{6,10},{8,4},{10,6},{12,0},{14,2},{1,13},{3,15... | collective-permute-start | bytes 294920 | tf_op jit(solution)/shard_map/ppermute | solution.py:31
  42.2 6.6 %collective-permute-start.9 = (s16[2,64,384]{2,1,0:T(8,128)(2,1)S(1)}, s16[2,64,384]{2,1,0:T(8,128)(2,1)S(1)}, u32[]{:S(2)}, u32[]{:S(2)}) collective-permute-start(s16[2,64,384]{2,1,0:T(8,128)(2,1)S(1)} %get-tuple-element.63), channel_id=1, source_target_pairs={{0,4},{2,6},{4,0},{6,2},{8,12},{10,14},{12,8},{14,10},{1,5},{3,7},... | collective-permute-start | bytes 294920 | tf_op jit(solution)/shard_map/ppermute | solution.py:31
  48.8 1.7 %collective-permute-start.12 = (bf16[128,384]{1,0:T(8,128)(2,1)S(1)}, bf16[128,384]{1,0:T(8,128)(2,1)S(1)}, u32[]{:S(2)}, u32[]{:S(2)}) collective-permute-start(bf16[128,384]{1,0:T(8,128)(2,1)S(1)} %drive.4.refs_2_), channel_id=1, source_target_pairs={{0,1},{1,0},{2,3},{3,2},{4,5},{5,4},{6,7},{7,6},{8,9},{9,8},{10,11... | collective-permute-start | bytes 294920 | tf_op jit(solution)/shard_map/ppermute | solution.py:31
  52.8 4.1 %collective-permute-start.13 = (bf16[64,2048]{1,0:T(8,128)(2,1)S(1)}, bf16[64,2048]{1,0:T(8,128)(2,1)S(1)}, u32[]{:S(2)}, u32[]{:S(2)}) collective-permute-start(bf16[64,2048]{1,0:T(8,128)(2,1)S(1)} %get-tuple-element.66.rates_ref.refs_7_), channel_id=1, source_target_pairs={{0,1},{1,0},{2,3},{3,2},{4,5},{5,4},{6,7},{7,6},{8,9},{9,8},{10,11... | collective-permute-start | bytes 786440 | tf_op jit(solution)/shard_map/ppermute | solution.py:31
  54.3 4.8 %collective-permute-start.15 = (bf16[2,64,384]{2,1,0:T(8,128)(2,1)S(1)}, bf16[2,64,384]{2,1,0:T(8,128)(2,1)S(1)}, u32[]{:S(2)}, u32[]{:S(2)}) collective-permute-start(bf16[2,64,384]{2,1,0:T(8,128)(2,1)S(1)} %pick.1.refs_4_.refs_6_), channel_id=1, source_target_pairs={{0,2},{2,0},{4,6},{6,4},{8,10},{10,8},{12,14},{14,12},{1,3},{3,1},... | collective-permute-start | bytes 294920 | tf_op jit(solution)/shard_map/ppermute | solution.py:31
  58.6 14.9 %collective-permute-start.14 = (bf16[64,2048]{1,0:T(8,128)(2,1)S(1)}, bf16[64,2048]{1,0:T(8,128)(2,1)S(1)}, u32[]{:S(2)}, u32[]{:S(2)}) collective-permute-start(bf16[64,2048]{1,0:T(8,128)(2,1)S(1)} %get-tuple-element.69.rates_ref.refs_8_), channel_id=1, source_target_pairs={{0,1},{1,0},{2,3},{3,2},{4,5},{5,4},{6,7},{7,6},{8,9},{9,8},{10,11... | collective-permute-start | bytes 786440 | tf_op jit(solution)/shard_map/ppermute | solution.py:31
  59.7 6.0 %collective-permute-start.16 = (s16[2,64,384]{2,1,0:T(8,128)(2,1)S(1)}, s16[2,64,384]{2,1,0:T(8,128)(2,1)S(1)}, u32[]{:S(2)}, u32[]{:S(2)}) collective-permute-start(s16[2,64,384]{2,1,0:T(8,128)(2,1)S(1)} %get-tuple-element.72), channel_id=1, source_target_pairs={{0,4},{2,6},{4,0},{6,2},{8,12},{10,14},{12,8},{14,10},{1,5},{3,7},... | collective-permute-start | bytes 294920 | tf_op jit(solution)/shard_map/ppermute | solution.py:31
  61.0 10.7 %collective-permute-start.17 = (s16[2,64,384]{2,1,0:T(8,128)(2,1)S(1)}, s16[2,64,384]{2,1,0:T(8,128)(2,1)S(1)}, u32[]{:S(2)}, u32[]{:S(2)}) collective-permute-start(s16[2,64,384]{2,1,0:T(8,128)(2,1)S(1)} %get-tuple-element.73), channel_id=1, source_target_pairs={{0,8},{2,10},{4,12},{6,14},{8,0},{10,2},{12,4},{14,6},{1,9},{3,11}... | collective-permute-start | bytes 294920 | tf_op jit(solution)/shard_map/ppermute | solution.py:31
  62.7 9.0 %collective-permute-start.18 = (s16[2,64,384]{2,1,0:T(8,128)(2,1)S(1)}, s16[2,64,384]{2,1,0:T(8,128)(2,1)S(1)}, u32[]{:S(2)}, u32[]{:S(2)}) collective-permute-start(s16[2,64,384]{2,1,0:T(8,128)(2,1)S(1)} %get-tuple-element.74), channel_id=1, source_target_pairs={{0,12},{2,14},{4,8},{6,10},{8,4},{10,6},{12,0},{14,2},{1,13},{3,15... | collective-permute-start | bytes 294920 | tf_op jit(solution)/shard_map/ppermute | solution.py:31
  71.8 1.7 %collective-permute-start.19 = (bf16[128,384]{1,0:T(8,128)(2,1)S(1)}, bf16[128,384]{1,0:T(8,128)(2,1)S(1)}, u32[]{:S(2)}, u32[]{:S(2)}) collective-permute-start(bf16[128,384]{1,0:T(8,128)(2,1)S(1)} %drive.5.refs_2_), channel_id=1, source_target_pairs={{0,1},{1,0},{2,3},{3,2},{4,5},{5,4},{6,7},{7,6},{8,9},{9,8},{10,11... | collective-permute-start | bytes 294920 | tf_op jit(solution)/shard_map/ppermute | solution.py:31
  75.8 2.2 %collective-permute-start.20 = (bf16[64,2048]{1,0:T(8,128)(2,1)S(1)}, bf16[64,2048]{1,0:T(8,128)(2,1)S(1)}, u32[]{:S(2)}, u32[]{:S(2)}) collective-permute-start(bf16[64,2048]{1,0:T(8,128)(2,1)S(1)} %get-tuple-element.75.rates_ref.refs_9_), channel_id=1, source_target_pairs={{0,1},{1,0},{2,3},{3,2},{4,5},{5,4},{6,7},{7,6},{8,9},{9,8},{10,11... | collective-permute-start | bytes 786440 | tf_op jit(solution)/shard_map/ppermute | solution.py:31
where the time goes:
time: 81.2 us; the launch traced here: 81 us
  Pallas kernels  32.7 us (40%)
  waiting for transfers between devices  25.9 us (32%)
  starting transfers between devices  20.2 us (25%)
  other arithmetic  1.12 us (1%)
  between operations  1.04 us (1%)
    ppermute x21, waiting for transfers between devices, crossed(): return lax.ppermute(value, axis, pairs)  25.9 us
    ppermute x21, starting transfers between devices, crossed(): return lax.ppermute(value, axis, pairs)  20.2 us
    pallas_call x5, Pallas kernels, step(): pl.pallas_call(functools.partial(step_kernel, flow is not None, drives is...  8.6 us
    pallas_call x5, Pallas kernels, own_part(): pl.pallas_call(own_kernel, out_shape=shaped(extra.shape, F32), in_specs=[...  8 us
    pallas_call x1, Pallas kernels, stage(): pl.pallas_call(functools.partial(stage_kernel, lines), out_shape=(pltpu.V...  5.25 us
    pallas_call x1, Pallas kernels, opening(): pl.pallas_call(opening_kernel, out_shape=(pltpu.VMEM(own.shape, BF16), pl...  5.08 us
    pallas_call x1, Pallas kernels, last_step(): pl.pallas_call(functools.partial(step_kernel, True, False, True), out_sha...  2.86 us
    pallas_call x3, Pallas kernels, partials(): pl.pallas_call(functools.partial(partial_kernel, times, lines, [field[:2]...  1.78 us
  transfers between devices with their start and end apart: 21, of which 9 were waited for; matrix products, arithmetic and copies ran while one was open for 1% of the time, Pallas kernels for 28%

commit v1 on v0

--- a/solution.py
+++ b/solution.py
@@ -148,8 +148,6 @@
     rates_ref,
     facing_ref,
     own_ref,
-    pick_own_ref,
-    pick_other_ref,
     rec_far,
     extra_far,
     state_far,
@@ -159,7 +157,6 @@
     state_ref,
     leak_ref,
     out_ref,
-    pick_ref,
     sems,
 ):
     unit = unit_ref[0]
@@ -178,9 +175,6 @@
     moves = started(moves, sems)
     for cols in columns_of(out_ref.shape[1]):
         out_ref[:, cols] = matmul(rates_ref[...], own_ref[:, cols])
-    picked = matmul(rates_ref[...], pick_own_ref[...])
-    picked += matmul(facing_ref[...], pick_other_ref[...])
-    pick_ref[...] = picked.astype(BF16)
     for move, span in zip(moves, spans):
         move.wait()
         for cols in columns_of(out_ref.shape[1]):
@@ -190,8 +184,7 @@
     out_ref[...] += extra_ref[...]
 
 
-def opening(unit, rates, facing, own, selects, w_rec, extra, state, leak):
-    part = selects[0].shape[1]
+def opening(unit, rates, facing, own, w_rec, extra, state, leak):
     return pl.pallas_call(
         opening_kernel,
         out_shape=(
@@ -200,14 +193,13 @@
             pltpu.VMEM(state.shape, F32),
             pltpu.VMEM(leak.shape, F32),
             pltpu.VMEM(extra.shape, F32),
-            pltpu.VMEM((rates.shape[0], part), BF16),
         ),
-        in_specs=[SM] + [VM] * 5 + [HB] * 4,
-        out_specs=(VM,) * 6,
+        in_specs=[SM] + [VM] * 3 + [HB] * 4,
+        out_specs=(VM,) * 5,
         scratch_shapes=[pltpu.SemaphoreType.DMA((5,))],
         compiler_params=params(),
         name="opening",
-    )(unit, rates, facing, own, *selects, *[far(array) for array in (w_rec, extra, state, leak)])
+    )(unit, rates, facing, own, *[far(array) for array in (w_rec, extra, state, leak)])
 
 
 def pick_kernel(count, *refs):
@@ -435,12 +427,13 @@
     def share(value, first):
         return [(0, first, value), (1, first, crossed(value, "area", 1))]
 
+    fresh = pick([(rates, other)], selects)
     sent = send((0, 1))
-    rec_other, external, state, leak_row, total, fresh = opening(
-        unit, rates, other, rec_own, selects, w_rec, external, state_start, leak_row
+    known += share(fresh, 0)
+    rec_other, external, state, leak_row, total = opening(
+        unit, rates, other, rec_own, w_rec, external, state_start, leak_row
     )
-    known += share(fresh[None], 0)
-    old, pairs, flow, kept = [fresh[None]], [], None, None
+    old, pairs, flow, kept = [fresh], [], None, None
     for time in range(STEPS):
         if time > 0:
             other = crossed(rates, "unit", 1)

time: 81.2 us -> 82.8 us (1.020)
  waiting for transfers between devices: 25.9 us -> 27.1 us
    ppermute x21, waiting for transfers between devices: 25.9 us -> 27.1 us  [crossed(): return lax.ppermute(value, axis, pairs)]
where the time goes in v1:
time: 82.8 us; the launch traced here: 82.6 us
  Pallas kernels  32.7 us (39%)
  waiting for transfers between devices  27.1 us (33%)
  starting transfers between devices  20.6 us (25%)
  other arithmetic  1.12 us (1%)
  between operations  1.05 us (1%)
    ppermute x21, waiting for transfers between devices, crossed(): return lax.ppermute(value, axis, pairs)  27.1 us
    ppermute x21, starting transfers between devices, crossed(): return lax.ppermute(value, axis, pairs)  20.6 us
    pallas_call x5, Pallas kernels, step(): pl.pallas_call(functools.partial(step_kernel, flow is not None, drives is...  8.62 us
    pallas_call x5, Pallas kernels, own_part(): pl.pallas_call(own_kernel, out_shape=shaped(extra.shape, F32), in_specs=[...  7.99 us
    pallas_call x1, Pallas kernels, stage(): pl.pallas_call(functools.partial(stage_kernel, lines), out_shape=(pltpu.V...  5.25 us
    pallas_call x1, Pallas kernels, opening(): pl.pallas_call(opening_kernel, out_shape=(pltpu.VMEM(own.shape, BF16), pl...  4.44 us
    pallas_call x1, Pallas kernels, last_step(): pl.pallas_call(functools.partial(step_kernel, True, False, True), out_sha...  2.86 us
    pallas_call x3, Pallas kernels, partials(): pl.pallas_call(functools.partial(partial_kernel, times, lines, [field[:2]...  1.79 us
  transfers between devices with their start and end apart: 21, of which 9 were waited for; matrix products, arithmetic and copies ran while one was open for 1% of the time, Pallas kernels for 28%

profile of v1, /device:TPU:0, one launch (start us, length us, event | category | flops | bytes accessed | tf_op | source)
XLA Modules:
  0.0 82.6 jit_solution(584853081170065347)
XLA Ops:
  0.6 3.0 %collective-permute-start.1 = (bf16[6,64,384]{2,1,0:T(8,128)(2,1)}, bf16[6,64,384]{2,1,0:T(8,128)(2,1)S(1)}, u32[]{:S(2)}, u32[]{:S(2)}) collective-permute-start(bf16[6,64,384]{2,1,0:T(8,128)(2,1)} %history_far.1), channel_id=1, source_target_pairs={{0,2},{2,0},{4,6},{6,4},{8,10},{10,8},{12,14},{14,12},{1,3},{3,1},... | collective-permute-start | bytes 884744 | tf_op jit(solution)/shard_map/ppermute | solution.py:31
  3.7 1.1 %tanh_convert_fusion.rates_ref.refs_0_ = bf16[64,2048]{1,0:T(8,128)(2,1)S(1)} fusion(f32[64,2048]{1,0:T(8,128)} %state_far.1), kind=kLoop, calls=%fused_computation | loop fusion | flops 131072 | bytes 786432 | tf_op jit(solution)/shard_map/convert_element_type | solution.py:408
  4.8 0.1 collective-permute-start
  4.9 5.3 %stage.1 = (bf16[6,64,384]{2,1,0:T(8,128)(2,1)S(1)}, bf16[2048,2048]{1,0:T(8,128)(2,1)S(1)}, bf16[384,2048]{1,0:T(8,128)(2,1)S(1)}, bf16[384,2048]{1,0:T(8,128)(...) custom-call(s32[1]{0:T(128)} %bitcast.1.area_ref, s32[1]{0:T(128)} %bitcast.unit_ref, ...), custom_call_target="tpu_custom_call" | custom-call | tf_op jit(solution)/shard_map/stage/pallas_call | solution.py:127
  10.1 0.8 collective-permute-done.1.refs_1_
  10.9 0.6 partials.3
  11.5 1.9 %collective-permute-start.2 = (s16[2,64,384]{2,1,0:T(8,128)(2,1)S(1)}, s16[2,64,384]{2,1,0:T(8,128)(2,1)S(1)}, u32[]{:S(2)}, u32[]{:S(2)}) collective-permute-start(s16[2,64,384]{2,1,0:T(8,128)(2,1)S(1)} %get-tuple-element.46), channel_id=1, source_target_pairs={{0,4},{2,6},{4,0},{6,2},{8,12},{10,14},{12,8},{14,10},{1,5},{3,7},... | collective-permute-start | bytes 294920 | tf_op jit(solution)/shard_map/ppermute | solution.py:31
  13.4 2.6 %collective-permute-start.3 = (s16[2,64,384]{2,1,0:T(8,128)(2,1)S(1)}, s16[2,64,384]{2,1,0:T(8,128)(2,1)S(1)}, u32[]{:S(2)}, u32[]{:S(2)}) collective-permute-start(s16[2,64,384]{2,1,0:T(8,128)(2,1)S(1)} %get-tuple-element.47), channel_id=1, source_target_pairs={{0,8},{2,10},{4,12},{6,14},{8,0},{10,2},{12,4},{14,6},{1,9},{3,11}... | collective-permute-start | bytes 294920 | tf_op jit(solution)/shard_map/ppermute | solution.py:31
  16.0 0.2 collective-permute-done.2.refs_0_
  16.2 7.3 %collective-permute-done.3.refs_1_ = s16[2,64,384]{2,1,0:T(8,128)(2,1)S(1)} collective-permute-done((s16[2,64,384]{2,1,0:T(8,128)(2,1)S(1)}, s16[2,64,384]{2,1,0:T(8,128)(2,1)S(1)}, u32[]{:S(2)}, u32[]{:S(2)}) %collective-permute-start.3) | collective-permute-done | bytes 98336 | tf_op jit(solution)/shard_map/ppermute | solution.py:31
  23.5 0.1 drive.3.refs_0_
  23.5 0.1 collective-permute-start.5
  23.6 4.4 %opening.1 = (bf16[2048,2048]{1,0:T(8,128)(2,1)S(1)}, f32[64,2048]{1,0:T(8,128)S(1)}, f32[64,2048]{1,0:T(8,128)S(1)}, f32[1,2048]{1,0:T(1,128)S(1)}, f32[64,2048]{1,0:T(8,128)S(1)}) custom-call(s32[1]{0:T(128)} %bitcast.unit_ref, bf16[64,2048]{1,0:T(8,128)(2,1)S(1)} %tanh_convert_fusion.rates_ref.refs_0_, ...), custom_call_target="tpu_custom_call" | custom-call | tf_op jit(solution)/shard_map/opening/pallas_call | solution.py:188
  28.1 0.8 step.5
  28.9 0.5 collective-permute-start.6
  29.4 1.6 %own_part.5.sum_ref = f32[64,2048]{1,0:T(8,128)S(1)} custom-call(bf16[64,2048]{1,0:T(8,128)(2,1)S(1)} %get-tuple-element.51.rates_ref.refs_0_, bf16[2048,2048]{1,0:T(8,128)(2,1)S(1)} %get-tuple-element.39.own_ref.weight_ref, f32[64,2048]{1,0:T(8,128)S(1)} %get-tuple-element.52.extra_ref), custom_call_target="tpu_custom_call" | custom-call | tf_op jit(solution)/shard_map/own_part/pallas_call | solution.py:231
  31.0 1.7 %step.6 = (f32[64,2048]{1,0:T(8,128)S(1)}, bf16[64,2048]{1,0:T(8,128)(2,1)S(1)}) custom-call(f32[64,2048]{1,0:T(8,128)S(1)} %own_part.5.sum_ref, f32[64,2048]{1,0:T(8,128)S(1)} %get-tuple-element.53.state_ref, f32[1,2048]{1,0:T(1,128)S(1)} %get-tuple-element.42.leak_ref, bf16[64,2048]{1,0:T(8,128)(2,1)S(1)} %collective-permute-done.6.refs_0_.refs_2_, ...), custom_call_target="tpu_custom_call" | custom-call | tf_op jit(solution)/shard_map/step/pallas_call | solution.py:303
  32.7 0.1 collective-permute-start.7
  32.8 0.6 pick.2.refs_2_.refs_5_
  33.4 1.0 %collective-permute-start.8 = (bf16[1,64,384]{2,1,0:T(8,128)(2,1)S(1)}, bf16[1,64,384]{2,1,0:T(8,128)(2,1)S(1)}, u32[]{:S(2)}, u32[]{:S(2)}) collective-permute-start(bf16[1,64,384]{2,1,0:T(8,128)(2,1)S(1)} %pick.2.refs_2_.refs_5_), channel_id=1, source_target_pairs={{0,2},{2,0},{4,6},{6,4},{8,10},{10,8},{12,14},{14,12},{1,3},{3,1},... | collective-permute-start | bytes 147464 | tf_op jit(solution)/shard_map/ppermute | solution.py:31
  34.5 3.1 %collective-permute-done.8.refs_3_ = bf16[1,64,384]{2,1,0:T(8,128)(2,1)S(1)} collective-permute-done((bf16[1,64,384]{2,1,0:T(8,128)(2,1)S(1)}, bf16[1,64,384]{2,1,0:T(8,128)(2,1)S(1)}, u32[]{:S(2)}, u32[]{:S(2)}) %collective-permute-start.8) | collective-permute-done | bytes 49184 | tf_op jit(solution)/shard_map/ppermute | solution.py:31
  37.6 0.6 partials.4
  38.2 1.7 %collective-permute-start.9 = (s16[2,64,384]{2,1,0:T(8,128)(2,1)S(1)}, s16[2,64,384]{2,1,0:T(8,128)(2,1)S(1)}, u32[]{:S(2)}, u32[]{:S(2)}) collective-permute-start(s16[2,64,384]{2,1,0:T(8,128)(2,1)S(1)} %get-tuple-element.61), channel_id=1, source_target_pairs={{0,4},{2,6},{4,0},{6,2},{8,12},{10,14},{12,8},{14,10},{1,5},{3,7},... | collective-permute-start | bytes 294920 | tf_op jit(solution)/shard_map/ppermute | solution.py:31
  39.9 1.4 %collective-permute-start.10 = (s16[2,64,384]{2,1,0:T(8,128)(2,1)S(1)}, s16[2,64,384]{2,1,0:T(8,128)(2,1)S(1)}, u32[]{:S(2)}, u32[]{:S(2)}) collective-permute-start(s16[2,64,384]{2,1,0:T(8,128)(2,1)S(1)} %get-tuple-element.62), channel_id=1, source_target_pairs={{0,8},{2,10},{4,12},{6,14},{8,0},{10,2},{12,4},{14,6},{1,9},{3,11}... | collective-permute-start | bytes 294920 | tf_op jit(solution)/shard_map/ppermute | solution.py:31
  41.3 1.3 %collective-permute-start.11 = (s16[2,64,384]{2,1,0:T(8,128)(2,1)S(1)}, s16[2,64,384]{2,1,0:T(8,128)(2,1)S(1)}, u32[]{:S(2)}, u32[]{:S(2)}) collective-permute-start(s16[2,64,384]{2,1,0:T(8,128)(2,1)S(1)} %get-tuple-element.63), channel_id=1, source_target_pairs={{0,12},{2,14},{4,8},{6,10},{8,4},{10,6},{12,0},{14,2},{1,13},{3,15... | collective-permute-start | bytes 294920 | tf_op jit(solution)/shard_map/ppermute | solution.py:31
  42.6 1.2 %collective-permute-done.9.refs_0_ = s16[2,64,384]{2,1,0:T(8,128)(2,1)S(1)} collective-permute-done((s16[2,64,384]{2,1,0:T(8,128)(2,1)S(1)}, s16[2,64,384]{2,1,0:T(8,128)(2,1)S(1)}, u32[]{:S(2)}, u32[]{:S(2)}) %collective-permute-start.9) | collective-permute-done | bytes 98336 | tf_op jit(solution)/shard_map/ppermute | solution.py:31
  43.8 6.3 %collective-permute-done.10.refs_1_ = s16[2,64,384]{2,1,0:T(8,128)(2,1)S(1)} collective-permute-done((s16[2,64,384]{2,1,0:T(8,128)(2,1)S(1)}, s16[2,64,384]{2,1,0:T(8,128)(2,1)S(1)}, u32[]{:S(2)}, u32[]{:S(2)}) %collective-permute-start.10) | collective-permute-done | bytes 98336 | tf_op jit(solution)/shard_map/ppermute | solution.py:31
  50.1 0.1 drive.4.refs_2_
  50.3 1.6 %own_part.6.sum_ref = f32[64,2048]{1,0:T(8,128)S(1)} custom-call(bf16[64,2048]{1,0:T(8,128)(2,1)S(1)} %get-tuple-element.56.rates_ref.refs_1_, bf16[2048,2048]{1,0:T(8,128)(2,1)S(1)} %get-tuple-element.39.own_ref.weight_ref, f32[64,2048]{1,0:T(8,128)S(1)} %get-tuple-element.52.extra_ref), custom_call_target="tpu_custom_call" | custom-call | tf_op jit(solution)/shard_map/own_part/pallas_call | solution.py:231
  51.9 2.3 %step.7 = (f32[64,2048]{1,0:T(8,128)S(1)}, bf16[64,2048]{1,0:T(8,128)(2,1)S(1)}, f32[64,2048]{1,0:T(8,128)S(1)}) custom-call(f32[64,2048]{1,0:T(8,128)S(1)} %own_part.6.sum_ref, f32[64,2048]{1,0:T(8,128)S(1)} %get-tuple-element.57.state_ref, f32[1,2048]{1,0:T(1,128)S(1)} %get-tuple-element.42.leak_ref, ...), custom_call_target="tpu_custom_call" | custom-call | tf_op jit(solution)/shard_map/step/pallas_call | solution.py:303
  54.2 0.6 collective-permute-start.13
  54.7 0.9 %pick.3.refs_4_.refs_6_ = bf16[2,64,384]{2,1,0:T(8,128)(2,1)S(1)} custom-call(bf16[64,2048]{1,0:T(8,128)(2,1)S(1)} %get-tuple-element.51.rates_ref.refs_0_, bf16[64,2048]{1,0:T(8,128)(2,1)S(1)} %get-tuple-element.56.rates_ref.refs_1_, bf16[64,2048]{1,0:T(8,128)(2,1)S(1)} %collective-permute-done.6.refs_0_.refs_2_, ...), custom_call_target="tpu_custom_call" | custom-call | tf_op jit(solution)/shard_map/pick/pallas_call | solution.py:215
  55.6 1.0 %collective-permute-start.15 = (bf16[2,64,384]{2,1,0:T(8,128)(2,1)S(1)}, bf16[2,64,384]{2,1,0:T(8,128)(2,1)S(1)}, u32[]{:S(2)}, u32[]{:S(2)}) collective-permute-start(bf16[2,64,384]{2,1,0:T(8,128)(2,1)S(1)} %pick.3.refs_4_.refs_6_), channel_id=1, source_target_pairs={{0,2},{2,0},{4,6},{6,4},{8,10},{10,8},{12,14},{14,12},{1,3},{3,1},... | collective-permute-start | bytes 294920 | tf_op jit(solution)/shard_map/ppermute | solution.py:31
  56.7 1.6 %own_part.7.sum_ref = f32[64,2048]{1,0:T(8,128)S(1)} custom-call(bf16[64,2048]{1,0:T(8,128)(2,1)S(1)} %get-tuple-element.64.rates_ref.refs_7_, bf16[2048,2048]{1,0:T(8,128)(2,1)S(1)} %get-tuple-element.39.own_ref.weight_ref, f32[64,2048]{1,0:T(8,128)S(1)} %get-tuple-element.52.extra_ref), custom_call_target="tpu_custom_call" | custom-call | tf_op jit(solution)/shard_map/own_part/pallas_call | solution.py:231
  58.3 1.7 %step.8 = (f32[64,2048]{1,0:T(8,128)S(1)}, bf16[64,2048]{1,0:T(8,128)(2,1)S(1)}) custom-call(f32[64,2048]{1,0:T(8,128)S(1)} %own_part.7.sum_ref, f32[64,2048]{1,0:T(8,128)S(1)} %get-tuple-element.65.state_ref, f32[1,2048]{1,0:T(1,128)S(1)} %get-tuple-element.42.leak_ref, bf16[64,2048]{1,0:T(8,128)(2,1)S(1)} %collective-permute-done.13.refs_0_.refs_10_, ...), custom_call_target="tpu_custom_call" | custom-call | tf_op jit(solution)/shard_map/step/pallas_call | solution.py:303
  60.0 0.4 collective-permute-done.15.refs_5_
  60.4 0.6 partials.5
  61.0 1.7 %collective-permute-start.16 = (s16[2,64,384]{2,1,0:T(8,128)(2,1)S(1)}, s16[2,64,384]{2,1,0:T(8,128)(2,1)S(1)}, u32[]{:S(2)}, u32[]{:S(2)}) collective-permute-start(s16[2,64,384]{2,1,0:T(8,128)(2,1)S(1)} %get-tuple-element.70), channel_id=1, source_target_pairs={{0,4},{2,6},{4,0},{6,2},{8,12},{10,14},{12,8},{14,10},{1,5},{3,7},... | collective-permute-start | bytes 294920 | tf_op jit(solution)/shard_map/ppermute | solution.py:31
  62.7 1.0 %collective-permute-start.17 = (s16[2,64,384]{2,1,0:T(8,128)(2,1)S(1)}, s16[2,64,384]{2,1,0:T(8,128)(2,1)S(1)}, u32[]{:S(2)}, u32[]{:S(2)}) collective-permute-start(s16[2,64,384]{2,1,0:T(8,128)(2,1)S(1)} %get-tuple-element.71), channel_id=1, source_target_pairs={{0,8},{2,10},{4,12},{6,14},{8,0},{10,2},{12,4},{14,6},{1,9},{3,11}... | collective-permute-start | bytes 294920 | tf_op jit(solution)/shard_map/ppermute | solution.py:31
  63.7 1.8 %collective-permute-start.18 = (s16[2,64,384]{2,1,0:T(8,128)(2,1)S(1)}, s16[2,64,384]{2,1,0:T(8,128)(2,1)S(1)}, u32[]{:S(2)}, u32[]{:S(2)}) collective-permute-start(s16[2,64,384]{2,1,0:T(8,128)(2,1)S(1)} %get-tuple-element.72), channel_id=1, source_target_pairs={{0,12},{2,14},{4,8},{6,10},{8,4},{10,6},{12,0},{14,2},{1,13},{3,15... | collective-permute-start | bytes 294920 | tf_op jit(solution)/shard_map/ppermute | solution.py:31
  65.5 0.4 collective-permute-done.16.refs_0_
  65.9 7.4 %collective-permute-done.17.refs_1_ = s16[2,64,384]{2,1,0:T(8,128)(2,1)S(1)} collective-permute-done((s16[2,64,384]{2,1,0:T(8,128)(2,1)S(1)}, s16[2,64,384]{2,1,0:T(8,128)(2,1)S(1)}, u32[]{:S(2)}, u32[]{:S(2)}) %collective-permute-start.17) | collective-permute-done | bytes 98336 | tf_op jit(solution)/shard_map/ppermute | solution.py:31
  73.3 0.1 drive.5.refs_2_
  73.5 1.6 %own_part.8.sum_ref = f32[64,2048]{1,0:T(8,128)S(1)} custom-call(bf16[64,2048]{1,0:T(8,128)(2,1)S(1)} %get-tuple-element.67.rates_ref.refs_8_, bf16[2048,2048]{1,0:T(8,128)(2,1)S(1)} %get-tuple-element.39.own_ref.weight_ref, f32[64,2048]{1,0:T(8,128)S(1)} %get-tuple-element.52.extra_ref), custom_call_target="tpu_custom_call" | custom-call | tf_op jit(solution)/shard_map/own_part/pallas_call | solution.py:231
  75.1 2.3 %step.9 = (f32[64,2048]{1,0:T(8,128)S(1)}, bf16[64,2048]{1,0:T(8,128)(2,1)S(1)}, f32[64,2048]{1,0:T(8,128)S(1)}) custom-call(f32[64,2048]{1,0:T(8,128)S(1)} %own_part.8.sum_ref, f32[64,2048]{1,0:T(8,128)S(1)} %get-tuple-element.68.state_ref, f32[1,2048]{1,0:T(1,128)S(1)} %get-tuple-element.42.leak_ref, ...), custom_call_target="tpu_custom_call" | custom-call | tf_op jit(solution)/shard_map/step/pallas_call | solution.py:303
  77.4 0.6 collective-permute-start.20
  78.0 1.6 %own_part.9.sum_ref = f32[64,2048]{1,0:T(8,128)S(1)} custom-call(bf16[64,2048]{1,0:T(8,128)(2,1)S(1)} %get-tuple-element.73.rates_ref.refs_9_, bf16[2048,2048]{1,0:T(8,128)(2,1)S(1)} %get-tuple-element.39.own_ref.weight_ref, f32[64,2048]{1,0:T(8,128)S(1)} %get-tuple-element.52.extra_ref), custom_call_target="tpu_custom_call" | custom-call | tf_op jit(solution)/shard_map/own_part/pallas_call | solution.py:231
  79.6 2.9 %last_step.1 = (f32[64,2048]{1,0:T(8,128)}, bf16[6,64,384]{2,1,0:T(8,128)(2,1)}) custom-call(f32[64,2048]{1,0:T(8,128)S(1)} %own_part.9.sum_ref, f32[64,2048]{1,0:T(8,128)S(1)} %get-tuple-element.74.state_ref, f32[1,2048]{1,0:T(1,128)S(1)} %get-tuple-element.42.leak_ref, bf16[64,2048]{1,0:T(8,128)(2,1)S(1)} %collective-permute-done.20.refs_0_.refs_12_, ...), custom_call_target="tpu_custom_call" | custom-call | tf_op jit(solution)/shard_map/last_step/pallas_call | solution.py:318
  (16 shorter events, 0.2 us)
Async XLA Ops:
  0.6 10.3 %collective-permute-start.1 = (bf16[6,64,384]{2,1,0:T(8,128)(2,1)}, bf16[6,64,384]{2,1,0:T(8,128)(2,1)S(1)}, u32[]{:S(2)}, u32[]{:S(2)}) collective-permute-start(bf16[6,64,384]{2,1,0:T(8,128)(2,1)} %history_far.1), channel_id=1, source_target_pairs={{0,2},{2,0},{4,6},{6,4},{8,10},{10,8},{12,14},{14,12},{1,3},{3,1},... | collective-permute-start | bytes 884744 | tf_op jit(solution)/shard_map/ppermute | solution.py:31
  4.8 18.8 %collective-permute-start = (bf16[64,2048]{1,0:T(8,128)(2,1)S(1)}, bf16[64,2048]{1,0:T(8,128)(2,1)S(1)}, u32[]{:S(2)}, u32[]{:S(2)}) collective-permute-start(bf16[64,2048]{1,0:T(8,128)(2,1)S(1)} %tanh_convert_fusion.rates_ref.refs_0_), channel_id=1, source_target_pairs={{0,1},{1,0},{2,3},{3,2},{4,5},{5,4},{6,7},{7,6},{8,9},{9,8},{10,11... | collective-permute-start | bytes 786440 | tf_op jit(solution)/shard_map/ppermute | solution.py:31
  11.5 4.7 %collective-permute-start.2 = (s16[2,64,384]{2,1,0:T(8,128)(2,1)S(1)}, s16[2,64,384]{2,1,0:T(8,128)(2,1)S(1)}, u32[]{:S(2)}, u32[]{:S(2)}) collective-permute-start(s16[2,64,384]{2,1,0:T(8,128)(2,1)S(1)} %get-tuple-element.46), channel_id=1, source_target_pairs={{0,4},{2,6},{4,0},{6,2},{8,12},{10,14},{12,8},{14,10},{1,5},{3,7},... | collective-permute-start | bytes 294920 | tf_op jit(solution)/shard_map/ppermute | solution.py:31
  13.4 10.1 %collective-permute-start.3 = (s16[2,64,384]{2,1,0:T(8,128)(2,1)S(1)}, s16[2,64,384]{2,1,0:T(8,128)(2,1)S(1)}, u32[]{:S(2)}, u32[]{:S(2)}) collective-permute-start(s16[2,64,384]{2,1,0:T(8,128)(2,1)S(1)} %get-tuple-element.47), channel_id=1, source_target_pairs={{0,8},{2,10},{4,12},{6,14},{8,0},{10,2},{12,4},{14,6},{1,9},{3,11}... | collective-permute-start | bytes 294920 | tf_op jit(solution)/shard_map/ppermute | solution.py:31
  16.0 7.5 %collective-permute-start.4 = (s16[2,64,384]{2,1,0:T(8,128)(2,1)S(1)}, s16[2,64,384]{2,1,0:T(8,128)(2,1)S(1)}, u32[]{:S(2)}, u32[]{:S(2)}) collective-permute-start(s16[2,64,384]{2,1,0:T(8,128)(2,1)S(1)} %get-tuple-element.48), channel_id=1, source_target_pairs={{0,12},{2,14},{4,8},{6,10},{8,4},{10,6},{12,0},{14,2},{1,13},{3,15... | collective-permute-start | bytes 294920 | tf_op jit(solution)/shard_map/ppermute | solution.py:31
  23.5 4.5 %collective-permute-start.5 = (bf16[128,384]{1,0:T(8,128)(2,1)S(1)}, bf16[128,384]{1,0:T(8,128)(2,1)S(1)}, u32[]{:S(2)}, u32[]{:S(2)}) collective-permute-start(bf16[128,384]{1,0:T(8,128)(2,1)S(1)} %drive.3.refs_0_), channel_id=1, source_target_pairs={{0,1},{1,0},{2,3},{3,2},{4,5},{5,4},{6,7},{7,6},{8,9},{9,8},{10,11... | collective-permute-start | bytes 294920 | tf_op jit(solution)/shard_map/ppermute | solution.py:31
  28.9 2.1 %collective-permute-start.6 = (bf16[64,2048]{1,0:T(8,128)(2,1)S(1)}, bf16[64,2048]{1,0:T(8,128)(2,1)S(1)}, u32[]{:S(2)}, u32[]{:S(2)}) collective-permute-start(bf16[64,2048]{1,0:T(8,128)(2,1)S(1)} %get-tuple-element.51.rates_ref.refs_0_), channel_id=1, source_target_pairs={{0,1},{1,0},{2,3},{3,2},{4,5},{5,4},{6,7},{7,6},{8,9},{9,8},{10,11... | collective-permute-start | bytes 786440 | tf_op jit(solution)/shard_map/ppermute | solution.py:31
  32.7 19.2 %collective-permute-start.7 = (bf16[64,2048]{1,0:T(8,128)(2,1)S(1)}, bf16[64,2048]{1,0:T(8,128)(2,1)S(1)}, u32[]{:S(2)}, u32[]{:S(2)}) collective-permute-start(bf16[64,2048]{1,0:T(8,128)(2,1)S(1)} %get-tuple-element.56.rates_ref.refs_1_), channel_id=1, source_target_pairs={{0,1},{1,0},{2,3},{3,2},{4,5},{5,4},{6,7},{7,6},{8,9},{9,8},{10,11... | collective-permute-start | bytes 786440 | tf_op jit(solution)/shard_map/ppermute | solution.py:31
  33.4 4.2 %collective-permute-start.8 = (bf16[1,64,384]{2,1,0:T(8,128)(2,1)S(1)}, bf16[1,64,384]{2,1,0:T(8,128)(2,1)S(1)}, u32[]{:S(2)}, u32[]{:S(2)}) collective-permute-start(bf16[1,64,384]{2,1,0:T(8,128)(2,1)S(1)} %pick.2.refs_2_.refs_5_), channel_id=1, source_target_pairs={{0,2},{2,0},{4,6},{6,4},{8,10},{10,8},{12,14},{14,12},{1,3},{3,1},... | collective-permute-start | bytes 147464 | tf_op jit(solution)/shard_map/ppermute | solution.py:31
  38.2 5.6 %collective-permute-start.9 = (s16[2,64,384]{2,1,0:T(8,128)(2,1)S(1)}, s16[2,64,384]{2,1,0:T(8,128)(2,1)S(1)}, u32[]{:S(2)}, u32[]{:S(2)}) collective-permute-start(s16[2,64,384]{2,1,0:T(8,128)(2,1)S(1)} %get-tuple-element.61), channel_id=1, source_target_pairs={{0,4},{2,6},{4,0},{6,2},{8,12},{10,14},{12,8},{14,10},{1,5},{3,7},... | collective-permute-start | bytes 294920 | tf_op jit(solution)/shard_map/ppermute | solution.py:31
  39.9 10.2 %collective-permute-start.10 = (s16[2,64,384]{2,1,0:T(8,128)(2,1)S(1)}, s16[2,64,384]{2,1,0:T(8,128)(2,1)S(1)}, u32[]{:S(2)}, u32[]{:S(2)}) collective-permute-start(s16[2,64,384]{2,1,0:T(8,128)(2,1)S(1)} %get-tuple-element.62), channel_id=1, source_target_pairs={{0,8},{2,10},{4,12},{6,14},{8,0},{10,2},{12,4},{14,6},{1,9},{3,11}... | collective-permute-start | bytes 294920 | tf_op jit(solution)/shard_map/ppermute | solution.py:31
  41.3 8.8 %collective-permute-start.11 = (s16[2,64,384]{2,1,0:T(8,128)(2,1)S(1)}, s16[2,64,384]{2,1,0:T(8,128)(2,1)S(1)}, u32[]{:S(2)}, u32[]{:S(2)}) collective-permute-start(s16[2,64,384]{2,1,0:T(8,128)(2,1)S(1)} %get-tuple-element.63), channel_id=1, source_target_pairs={{0,12},{2,14},{4,8},{6,10},{8,4},{10,6},{12,0},{14,2},{1,13},{3,15... | collective-permute-start | bytes 294920 | tf_op jit(solution)/shard_map/ppermute | solution.py:31
  50.2 1.7 %collective-permute-start.12 = (bf16[128,384]{1,0:T(8,128)(2,1)S(1)}, bf16[128,384]{1,0:T(8,128)(2,1)S(1)}, u32[]{:S(2)}, u32[]{:S(2)}) collective-permute-start(bf16[128,384]{1,0:T(8,128)(2,1)S(1)} %drive.4.refs_2_), channel_id=1, source_target_pairs={{0,1},{1,0},{2,3},{3,2},{4,5},{5,4},{6,7},{7,6},{8,9},{9,8},{10,11... | collective-permute-start | bytes 294920 | tf_op jit(solution)/shard_map/ppermute | solution.py:31
  54.2 4.1 %collective-permute-start.13 = (bf16[64,2048]{1,0:T(8,128)(2,1)S(1)}, bf16[64,2048]{1,0:T(8,128)(2,1)S(1)}, u32[]{:S(2)}, u32[]{:S(2)}) collective-permute-start(bf16[64,2048]{1,0:T(8,128)(2,1)S(1)} %get-tuple-element.64.rates_ref.refs_7_), channel_id=1, source_target_pairs={{0,1},{1,0},{2,3},{3,2},{4,5},{5,4},{6,7},{7,6},{8,9},{9,8},{10,11... | collective-permute-start | bytes 786440 | tf_op jit(solution)/shard_map/ppermute | solution.py:31
  55.6 4.8 %collective-permute-start.15 = (bf16[2,64,384]{2,1,0:T(8,128)(2,1)S(1)}, bf16[2,64,384]{2,1,0:T(8,128)(2,1)S(1)}, u32[]{:S(2)}, u32[]{:S(2)}) collective-permute-start(bf16[2,64,384]{2,1,0:T(8,128)(2,1)S(1)} %pick.3.refs_4_.refs_6_), channel_id=1, source_target_pairs={{0,2},{2,0},{4,6},{6,4},{8,10},{10,8},{12,14},{14,12},{1,3},{3,1},... | collective-permute-start | bytes 294920 | tf_op jit(solution)/shard_map/ppermute | solution.py:31
  59.9 15.2 %collective-permute-start.14 = (bf16[64,2048]{1,0:T(8,128)(2,1)S(1)}, bf16[64,2048]{1,0:T(8,128)(2,1)S(1)}, u32[]{:S(2)}, u32[]{:S(2)}) collective-permute-start(bf16[64,2048]{1,0:T(8,128)(2,1)S(1)} %get-tuple-element.67.rates_ref.refs_8_), channel_id=1, source_target_pairs={{0,1},{1,0},{2,3},{3,2},{4,5},{5,4},{6,7},{7,6},{8,9},{9,8},{10,11... | collective-permute-start | bytes 786440 | tf_op jit(solution)/shard_map/ppermute | solution.py:31
  61.0 4.9 %collective-permute-start.16 = (s16[2,64,384]{2,1,0:T(8,128)(2,1)S(1)}, s16[2,64,384]{2,1,0:T(8,128)(2,1)S(1)}, u32[]{:S(2)}, u32[]{:S(2)}) collective-permute-start(s16[2,64,384]{2,1,0:T(8,128)(2,1)S(1)} %get-tuple-element.70), channel_id=1, source_target_pairs={{0,4},{2,6},{4,0},{6,2},{8,12},{10,14},{12,8},{14,10},{1,5},{3,7},... | collective-permute-start | bytes 294920 | tf_op jit(solution)/shard_map/ppermute | solution.py:31
  62.7 10.7 %collective-permute-start.17 = (s16[2,64,384]{2,1,0:T(8,128)(2,1)S(1)}, s16[2,64,384]{2,1,0:T(8,128)(2,1)S(1)}, u32[]{:S(2)}, u32[]{:S(2)}) collective-permute-start(s16[2,64,384]{2,1,0:T(8,128)(2,1)S(1)} %get-tuple-element.71), channel_id=1, source_target_pairs={{0,8},{2,10},{4,12},{6,14},{8,0},{10,2},{12,4},{14,6},{1,9},{3,11}... | collective-permute-start | bytes 294920 | tf_op jit(solution)/shard_map/ppermute | solution.py:31
  63.7 9.6 %collective-permute-start.18 = (s16[2,64,384]{2,1,0:T(8,128)(2,1)S(1)}, s16[2,64,384]{2,1,0:T(8,128)(2,1)S(1)}, u32[]{:S(2)}, u32[]{:S(2)}) collective-permute-start(s16[2,64,384]{2,1,0:T(8,128)(2,1)S(1)} %get-tuple-element.72), channel_id=1, source_target_pairs={{0,12},{2,14},{4,8},{6,10},{8,4},{10,6},{12,0},{14,2},{1,13},{3,15... | collective-permute-start | bytes 294920 | tf_op jit(solution)/shard_map/ppermute | solution.py:31
  73.4 1.7 %collective-permute-start.19 = (bf16[128,384]{1,0:T(8,128)(2,1)S(1)}, bf16[128,384]{1,0:T(8,128)(2,1)S(1)}, u32[]{:S(2)}, u32[]{:S(2)}) collective-permute-start(bf16[128,384]{1,0:T(8,128)(2,1)S(1)} %drive.5.refs_2_), channel_id=1, source_target_pairs={{0,1},{1,0},{2,3},{3,2},{4,5},{5,4},{6,7},{7,6},{8,9},{9,8},{10,11... | collective-permute-start | bytes 294920 | tf_op jit(solution)/shard_map/ppermute | solution.py:31
  77.4 2.2 %collective-permute-start.20 = (bf16[64,2048]{1,0:T(8,128)(2,1)S(1)}, bf16[64,2048]{1,0:T(8,128)(2,1)S(1)}, u32[]{:S(2)}, u32[]{:S(2)}) collective-permute-start(bf16[64,2048]{1,0:T(8,128)(2,1)S(1)} %get-tuple-element.73.rates_ref.refs_9_), channel_id=1, source_target_pairs={{0,1},{1,0},{2,3},{3,2},{4,5},{5,4},{6,7},{7,6},{8,9},{9,8},{10,11... | collective-permute-start | bytes 786440 | tf_op jit(solution)/shard_map/ppermute | solution.py:31

commit v2 on v1

--- a/solution.py
+++ b/solution.py
@@ -202,24 +202,57 @@
     )(unit, rates, facing, own, *[far(array) for array in (w_rec, extra, state, leak)])
 
 
-def pick_kernel(count, *refs):
-    owns, others, (pick_own_ref, pick_other_ref, out_ref) = refs[:count], refs[count : 2 * count], refs[2 * count :]
-    left = jnp.concatenate([ref[...] for ref in owns], axis=0)
-    right = jnp.concatenate([ref[...] for ref in others], axis=0)
-    picked = matmul(left, pick_own_ref[...]) + matmul(right, pick_other_ref[...])
+def stacked(refs):
+    return jnp.concatenate([ref[...] for ref in refs], axis=0)
+
+
+def pick_half_kernel(*refs):
+    rates, (select_ref, out_ref) = refs[:-2], refs[-2:]
+    out_ref[...] = matmul(stacked(rates), select_ref[...])
+
+
+def pick_half(rates, select):
+    return pl.pallas_call(
+        pick_half_kernel,
+        out_shape=shaped((len(rates) * rates[0].shape[0], select.shape[1]), F32),
+        in_specs=[VM] * (len(rates) + 1),
+        out_specs=VM,
+        compiler_params=params(),
+        name="pick_half",
+    )(*rates, select)
+
+
+def pick_kernel(*refs):
+    rates, (half_ref, select_ref, out_ref) = refs[:-3], refs[-3:]
+    picked = half_ref[...] + matmul(stacked(rates), select_ref[...])
     out_ref[...] = picked.astype(BF16).reshape(out_ref.shape)
 
 
-def pick(pairs, selects):
-    owns, others = zip(*pairs)
-    return pl.pallas_call(
-        functools.partial(pick_kernel, len(pairs)),
-        out_shape=shaped((len(pairs), owns[0].shape[0], selects[0].shape[1]), BF16),
-        in_specs=[VM] * (2 * len(pairs) + 2),
+def pick(rates, half, select):
+    return pl.pallas_call(
+        pick_kernel,
+        out_shape=shaped((len(rates), rates[0].shape[0], select.shape[1]), BF16),
+        in_specs=[VM] * (len(rates) + 2),
         out_specs=VM,
         compiler_params=params(),
         name="pick",
-    )(*owns, *others, *selects)
+    )(*rates, half, select)
+
+
+def half_kernel(drive_ref, weight_ref, out_ref):
+    for cols in columns_of(out_ref.shape[1]):
+        out_ref[:, cols] = matmul(drive_ref[...], weight_ref[:, cols])
+
+
+def half_current(drive, weight):
+    return pl.pallas_call(
+        half_kernel,
+        out_shape=shaped((drive.shape[0], weight.shape[1]), F32),
+        in_specs=[VM, VM],
+        out_specs=VM,
+        compiler_params=params(),
+        name="half",
+    )(drive, weight)
 
 
 def own_kernel(rates_ref, weight_ref, extra_ref, out_ref):
@@ -247,7 +280,7 @@
     refs = list(refs)
     rates_ref, weight_ref = (refs.pop(0), refs.pop(0)) if flow else (None, None)
     if drives:
-        d0_ref, d1_ref, i0_ref, i1_ref = (refs.pop(0) for _ in range(4))
+        half_ref, drive_ref, in_ref = (refs.pop(0) for _ in range(3))
     else:
         kept_ref = refs.pop(0)
     trials = state_ref.shape[0]
@@ -265,9 +298,8 @@
         for ref in (first_ref, second_ref):
             send(ref, all_ref.at[pl.ds(old, ref.shape[0])])
             old += ref.shape[0]
-        left = jnp.concatenate([ref[...] for ref in refs[:count]], axis=0)
-        right = jnp.concatenate([ref[...] for ref in refs[count:]], axis=0)
-        picked = matmul(left, pick_own_ref[...]) + matmul(right, pick_other_ref[...])
+        picked = matmul(stacked(refs[:count]), pick_own_ref[...])
+        picked += matmul(stacked(refs[count:]), pick_other_ref[...])
         fresh[...] = picked.astype(BF16).reshape(fresh.shape)
         send(fresh, all_ref.at[pl.ds(old, fresh.shape[0])])
     else:
@@ -277,7 +309,7 @@
         if flow:
             total += matmul(rates_ref[...], weight_ref[:, cols])
         if drives:
-            current = matmul(d0_ref[...], i0_ref[:, cols]) + matmul(d1_ref[...], i1_ref[:, cols])
+            current = half_ref[:, cols] + matmul(drive_ref[...], in_ref[:, cols])
             refs[2][:, cols] = current[trials:, :]
             total += current[:trials, :]
         else:
@@ -422,12 +454,14 @@
 
     def drive_pair(group):
         own = drive_of(*group)
-        return [own, crossed(own, "unit", 1), in_own, in_other]
+        met = crossed(own, "unit", 1)
+        return [half_current(own, in_own), met, in_other]
 
     def share(value, first):
         return [(0, first, value), (1, first, crossed(value, "area", 1))]
 
-    fresh = pick([(rates, other)], selects)
+    half = pick_half([rates], select_own)
+    fresh = pick([other], half, select_other)
     sent = send((0, 1))
     known += share(fresh, 0)
     rec_other, external, state, leak_row, total = opening(
@@ -440,7 +474,9 @@
             pairs.append((rates, other))
             flow = (other, rec_other)
             if time == 2:
-                fresh = pick(pairs, selects)
+                owns, others = zip(*pairs)
+                half = pick_half(owns, select_own)
+                fresh = pick(others, half, select_other)
                 old.append(fresh)
                 pairs = []
                 known += share(fresh, 1)

time: 82.8 us -> 82.2 us (level)
  waiting for transfers between devices: 27.1 us -> 26.2 us
    pallas_call x2 -> x7, Pallas kernels: 1.52 us -> 3.11 us  [the longest x3 1.32 us: half_current(): pl.pallas_call(half_kernel, out_shape=shaped((drive.shape[0], weight.shap...]
    ppermute x21, waiting for transfers between devices: 27.1 us -> 26.2 us  [crossed(): return lax.ppermute(value, axis, pairs)]
  transfers between devices with their start and end apart: 21 -> 21, of which waited for: 9 -> 9; matrix products, arithmetic and copies ran while one was open for 1% -> 1% of each run, Pallas kernels for 28% -> 30%
where the time goes in v2:
time: 82.2 us; the launch traced here: 82 us
  Pallas kernels  33.4 us (41%)
  waiting for transfers between devices  26.2 us (32%)
  starting transfers between devices  20.3 us (25%)
  other arithmetic  1.12 us (1%)
  between operations  1.08 us (1%)
    ppermute x21, waiting for transfers between devices, crossed(): return lax.ppermute(value, axis, pairs)  26.2 us
    ppermute x21, starting transfers between devices, crossed(): return lax.ppermute(value, axis, pairs)  20.3 us
    pallas_call x5, Pallas kernels, own_part(): pl.pallas_call(own_kernel, out_shape=shaped(extra.shape, F32), in_specs=[...  7.99 us
    pallas_call x5, Pallas kernels, step(): pl.pallas_call(functools.partial(step_kernel, flow is not None, drives is...  7.89 us
    pallas_call x1, Pallas kernels, stage(): pl.pallas_call(functools.partial(stage_kernel, lines), out_shape=(pltpu.V...  5.25 us
    pallas_call x1, Pallas kernels, opening(): pl.pallas_call(opening_kernel, out_shape=(pltpu.VMEM(own.shape, BF16), pl...  4.44 us
    pallas_call x1, Pallas kernels, last_step(): pl.pallas_call(functools.partial(step_kernel, True, False, True), out_sha...  2.86 us
  transfers between devices with their start and end apart: 21, of which 9 were waited for; matrix products, arithmetic and copies ran while one was open for 1% of the time, Pallas kernels for 30%

profile of v2, /device:TPU:0, one launch (start us, length us, event | category | flops | bytes accessed | tf_op | source)
XLA Modules:
  0.0 82.0 jit_solution(11918817856118257070)
XLA Ops:
  0.6 3.0 %collective-permute-start.1 = (bf16[6,64,384]{2,1,0:T(8,128)(2,1)}, bf16[6,64,384]{2,1,0:T(8,128)(2,1)S(1)}, u32[]{:S(2)}, u32[]{:S(2)}) collective-permute-start(bf16[6,64,384]{2,1,0:T(8,128)(2,1)} %history_far.1), channel_id=1, source_target_pairs={{0,2},{2,0},{4,6},{6,4},{8,10},{10,8},{12,14},{14,12},{1,3},{3,1},... | collective-permute-start | bytes 884744 | tf_op jit(solution)/shard_map/ppermute | solution.py:31
  3.7 1.1 %tanh_convert_fusion.rates_ref.refs_0_ = bf16[64,2048]{1,0:T(8,128)(2,1)S(1)} fusion(f32[64,2048]{1,0:T(8,128)} %state_far.1), kind=kLoop, calls=%fused_computation | loop fusion | flops 131072 | bytes 786432 | tf_op jit(solution)/shard_map/convert_element_type | solution.py:440
  4.9 5.3 %stage.1 = (bf16[6,64,384]{2,1,0:T(8,128)(2,1)S(1)}, bf16[2048,2048]{1,0:T(8,128)(2,1)S(1)}, bf16[384,2048]{1,0:T(8,128)(2,1)S(1)}, bf16[384,2048]{1,0:T(8,128)(...) custom-call(s32[1]{0:T(128)} %bitcast.1.area_ref, s32[1]{0:T(128)} %bitcast.unit_ref, ...), custom_call_target="tpu_custom_call" | custom-call | tf_op jit(solution)/shard_map/stage/pallas_call | solution.py:127
  10.1 0.8 collective-permute-done.1.refs_1_
  10.9 0.5 partials.3
  11.4 1.9 %collective-permute-start.2 = (s16[2,64,384]{2,1,0:T(8,128)(2,1)S(1)}, s16[2,64,384]{2,1,0:T(8,128)(2,1)S(1)}, u32[]{:S(2)}, u32[]{:S(2)}) collective-permute-start(s16[2,64,384]{2,1,0:T(8,128)(2,1)S(1)} %get-tuple-element.46), channel_id=1, source_target_pairs={{0,4},{2,6},{4,0},{6,2},{8,12},{10,14},{12,8},{14,10},{1,5},{3,7},... | collective-permute-start | bytes 294920 | tf_op jit(solution)/shard_map/ppermute | solution.py:31
  13.3 2.6 %collective-permute-start.3 = (s16[2,64,384]{2,1,0:T(8,128)(2,1)S(1)}, s16[2,64,384]{2,1,0:T(8,128)(2,1)S(1)}, u32[]{:S(2)}, u32[]{:S(2)}) collective-permute-start(s16[2,64,384]{2,1,0:T(8,128)(2,1)S(1)} %get-tuple-element.47), channel_id=1, source_target_pairs={{0,8},{2,10},{4,12},{6,14},{8,0},{10,2},{12,4},{14,6},{1,9},{3,11}... | collective-permute-start | bytes 294920 | tf_op jit(solution)/shard_map/ppermute | solution.py:31
  15.9 0.2 collective-permute-done.2.refs_0_
  16.1 7.3 %collective-permute-done.3.refs_1_ = s16[2,64,384]{2,1,0:T(8,128)(2,1)S(1)} collective-permute-done((s16[2,64,384]{2,1,0:T(8,128)(2,1)S(1)}, s16[2,64,384]{2,1,0:T(8,128)(2,1)S(1)}, u32[]{:S(2)}, u32[]{:S(2)}) %collective-permute-start.3) | collective-permute-done | bytes 98336 | tf_op jit(solution)/shard_map/ppermute | solution.py:31
  23.4 0.1 drive.3.drive_ref
  23.6 4.4 %opening.1 = (bf16[2048,2048]{1,0:T(8,128)(2,1)S(1)}, f32[64,2048]{1,0:T(8,128)S(1)}, f32[64,2048]{1,0:T(8,128)S(1)}, f32[1,2048]{1,0:T(1,128)S(1)}, f32[64,2048]{1,0:T(8,128)S(1)}) custom-call(s32[1]{0:T(128)} %bitcast.unit_ref, bf16[64,2048]{1,0:T(8,128)(2,1)S(1)} %tanh_convert_fusion.rates_ref.refs_0_, ...), custom_call_target="tpu_custom_call" | custom-call | tf_op jit(solution)/shard_map/opening/pallas_call | solution.py:188
  28.0 0.4 half.3.refs_0_
  28.5 0.5 step.5
  29.0 0.6 collective-permute-start.6
  29.5 1.6 %own_part.5.sum_ref = f32[64,2048]{1,0:T(8,128)S(1)} custom-call(bf16[64,2048]{1,0:T(8,128)(2,1)S(1)} %get-tuple-element.51.rates_ref.refs_0_, bf16[2048,2048]{1,0:T(8,128)(2,1)S(1)} %get-tuple-element.39.own_ref.weight_ref, f32[64,2048]{1,0:T(8,128)S(1)} %get-tuple-element.52.extra_ref), custom_call_target="tpu_custom_call" | custom-call | tf_op jit(solution)/shard_map/own_part/pallas_call | solution.py:264
  31.1 1.7 %step.6 = (f32[64,2048]{1,0:T(8,128)S(1)}, bf16[64,2048]{1,0:T(8,128)(2,1)S(1)}) custom-call(f32[64,2048]{1,0:T(8,128)S(1)} %own_part.5.sum_ref, f32[64,2048]{1,0:T(8,128)S(1)} %get-tuple-element.53.state_ref, f32[1,2048]{1,0:T(1,128)S(1)} %get-tuple-element.42.leak_ref, bf16[64,2048]{1,0:T(8,128)(2,1)S(1)} %collective-permute-done.6.refs_0_, ...), custom_call_target="tpu_custom_call" | custom-call | tf_op jit(solution)/shard_map/step/pallas_call | solution.py:335
  32.9 0.4 pick_half.2.refs_1_
  33.3 0.4 pick.2.refs_2_.refs_5_
  33.6 1.0 %collective-permute-start.8 = (bf16[1,64,384]{2,1,0:T(8,128)(2,1)S(1)}, bf16[1,64,384]{2,1,0:T(8,128)(2,1)S(1)}, u32[]{:S(2)}, u32[]{:S(2)}) collective-permute-start(bf16[1,64,384]{2,1,0:T(8,128)(2,1)S(1)} %pick.2.refs_2_.refs_5_), channel_id=1, source_target_pairs={{0,2},{2,0},{4,6},{6,4},{8,10},{10,8},{12,14},{14,12},{1,3},{3,1},... | collective-permute-start | bytes 147464 | tf_op jit(solution)/shard_map/ppermute | solution.py:31
  34.7 3.2 %collective-permute-done.8.refs_3_ = bf16[1,64,384]{2,1,0:T(8,128)(2,1)S(1)} collective-permute-done((bf16[1,64,384]{2,1,0:T(8,128)(2,1)S(1)}, bf16[1,64,384]{2,1,0:T(8,128)(2,1)S(1)}, u32[]{:S(2)}, u32[]{:S(2)}) %collective-permute-start.8) | collective-permute-done | bytes 49184 | tf_op jit(solution)/shard_map/ppermute | solution.py:31
  37.8 0.5 partials.4
  38.4 2.7 %collective-permute-start.10 = (s16[2,64,384]{2,1,0:T(8,128)(2,1)S(1)}, s16[2,64,384]{2,1,0:T(8,128)(2,1)S(1)}, u32[]{:S(2)}, u32[]{:S(2)}) collective-permute-start(s16[2,64,384]{2,1,0:T(8,128)(2,1)S(1)} %get-tuple-element.62), channel_id=1, source_target_pairs={{0,8},{2,10},{4,12},{6,14},{8,0},{10,2},{12,4},{14,6},{1,9},{3,11}... | collective-permute-start | bytes 294920 | tf_op jit(solution)/shard_map/ppermute | solution.py:31
  41.1 1.3 %collective-permute-start.11 = (s16[2,64,384]{2,1,0:T(8,128)(2,1)S(1)}, s16[2,64,384]{2,1,0:T(8,128)(2,1)S(1)}, u32[]{:S(2)}, u32[]{:S(2)}) collective-permute-start(s16[2,64,384]{2,1,0:T(8,128)(2,1)S(1)} %get-tuple-element.63), channel_id=1, source_target_pairs={{0,12},{2,14},{4,8},{6,10},{8,4},{10,6},{12,0},{14,2},{1,13},{3,15... | collective-permute-start | bytes 294920 | tf_op jit(solution)/shard_map/ppermute | solution.py:31
  42.4 6.5 %collective-permute-done.10.refs_1_ = s16[2,64,384]{2,1,0:T(8,128)(2,1)S(1)} collective-permute-done((s16[2,64,384]{2,1,0:T(8,128)(2,1)S(1)}, s16[2,64,384]{2,1,0:T(8,128)(2,1)S(1)}, u32[]{:S(2)}, u32[]{:S(2)}) %collective-permute-start.10) | collective-permute-done | bytes 98336 | tf_op jit(solution)/shard_map/ppermute | solution.py:31
  48.9 0.2 collective-permute-done.9.refs_0_
  49.3 0.4 half.4.refs_2_
  49.8 1.6 %own_part.6.sum_ref = f32[64,2048]{1,0:T(8,128)S(1)} custom-call(bf16[64,2048]{1,0:T(8,128)(2,1)S(1)} %get-tuple-element.56.rates_ref.refs_1_, bf16[2048,2048]{1,0:T(8,128)(2,1)S(1)} %get-tuple-element.39.own_ref.weight_ref, f32[64,2048]{1,0:T(8,128)S(1)} %get-tuple-element.52.extra_ref), custom_call_target="tpu_custom_call" | custom-call | tf_op jit(solution)/shard_map/own_part/pallas_call | solution.py:264
  51.4 2.0 %step.7 = (f32[64,2048]{1,0:T(8,128)S(1)}, bf16[64,2048]{1,0:T(8,128)(2,1)S(1)}, f32[64,2048]{1,0:T(8,128)S(1)}) custom-call(f32[64,2048]{1,0:T(8,128)S(1)} %own_part.6.sum_ref, f32[64,2048]{1,0:T(8,128)S(1)} %get-tuple-element.57.state_ref, f32[1,2048]{1,0:T(1,128)S(1)} %get-tuple-element.42.leak_ref, ...), custom_call_target="tpu_custom_call" | custom-call | tf_op jit(solution)/shard_map/step/pallas_call | solution.py:335
  53.5 0.6 collective-permute-start.13
  54.0 0.6 pick_half.3.refs_2_
  54.6 0.4 pick.3.refs_4_.refs_6_
  55.1 1.1 %collective-permute-start.15 = (bf16[2,64,384]{2,1,0:T(8,128)(2,1)S(1)}, bf16[2,64,384]{2,1,0:T(8,128)(2,1)S(1)}, u32[]{:S(2)}, u32[]{:S(2)}) collective-permute-start(bf16[2,64,384]{2,1,0:T(8,128)(2,1)S(1)} %pick.3.refs_4_.refs_6_), channel_id=1, source_target_pairs={{0,2},{2,0},{4,6},{6,4},{8,10},{10,8},{12,14},{14,12},{1,3},{3,1},... | collective-permute-start | bytes 294920 | tf_op jit(solution)/shard_map/ppermute | solution.py:31
  56.2 1.6 %own_part.7.sum_ref = f32[64,2048]{1,0:T(8,128)S(1)} custom-call(bf16[64,2048]{1,0:T(8,128)(2,1)S(1)} %get-tuple-element.64.rates_ref.refs_7_, bf16[2048,2048]{1,0:T(8,128)(2,1)S(1)} %get-tuple-element.39.own_ref.weight_ref, f32[64,2048]{1,0:T(8,128)S(1)} %get-tuple-element.52.extra_ref), custom_call_target="tpu_custom_call" | custom-call | tf_op jit(solution)/shard_map/own_part/pallas_call | solution.py:264
  57.8 1.7 %step.8 = (f32[64,2048]{1,0:T(8,128)S(1)}, bf16[64,2048]{1,0:T(8,128)(2,1)S(1)}) custom-call(f32[64,2048]{1,0:T(8,128)S(1)} %own_part.7.sum_ref, f32[64,2048]{1,0:T(8,128)S(1)} %get-tuple-element.65.state_ref, f32[1,2048]{1,0:T(1,128)S(1)} %get-tuple-element.42.leak_ref, bf16[64,2048]{1,0:T(8,128)(2,1)S(1)} %collective-permute-done.13.refs_0_.refs_10_, ...), custom_call_target="tpu_custom_call" | custom-call | tf_op jit(solution)/shard_map/step/pallas_call | solution.py:335
  59.5 0.3 collective-permute-done.15.refs_5_
  59.8 0.5 partials.5
  60.4 1.5 %collective-permute-start.16 = (s16[2,64,384]{2,1,0:T(8,128)(2,1)S(1)}, s16[2,64,384]{2,1,0:T(8,128)(2,1)S(1)}, u32[]{:S(2)}, u32[]{:S(2)}) collective-permute-start(s16[2,64,384]{2,1,0:T(8,128)(2,1)S(1)} %get-tuple-element.70), channel_id=1, source_target_pairs={{0,4},{2,6},{4,0},{6,2},{8,12},{10,14},{12,8},{14,10},{1,5},{3,7},... | collective-permute-start | bytes 294920 | tf_op jit(solution)/shard_map/ppermute | solution.py:31
  61.8 1.5 %collective-permute-start.17 = (s16[2,64,384]{2,1,0:T(8,128)(2,1)S(1)}, s16[2,64,384]{2,1,0:T(8,128)(2,1)S(1)}, u32[]{:S(2)}, u32[]{:S(2)}) collective-permute-start(s16[2,64,384]{2,1,0:T(8,128)(2,1)S(1)} %get-tuple-element.71), channel_id=1, source_target_pairs={{0,8},{2,10},{4,12},{6,14},{8,0},{10,2},{12,4},{14,6},{1,9},{3,11}... | collective-permute-start | bytes 294920 | tf_op jit(solution)/shard_map/ppermute | solution.py:31
  63.4 1.4 %collective-permute-start.18 = (s16[2,64,384]{2,1,0:T(8,128)(2,1)S(1)}, s16[2,64,384]{2,1,0:T(8,128)(2,1)S(1)}, u32[]{:S(2)}, u32[]{:S(2)}) collective-permute-start(s16[2,64,384]{2,1,0:T(8,128)(2,1)S(1)} %get-tuple-element.72), channel_id=1, source_target_pairs={{0,12},{2,14},{4,8},{6,10},{8,4},{10,6},{12,0},{14,2},{1,13},{3,15... | collective-permute-start | bytes 294920 | tf_op jit(solution)/shard_map/ppermute | solution.py:31
  64.8 1.6 %collective-permute-done.16.refs_0_ = s16[2,64,384]{2,1,0:T(8,128)(2,1)S(1)} collective-permute-done((s16[2,64,384]{2,1,0:T(8,128)(2,1)S(1)}, s16[2,64,384]{2,1,0:T(8,128)(2,1)S(1)}, u32[]{:S(2)}, u32[]{:S(2)}) %collective-permute-start.16) | collective-permute-done | bytes 98336 | tf_op jit(solution)/shard_map/ppermute | solution.py:31
  66.4 6.1 %collective-permute-done.17.refs_1_ = s16[2,64,384]{2,1,0:T(8,128)(2,1)S(1)} collective-permute-done((s16[2,64,384]{2,1,0:T(8,128)(2,1)S(1)}, s16[2,64,384]{2,1,0:T(8,128)(2,1)S(1)}, u32[]{:S(2)}, u32[]{:S(2)}) %collective-permute-start.17) | collective-permute-done | bytes 98336 | tf_op jit(solution)/shard_map/ppermute | solution.py:31
  72.5 0.1 drive.5.drive_ref
  72.7 0.4 half.5.refs_2_
  73.1 1.6 %own_part.8.sum_ref = f32[64,2048]{1,0:T(8,128)S(1)} custom-call(bf16[64,2048]{1,0:T(8,128)(2,1)S(1)} %get-tuple-element.67.rates_ref.refs_8_, bf16[2048,2048]{1,0:T(8,128)(2,1)S(1)} %get-tuple-element.39.own_ref.weight_ref, f32[64,2048]{1,0:T(8,128)S(1)} %get-tuple-element.52.extra_ref), custom_call_target="tpu_custom_call" | custom-call | tf_op jit(solution)/shard_map/own_part/pallas_call | solution.py:264
  74.8 2.0 %step.9 = (f32[64,2048]{1,0:T(8,128)S(1)}, bf16[64,2048]{1,0:T(8,128)(2,1)S(1)}, f32[64,2048]{1,0:T(8,128)S(1)}) custom-call(f32[64,2048]{1,0:T(8,128)S(1)} %own_part.8.sum_ref, f32[64,2048]{1,0:T(8,128)S(1)} %get-tuple-element.68.state_ref, f32[1,2048]{1,0:T(1,128)S(1)} %get-tuple-element.42.leak_ref, ...), custom_call_target="tpu_custom_call" | custom-call | tf_op jit(solution)/shard_map/step/pallas_call | solution.py:335
  76.8 0.6 collective-permute-start.20
  77.4 1.6 %own_part.9.sum_ref = f32[64,2048]{1,0:T(8,128)S(1)} custom-call(bf16[64,2048]{1,0:T(8,128)(2,1)S(1)} %get-tuple-element.73.rates_ref.refs_9_, bf16[2048,2048]{1,0:T(8,128)(2,1)S(1)} %get-tuple-element.39.own_ref.weight_ref, f32[64,2048]{1,0:T(8,128)S(1)} %get-tuple-element.52.extra_ref), custom_call_target="tpu_custom_call" | custom-call | tf_op jit(solution)/shard_map/own_part/pallas_call | solution.py:264
  79.0 2.9 %last_step.1 = (f32[64,2048]{1,0:T(8,128)}, bf16[6,64,384]{2,1,0:T(8,128)(2,1)}) custom-call(f32[64,2048]{1,0:T(8,128)S(1)} %own_part.9.sum_ref, f32[64,2048]{1,0:T(8,128)S(1)} %get-tuple-element.74.state_ref, f32[1,2048]{1,0:T(1,128)S(1)} %get-tuple-element.42.leak_ref, bf16[64,2048]{1,0:T(8,128)(2,1)S(1)} %collective-permute-done.20.refs_0_.refs_12_, ...), custom_call_target="tpu_custom_call" | custom-call | tf_op jit(solution)/shard_map/last_step/pallas_call | solution.py:350
  (21 shorter events, 0.6 us)
Async XLA Ops:
  0.6 10.3 %collective-permute-start.1 = (bf16[6,64,384]{2,1,0:T(8,128)(2,1)}, bf16[6,64,384]{2,1,0:T(8,128)(2,1)S(1)}, u32[]{:S(2)}, u32[]{:S(2)}) collective-permute-start(bf16[6,64,384]{2,1,0:T(8,128)(2,1)} %history_far.1), channel_id=1, source_target_pairs={{0,2},{2,0},{4,6},{6,4},{8,10},{10,8},{12,14},{14,12},{1,3},{3,1},... | collective-permute-start | bytes 884744 | tf_op jit(solution)/shard_map/ppermute | solution.py:31
  4.8 18.8 %collective-permute-start = (bf16[64,2048]{1,0:T(8,128)(2,1)S(1)}, bf16[64,2048]{1,0:T(8,128)(2,1)S(1)}, u32[]{:S(2)}, u32[]{:S(2)}) collective-permute-start(bf16[64,2048]{1,0:T(8,128)(2,1)S(1)} %tanh_convert_fusion.rates_ref.refs_0_), channel_id=1, source_target_pairs={{0,1},{1,0},{2,3},{3,2},{4,5},{5,4},{6,7},{7,6},{8,9},{9,8},{10,11... | collective-permute-start | bytes 786440 | tf_op jit(solution)/shard_map/ppermute | solution.py:31
  11.4 4.7 %collective-permute-start.2 = (s16[2,64,384]{2,1,0:T(8,128)(2,1)S(1)}, s16[2,64,384]{2,1,0:T(8,128)(2,1)S(1)}, u32[]{:S(2)}, u32[]{:S(2)}) collective-permute-start(s16[2,64,384]{2,1,0:T(8,128)(2,1)S(1)} %get-tuple-element.46), channel_id=1, source_target_pairs={{0,4},{2,6},{4,0},{6,2},{8,12},{10,14},{12,8},{14,10},{1,5},{3,7},... | collective-permute-start | bytes 294920 | tf_op jit(solution)/shard_map/ppermute | solution.py:31
  13.3 10.1 %collective-permute-start.3 = (s16[2,64,384]{2,1,0:T(8,128)(2,1)S(1)}, s16[2,64,384]{2,1,0:T(8,128)(2,1)S(1)}, u32[]{:S(2)}, u32[]{:S(2)}) collective-permute-start(s16[2,64,384]{2,1,0:T(8,128)(2,1)S(1)} %get-tuple-element.47), channel_id=1, source_target_pairs={{0,8},{2,10},{4,12},{6,14},{8,0},{10,2},{12,4},{14,6},{1,9},{3,11}... | collective-permute-start | bytes 294920 | tf_op jit(solution)/shard_map/ppermute | solution.py:31
  15.9 7.5 %collective-permute-start.4 = (s16[2,64,384]{2,1,0:T(8,128)(2,1)S(1)}, s16[2,64,384]{2,1,0:T(8,128)(2,1)S(1)}, u32[]{:S(2)}, u32[]{:S(2)}) collective-permute-start(s16[2,64,384]{2,1,0:T(8,128)(2,1)S(1)} %get-tuple-element.48), channel_id=1, source_target_pairs={{0,12},{2,14},{4,8},{6,10},{8,4},{10,6},{12,0},{14,2},{1,13},{3,15... | collective-permute-start | bytes 294920 | tf_op jit(solution)/shard_map/ppermute | solution.py:31
  23.5 5.0 %collective-permute-start.5 = (bf16[128,384]{1,0:T(8,128)(2,1)S(1)}, bf16[128,384]{1,0:T(8,128)(2,1)S(1)}, u32[]{:S(2)}, u32[]{:S(2)}) collective-permute-start(bf16[128,384]{1,0:T(8,128)(2,1)S(1)} %drive.3.drive_ref), channel_id=1, source_target_pairs={{0,1},{1,0},{2,3},{3,2},{4,5},{5,4},{6,7},{7,6},{8,9},{9,8},{10,11... | collective-permute-start | bytes 294920 | tf_op jit(solution)/shard_map/ppermute | solution.py:31
  29.0 2.2 %collective-permute-start.6 = (bf16[64,2048]{1,0:T(8,128)(2,1)S(1)}, bf16[64,2048]{1,0:T(8,128)(2,1)S(1)}, u32[]{:S(2)}, u32[]{:S(2)}) collective-permute-start(bf16[64,2048]{1,0:T(8,128)(2,1)S(1)} %get-tuple-element.51.rates_ref.refs_0_), channel_id=1, source_target_pairs={{0,1},{1,0},{2,3},{3,2},{4,5},{5,4},{6,7},{7,6},{8,9},{9,8},{10,11... | collective-permute-start | bytes 786440 | tf_op jit(solution)/shard_map/ppermute | solution.py:31
  32.8 18.6 %collective-permute-start.7 = (bf16[64,2048]{1,0:T(8,128)(2,1)S(1)}, bf16[64,2048]{1,0:T(8,128)(2,1)S(1)}, u32[]{:S(2)}, u32[]{:S(2)}) collective-permute-start(bf16[64,2048]{1,0:T(8,128)(2,1)S(1)} %get-tuple-element.56.rates_ref.refs_1_), channel_id=1, source_target_pairs={{0,1},{1,0},{2,3},{3,2},{4,5},{5,4},{6,7},{7,6},{8,9},{9,8},{10,11... | collective-permute-start | bytes 786440 | tf_op jit(solution)/shard_map/ppermute | solution.py:31
  33.6 4.2 %collective-permute-start.8 = (bf16[1,64,384]{2,1,0:T(8,128)(2,1)S(1)}, bf16[1,64,384]{2,1,0:T(8,128)(2,1)S(1)}, u32[]{:S(2)}, u32[]{:S(2)}) collective-permute-start(bf16[1,64,384]{2,1,0:T(8,128)(2,1)S(1)} %pick.2.refs_2_.refs_5_), channel_id=1, source_target_pairs={{0,2},{2,0},{4,6},{6,4},{8,10},{10,8},{12,14},{14,12},{1,3},{3,1},... | collective-permute-start | bytes 147464 | tf_op jit(solution)/shard_map/ppermute | solution.py:31
  38.4 10.6 %collective-permute-start.10 = (s16[2,64,384]{2,1,0:T(8,128)(2,1)S(1)}, s16[2,64,384]{2,1,0:T(8,128)(2,1)S(1)}, u32[]{:S(2)}, u32[]{:S(2)}) collective-permute-start(s16[2,64,384]{2,1,0:T(8,128)(2,1)S(1)} %get-tuple-element.62), channel_id=1, source_target_pairs={{0,8},{2,10},{4,12},{6,14},{8,0},{10,2},{12,4},{14,6},{1,9},{3,11}... | collective-permute-start | bytes 294920 | tf_op jit(solution)/shard_map/ppermute | solution.py:31
  41.1 7.9 %collective-permute-start.11 = (s16[2,64,384]{2,1,0:T(8,128)(2,1)S(1)}, s16[2,64,384]{2,1,0:T(8,128)(2,1)S(1)}, u32[]{:S(2)}, u32[]{:S(2)}) collective-permute-start(s16[2,64,384]{2,1,0:T(8,128)(2,1)S(1)} %get-tuple-element.63), channel_id=1, source_target_pairs={{0,12},{2,14},{4,8},{6,10},{8,4},{10,6},{12,0},{14,2},{1,13},{3,15... | collective-permute-start | bytes 294920 | tf_op jit(solution)/shard_map/ppermute | solution.py:31
  42.4 6.8 %collective-permute-start.9 = (s16[2,64,384]{2,1,0:T(8,128)(2,1)S(1)}, s16[2,64,384]{2,1,0:T(8,128)(2,1)S(1)}, u32[]{:S(2)}, u32[]{:S(2)}) collective-permute-start(s16[2,64,384]{2,1,0:T(8,128)(2,1)S(1)} %get-tuple-element.61), channel_id=1, source_target_pairs={{0,4},{2,6},{4,0},{6,2},{8,12},{10,14},{12,8},{14,10},{1,5},{3,7},... | collective-permute-start | bytes 294920 | tf_op jit(solution)/shard_map/ppermute | solution.py:31
  49.2 2.1 %collective-permute-start.12 = (bf16[128,384]{1,0:T(8,128)(2,1)S(1)}, bf16[128,384]{1,0:T(8,128)(2,1)S(1)}, u32[]{:S(2)}, u32[]{:S(2)}) collective-permute-start(bf16[128,384]{1,0:T(8,128)(2,1)S(1)} %drive.4.drive_ref), channel_id=1, source_target_pairs={{0,1},{1,0},{2,3},{3,2},{4,5},{5,4},{6,7},{7,6},{8,9},{9,8},{10,11... | collective-permute-start | bytes 294920 | tf_op jit(solution)/shard_map/ppermute | solution.py:31
  53.5 4.3 %collective-permute-start.13 = (bf16[64,2048]{1,0:T(8,128)(2,1)S(1)}, bf16[64,2048]{1,0:T(8,128)(2,1)S(1)}, u32[]{:S(2)}, u32[]{:S(2)}) collective-permute-start(bf16[64,2048]{1,0:T(8,128)(2,1)S(1)} %get-tuple-element.64.rates_ref.refs_7_), channel_id=1, source_target_pairs={{0,1},{1,0},{2,3},{3,2},{4,5},{5,4},{6,7},{7,6},{8,9},{9,8},{10,11... | collective-permute-start | bytes 786440 | tf_op jit(solution)/shard_map/ppermute | solution.py:31
  55.1 4.8 %collective-permute-start.15 = (bf16[2,64,384]{2,1,0:T(8,128)(2,1)S(1)}, bf16[2,64,384]{2,1,0:T(8,128)(2,1)S(1)}, u32[]{:S(2)}, u32[]{:S(2)}) collective-permute-start(bf16[2,64,384]{2,1,0:T(8,128)(2,1)S(1)} %pick.3.refs_4_.refs_6_), channel_id=1, source_target_pairs={{0,2},{2,0},{4,6},{6,4},{8,10},{10,8},{12,14},{14,12},{1,3},{3,1},... | collective-permute-start | bytes 294920 | tf_op jit(solution)/shard_map/ppermute | solution.py:31
  59.4 15.3 %collective-permute-start.14 = (bf16[64,2048]{1,0:T(8,128)(2,1)S(1)}, bf16[64,2048]{1,0:T(8,128)(2,1)S(1)}, u32[]{:S(2)}, u32[]{:S(2)}) collective-permute-start(bf16[64,2048]{1,0:T(8,128)(2,1)S(1)} %get-tuple-element.67.rates_ref.refs_8_), channel_id=1, source_target_pairs={{0,1},{1,0},{2,3},{3,2},{4,5},{5,4},{6,7},{7,6},{8,9},{9,8},{10,11... | collective-permute-start | bytes 786440 | tf_op jit(solution)/shard_map/ppermute | solution.py:31
  60.4 6.0 %collective-permute-start.16 = (s16[2,64,384]{2,1,0:T(8,128)(2,1)S(1)}, s16[2,64,384]{2,1,0:T(8,128)(2,1)S(1)}, u32[]{:S(2)}, u32[]{:S(2)}) collective-permute-start(s16[2,64,384]{2,1,0:T(8,128)(2,1)S(1)} %get-tuple-element.70), channel_id=1, source_target_pairs={{0,4},{2,6},{4,0},{6,2},{8,12},{10,14},{12,8},{14,10},{1,5},{3,7},... | collective-permute-start | bytes 294920 | tf_op jit(solution)/shard_map/ppermute | solution.py:31
  61.8 10.7 %collective-permute-start.17 = (s16[2,64,384]{2,1,0:T(8,128)(2,1)S(1)}, s16[2,64,384]{2,1,0:T(8,128)(2,1)S(1)}, u32[]{:S(2)}, u32[]{:S(2)}) collective-permute-start(s16[2,64,384]{2,1,0:T(8,128)(2,1)S(1)} %get-tuple-element.71), channel_id=1, source_target_pairs={{0,8},{2,10},{4,12},{6,14},{8,0},{10,2},{12,4},{14,6},{1,9},{3,11}... | collective-permute-start | bytes 294920 | tf_op jit(solution)/shard_map/ppermute | solution.py:31
  63.4 9.1 %collective-permute-start.18 = (s16[2,64,384]{2,1,0:T(8,128)(2,1)S(1)}, s16[2,64,384]{2,1,0:T(8,128)(2,1)S(1)}, u32[]{:S(2)}, u32[]{:S(2)}) collective-permute-start(s16[2,64,384]{2,1,0:T(8,128)(2,1)S(1)} %get-tuple-element.72), channel_id=1, source_target_pairs={{0,12},{2,14},{4,8},{6,10},{8,4},{10,6},{12,0},{14,2},{1,13},{3,15... | collective-permute-start | bytes 294920 | tf_op jit(solution)/shard_map/ppermute | solution.py:31
  72.6 2.1 %collective-permute-start.19 = (bf16[128,384]{1,0:T(8,128)(2,1)S(1)}, bf16[128,384]{1,0:T(8,128)(2,1)S(1)}, u32[]{:S(2)}, u32[]{:S(2)}) collective-permute-start(bf16[128,384]{1,0:T(8,128)(2,1)S(1)} %drive.5.drive_ref), channel_id=1, source_target_pairs={{0,1},{1,0},{2,3},{3,2},{4,5},{5,4},{6,7},{7,6},{8,9},{9,8},{10,11... | collective-permute-start | bytes 294920 | tf_op jit(solution)/shard_map/ppermute | solution.py:31
  76.8 2.2 %collective-permute-start.20 = (bf16[64,2048]{1,0:T(8,128)(2,1)S(1)}, bf16[64,2048]{1,0:T(8,128)(2,1)S(1)}, u32[]{:S(2)}, u32[]{:S(2)}) collective-permute-start(bf16[64,2048]{1,0:T(8,128)(2,1)S(1)} %get-tuple-element.73.rates_ref.refs_9_), channel_id=1, source_target_pairs={{0,1},{1,0},{2,3},{3,2},{4,5},{5,4},{6,7},{7,6},{8,9},{9,8},{10,11... | collective-permute-start | bytes 786440 | tf_op jit(solution)/shard_map/ppermute | solution.py:31

commit v3 on v2

--- a/solution.py
+++ b/solution.py
@@ -255,6 +255,22 @@
     )(drive, weight)
 
 
+def full_kernel(half_ref, drive_ref, weight_ref, out_ref):
+    for cols in columns_of(out_ref.shape[1]):
+        out_ref[:, cols] = half_ref[:, cols] + matmul(drive_ref[...], weight_ref[:, cols])
+
+
+def full_current(half, drive, weight):
+    return pl.pallas_call(
+        full_kernel,
+        out_shape=shaped(half.shape, F32),
+        in_specs=[VM] * 3,
+        out_specs=VM,
+        compiler_params=params(),
+        name="full",
+    )(half, drive, weight)
+
+
 def own_kernel(rates_ref, weight_ref, extra_ref, out_ref):
     for cols in columns_of(out_ref.shape[1]):
         out_ref[:, cols] = extra_ref[:, cols] + matmul(rates_ref[...], weight_ref[:, cols])
@@ -276,7 +292,7 @@
     return state + leak_ref[:, cols] * (total - state)
 
 
-def step_kernel(flow, drives, last, sum_ref, state_ref, leak_ref, *refs):
+def step_kernel(flow, drives, row, last, sum_ref, state_ref, leak_ref, *refs):
     refs = list(refs)
     rates_ref, weight_ref = (refs.pop(0), refs.pop(0)) if flow else (None, None)
     if drives:
@@ -313,7 +329,7 @@
             refs[2][:, cols] = current[trials:, :]
             total += current[:trials, :]
         else:
-            total += kept_ref[:, cols]
+            total += kept_ref[row * trials : (row + 1) * trials, cols]
         state = renewed(cols, total, state_ref, leak_ref)
         state_buf[:, cols] = state
         if last:
@@ -324,7 +340,7 @@
         move.wait()
 
 
-def step(total, state, leak, flow, drives, kept):
+def step(total, state, leak, flow, drives, kept, row):
     outs = [shaped(state.shape, F32), shaped(state.shape, BF16)]
     given = list(flow or ())
     if drives:
@@ -333,7 +349,7 @@
     else:
         given.append(kept)
     return pl.pallas_call(
-        functools.partial(step_kernel, flow is not None, drives is not None, False),
+        functools.partial(step_kernel, flow is not None, drives is not None, row, False),
         out_shape=tuple(outs),
         in_specs=[VM] * (3 + len(given)),
         out_specs=(VM,) * len(outs),
@@ -348,7 +364,7 @@
     first = sum(value.shape[0] for value in old)
     given = [*flow, kept, *selects, *old, *owns, *others]
     return pl.pallas_call(
-        functools.partial(step_kernel, True, False, True),
+        functools.partial(step_kernel, True, False, 0, True),
         out_shape=(shaped(state.shape, F32), shaped((first + len(pairs), trials, part), BF16)),
         in_specs=[VM] * (3 + len(given)),
         out_specs=(HB, HB),
@@ -370,7 +386,8 @@
     return value.astype(jnp.int32).astype(F32) * (1.0 / CODE)
 
 
-def partial_kernel(times, lines, slots, coef_ref, *refs):
+def partial_kernel(times, lines, slots, base, final, coef_ref, *refs):
+    bases, refs = refs[:base], refs[base:]
     fields, outs = refs[: len(slots)], refs[len(slots) :]
     trials = fields[0].shape[-2]
     size = 16 if trials % 16 == 0 else trials
@@ -381,9 +398,11 @@
     for start in range(0, trials, size):
         band = slice(start, start + size)
         for index, time in enumerate(times):
-            totals = [None] * lines
+            totals = [ref[index, band, :] for ref in bases] or [None] * lines
             for who in range(2):
                 for lag in LAGS:
+                    if (who, time - lag) not in spans:
+                        continue
                     ref, pos = spans[who, time - lag]
                     value = ref[pos, band, :].astype(F32)
                     for line in range(lines):
@@ -391,20 +410,23 @@
                         term = coef_ref[row : row + 1, :] * value
                         totals[line] = term if totals[line] is None else totals[line] + term
             for line in range(lines):
-                outs[line][index, band, :] = totals[line] if line == 0 else coded(totals[line])
-
-
-def partials(coef, times, lines, fields):
+                sent = final and line > 0
+                outs[line][index, band, :] = coded(totals[line]) if sent else totals[line]
+
+
+def partials(coef, times, lines, fields, bases=(), final=True):
     shape = (len(times),) + fields[0][2].shape[1:]
-    outs = [shaped(shape, F32)] + [shaped(shape, jnp.int16)] * (lines - 1)
-    return pl.pallas_call(
-        functools.partial(partial_kernel, times, lines, [field[:2] for field in fields]),
+    outs = [shaped(shape, F32)] + [shaped(shape, jnp.int16 if final else F32)] * (lines - 1)
+    return pl.pallas_call(
+        functools.partial(
+            partial_kernel, times, lines, [field[:2] for field in fields], len(bases), final
+        ),
         out_shape=tuple(outs),
-        in_specs=[VM] * (1 + len(fields)),
+        in_specs=[VM] * (1 + len(bases) + len(fields)),
         out_specs=(VM,) * len(outs),
         compiler_params=params(),
         name="partials",
-    )(coef, *[field[2] for field in fields])
+    )(coef, *bases, *[field[2] for field in fields])
 
 
 def drive_kernel(own_ref, *refs):
@@ -445,8 +467,12 @@
     selects = (select_own, select_other)
     known = [(0, -2 * WIN, history), (1, -2 * WIN, facing)]
 
-    def send(times):
-        sums = partials(coef, times, lines, known)
+    def send(times, ready, late):
+        if late:
+            bases = partials(coef, times, lines, ready, final=False)
+            sums = partials(coef, times, lines, late, bases)
+        else:
+            sums = partials(coef, times, lines, ready)
         arrived = []
         for line in range(1, lines):
             arrived.append(crossed(sums[line], "area", 2 * line))
@@ -462,7 +488,7 @@
 
     half = pick_half([rates], select_own)
     fresh = pick([other], half, select_other)
-    sent = send((0, 1))
+    sent = send((0, 1), known, None)
     known += share(fresh, 0)
     rec_other, external, state, leak_row, total = opening(
         unit, rates, other, rec_own, w_rec, external, state_start, leak_row
@@ -479,15 +505,20 @@
                 fresh = pick(others, half, select_other)
                 old.append(fresh)
                 pairs = []
-                known += share(fresh, 1)
+                here, there = share(fresh, 1)
             total = own_part(rates, rec_own, external)
         if time == STEPS - 1:
             return last_step(total, state, leak_row, flow, kept, selects, old, pairs)
-        drives = drive_pair(sent) if time % 2 == 0 else None
-        if time in (0, 2):
-            sent = send((time + 2, time + 3))
-        state, rates, *more = step(total, state, leak_row, flow, drives, kept)
-        kept = more[0] if more else None
+        drives, row = drive_pair(sent) if time % 2 == 0 else None, 0
+        if time == 2:
+            kept, drives = full_current(*drives), None
+            sent = send((4, 5), known + [here], [there])
+        if time == 3:
+            row = 1
+        if time == 0:
+            sent = send((2, 3), known, None)
+        state, rates, *more = step(total, state, leak_row, flow, drives, kept, row)
+        kept = more[0] if more else kept
 
 
 def wide_body(state_start, history, external, leak, w_rec, w_in, sources, delays, gains, proj_units):

time: 82.2 us -> 82.9 us (level)
    pallas_call x1 -> x2, Pallas kernels: 2.86 us -> 3.34 us  [the longest x1 2.88 us: last_step(): pl.pallas_call(functools.partial(step_kernel, True, False, 0, True), out_...]
    pallas_call x3 -> x4, Pallas kernels: 1.57 us -> 1.73 us  [partials(): pl.pallas_call(functools.partial(partial_kernel, times, lines, [field[:2]...]
  transfers between devices with their start and end apart: 21 -> 21, of which waited for: 9 -> 10; matrix products, arithmetic and copies ran while one was open for 1% -> 1% of each run, Pallas kernels for 30% -> 30%
where the time goes in v3:
time: 82.9 us; the launch traced here: 82.7 us
  Pallas kernels  33.7 us (41%)
  waiting for transfers between devices  26.9 us (32%)
  starting transfers between devices  19.9 us (24%)
  other arithmetic  1.12 us (1%)
  between operations  1.08 us (1%)
    ppermute x21, waiting for transfers between devices, crossed(): return lax.ppermute(value, axis, pairs)  26.9 us
    ppermute x21, starting transfers between devices, crossed(): return lax.ppermute(value, axis, pairs)  19.9 us
    pallas_call x5, Pallas kernels, own_part(): pl.pallas_call(own_kernel, out_shape=shaped(extra.shape, F32), in_specs=[...  8 us
    pallas_call x5, Pallas kernels, step(): pl.pallas_call(functools.partial(step_kernel, flow is not None, drives is...  7.46 us
    pallas_call x1, Pallas kernels, stage(): pl.pallas_call(functools.partial(stage_kernel, lines), out_shape=(pltpu.V...  5.25 us
    pallas_call x1, Pallas kernels, opening(): pl.pallas_call(opening_kernel, out_shape=(pltpu.VMEM(own.shape, BF16), pl...  4.43 us
    pallas_call x1, Pallas kernels, last_step(): pl.pallas_call(functools.partial(step_kernel, True, False, 0, True), out_...  2.88 us
    pallas_call x4, Pallas kernels, partials(): pl.pallas_call(functools.partial(partial_kernel, times, lines, [field[:2]...  1.73 us
  transfers between devices with their start and end apart: 21, of which 10 were waited for; matrix products, arithmetic and copies ran while one was open for 1% of the time, Pallas kernels for 30%

profile of v3, /device:TPU:0, one launch (start us, length us, event | category | flops | bytes accessed | tf_op | source)
XLA Modules:
  0.0 82.7 jit_solution(13317647241547039189)
XLA Ops:
  0.6 3.0 %collective-permute-start.1 = (bf16[6,64,384]{2,1,0:T(8,128)(2,1)}, bf16[6,64,384]{2,1,0:T(8,128)(2,1)S(1)}, u32[]{:S(2)}, u32[]{:S(2)}) collective-permute-start(bf16[6,64,384]{2,1,0:T(8,128)(2,1)} %history_far.1), channel_id=1, source_target_pairs={{0,2},{2,0},{4,6},{6,4},{8,10},{10,8},{12,14},{14,12},{1,3},{3,1},... | collective-permute-start | bytes 884744 | tf_op jit(solution)/shard_map/ppermute | solution.py:31
  3.7 1.1 %tanh_convert_fusion.rates_ref.refs_0_ = bf16[64,2048]{1,0:T(8,128)(2,1)S(1)} fusion(f32[64,2048]{1,0:T(8,128)} %state_far.1), kind=kLoop, calls=%fused_computation | loop fusion | flops 131072 | bytes 786432 | tf_op jit(solution)/shard_map/convert_element_type | solution.py:462
  4.9 5.3 %stage.1 = (bf16[6,64,384]{2,1,0:T(8,128)(2,1)S(1)}, bf16[2048,2048]{1,0:T(8,128)(2,1)S(1)}, bf16[384,2048]{1,0:T(8,128)(2,1)S(1)}, bf16[384,2048]{1,0:T(8,128)(...) custom-call(s32[1]{0:T(128)} %bitcast.1.area_ref, s32[1]{0:T(128)} %bitcast.unit_ref, ...), custom_call_target="tpu_custom_call" | custom-call | tf_op jit(solution)/shard_map/stage/pallas_call | solution.py:127
  10.1 0.8 collective-permute-done.1.refs_1_
  10.9 0.6 partials.4
  11.5 1.9 %collective-permute-start.2 = (s16[2,64,384]{2,1,0:T(8,128)(2,1)S(1)}, s16[2,64,384]{2,1,0:T(8,128)(2,1)S(1)}, u32[]{:S(2)}, u32[]{:S(2)}) collective-permute-start(s16[2,64,384]{2,1,0:T(8,128)(2,1)S(1)} %get-tuple-element.49), channel_id=1, source_target_pairs={{0,4},{2,6},{4,0},{6,2},{8,12},{10,14},{12,8},{14,10},{1,5},{3,7},... | collective-permute-start | bytes 294920 | tf_op jit(solution)/shard_map/ppermute | solution.py:31
  13.4 2.6 %collective-permute-start.3 = (s16[2,64,384]{2,1,0:T(8,128)(2,1)S(1)}, s16[2,64,384]{2,1,0:T(8,128)(2,1)S(1)}, u32[]{:S(2)}, u32[]{:S(2)}) collective-permute-start(s16[2,64,384]{2,1,0:T(8,128)(2,1)S(1)} %get-tuple-element.50), channel_id=1, source_target_pairs={{0,8},{2,10},{4,12},{6,14},{8,0},{10,2},{12,4},{14,6},{1,9},{3,11}... | collective-permute-start | bytes 294920 | tf_op jit(solution)/shard_map/ppermute | solution.py:31
  16.0 0.2 collective-permute-done.2.refs_0_
  16.2 7.3 %collective-permute-done.3.refs_1_ = s16[2,64,384]{2,1,0:T(8,128)(2,1)S(1)} collective-permute-done((s16[2,64,384]{2,1,0:T(8,128)(2,1)S(1)}, s16[2,64,384]{2,1,0:T(8,128)(2,1)S(1)}, u32[]{:S(2)}, u32[]{:S(2)}) %collective-permute-start.3) | collective-permute-done | bytes 98336 | tf_op jit(solution)/shard_map/ppermute | solution.py:31
  23.6 4.4 %opening.1 = (bf16[2048,2048]{1,0:T(8,128)(2,1)S(1)}, f32[64,2048]{1,0:T(8,128)S(1)}, f32[64,2048]{1,0:T(8,128)S(1)}, f32[1,2048]{1,0:T(1,128)S(1)}, f32[64,2048]{1,0:T(8,128)S(1)}) custom-call(s32[1]{0:T(128)} %bitcast.unit_ref, bf16[64,2048]{1,0:T(8,128)(2,1)S(1)} %tanh_convert_fusion.rates_ref.refs_0_, ...), custom_call_target="tpu_custom_call" | custom-call | tf_op jit(solution)/shard_map/opening/pallas_call | solution.py:188
  28.1 0.5 half.3.refs_0_
  28.6 0.5 step.5
  29.0 0.6 collective-permute-start.6
  29.6 1.6 %own_part.5.sum_ref = f32[64,2048]{1,0:T(8,128)S(1)} custom-call(bf16[64,2048]{1,0:T(8,128)(2,1)S(1)} %get-tuple-element.54.rates_ref.refs_0_, bf16[2048,2048]{1,0:T(8,128)(2,1)S(1)} %get-tuple-element.42.own_ref.weight_ref, f32[64,2048]{1,0:T(8,128)S(1)} %get-tuple-element.55.extra_ref), custom_call_target="tpu_custom_call" | custom-call | tf_op jit(solution)/shard_map/own_part/pallas_call | solution.py:280
  31.2 1.7 %step.6 = (f32[64,2048]{1,0:T(8,128)S(1)}, bf16[64,2048]{1,0:T(8,128)(2,1)S(1)}) custom-call(f32[64,2048]{1,0:T(8,128)S(1)} %own_part.5.sum_ref, f32[64,2048]{1,0:T(8,128)S(1)} %get-tuple-element.56.state_ref, f32[1,2048]{1,0:T(1,128)S(1)} %get-tuple-element.45.leak_ref, bf16[64,2048]{1,0:T(8,128)(2,1)S(1)} %collective-permute-done.6.refs_0_, ...), custom_call_target="tpu_custom_call" | custom-call | tf_op jit(solution)/shard_map/step/pallas_call | solution.py:351
  32.9 0.4 pick_half.2.refs_1_
  33.3 0.4 pick.2.refs_2_.refs_5_
  33.7 1.0 %collective-permute-start.8 = (bf16[1,64,384]{2,1,0:T(8,128)(2,1)S(1)}, bf16[1,64,384]{2,1,0:T(8,128)(2,1)S(1)}, u32[]{:S(2)}, u32[]{:S(2)}) collective-permute-start(bf16[1,64,384]{2,1,0:T(8,128)(2,1)S(1)} %pick.2.refs_2_.refs_5_), channel_id=1, source_target_pairs={{0,2},{2,0},{4,6},{6,4},{8,10},{10,8},{12,14},{14,12},{1,3},{3,1},... | collective-permute-start | bytes 147464 | tf_op jit(solution)/shard_map/ppermute | solution.py:31
  34.7 3.2 %collective-permute-done.8.refs_3_ = bf16[1,64,384]{2,1,0:T(8,128)(2,1)S(1)} collective-permute-done((bf16[1,64,384]{2,1,0:T(8,128)(2,1)S(1)}, bf16[1,64,384]{2,1,0:T(8,128)(2,1)S(1)}, u32[]{:S(2)}, u32[]{:S(2)}) %collective-permute-start.8) | collective-permute-done | bytes 49184 | tf_op jit(solution)/shard_map/ppermute | solution.py:31
  37.9 0.6 partials.5
  38.5 2.7 %collective-permute-start.10 = (s16[2,64,384]{2,1,0:T(8,128)(2,1)S(1)}, s16[2,64,384]{2,1,0:T(8,128)(2,1)S(1)}, u32[]{:S(2)}, u32[]{:S(2)}) collective-permute-start(s16[2,64,384]{2,1,0:T(8,128)(2,1)S(1)} %get-tuple-element.65), channel_id=1, source_target_pairs={{0,8},{2,10},{4,12},{6,14},{8,0},{10,2},{12,4},{14,6},{1,9},{3,11}... | collective-permute-start | bytes 294920 | tf_op jit(solution)/shard_map/ppermute | solution.py:31
  41.2 1.3 %collective-permute-start.11 = (s16[2,64,384]{2,1,0:T(8,128)(2,1)S(1)}, s16[2,64,384]{2,1,0:T(8,128)(2,1)S(1)}, u32[]{:S(2)}, u32[]{:S(2)}) collective-permute-start(s16[2,64,384]{2,1,0:T(8,128)(2,1)S(1)} %get-tuple-element.66), channel_id=1, source_target_pairs={{0,12},{2,14},{4,8},{6,10},{8,4},{10,6},{12,0},{14,2},{1,13},{3,15... | collective-permute-start | bytes 294920 | tf_op jit(solution)/shard_map/ppermute | solution.py:31
  42.5 6.5 %collective-permute-done.10.refs_1_ = s16[2,64,384]{2,1,0:T(8,128)(2,1)S(1)} collective-permute-done((s16[2,64,384]{2,1,0:T(8,128)(2,1)S(1)}, s16[2,64,384]{2,1,0:T(8,128)(2,1)S(1)}, u32[]{:S(2)}, u32[]{:S(2)}) %collective-permute-start.10) | collective-permute-done | bytes 98336 | tf_op jit(solution)/shard_map/ppermute | solution.py:31
  49.1 0.3 collective-permute-done.9.refs_0_
  49.5 0.5 half.4.half_ref
  49.9 0.8 collective-permute-done.12.drive_ref
  50.8 0.5 full.1.refs_2_
  51.3 1.6 %own_part.6.sum_ref = f32[64,2048]{1,0:T(8,128)S(1)} custom-call(bf16[64,2048]{1,0:T(8,128)(2,1)S(1)} %get-tuple-element.59.rates_ref.refs_1_, bf16[2048,2048]{1,0:T(8,128)(2,1)S(1)} %get-tuple-element.42.own_ref.weight_ref, f32[64,2048]{1,0:T(8,128)S(1)} %get-tuple-element.55.extra_ref), custom_call_target="tpu_custom_call" | custom-call | tf_op jit(solution)/shard_map/own_part/pallas_call | solution.py:280
  52.9 1.7 %step.7 = (f32[64,2048]{1,0:T(8,128)S(1)}, bf16[64,2048]{1,0:T(8,128)(2,1)S(1)}) custom-call(f32[64,2048]{1,0:T(8,128)S(1)} %own_part.6.sum_ref, f32[64,2048]{1,0:T(8,128)S(1)} %get-tuple-element.60.state_ref, f32[1,2048]{1,0:T(1,128)S(1)} %get-tuple-element.45.leak_ref, bf16[64,2048]{1,0:T(8,128)(2,1)S(1)} %collective-permute-done.7.refs_0_.refs_1_, ...), custom_call_target="tpu_custom_call" | custom-call | tf_op jit(solution)/shard_map/step/pallas_call | solution.py:351
  54.5 0.2 collective-permute-start.13
  54.7 0.6 pick_half.3.refs_2_
  55.4 0.4 pick.3.refs_4_.refs_6_
  55.8 1.0 %collective-permute-start.15 = (bf16[2,64,384]{2,1,0:T(8,128)(2,1)S(1)}, bf16[2,64,384]{2,1,0:T(8,128)(2,1)S(1)}, u32[]{:S(2)}, u32[]{:S(2)}) collective-permute-start(bf16[2,64,384]{2,1,0:T(8,128)(2,1)S(1)} %pick.3.refs_4_.refs_6_), channel_id=1, source_target_pairs={{0,2},{2,0},{4,6},{6,4},{8,10},{10,8},{12,14},{14,12},{1,3},{3,1},... | collective-permute-start | bytes 294920 | tf_op jit(solution)/shard_map/ppermute | solution.py:31
  56.9 1.6 %own_part.7.sum_ref = f32[64,2048]{1,0:T(8,128)S(1)} custom-call(bf16[64,2048]{1,0:T(8,128)(2,1)S(1)} %get-tuple-element.67.rates_ref.refs_7_, bf16[2048,2048]{1,0:T(8,128)(2,1)S(1)} %get-tuple-element.42.own_ref.weight_ref, f32[64,2048]{1,0:T(8,128)S(1)} %get-tuple-element.55.extra_ref), custom_call_target="tpu_custom_call" | custom-call | tf_op jit(solution)/shard_map/own_part/pallas_call | solution.py:280
  58.5 1.7 %step.8 = (f32[64,2048]{1,0:T(8,128)S(1)}, bf16[64,2048]{1,0:T(8,128)(2,1)S(1)}) custom-call(f32[64,2048]{1,0:T(8,128)S(1)} %own_part.7.sum_ref, f32[64,2048]{1,0:T(8,128)S(1)} %get-tuple-element.68.state_ref, f32[1,2048]{1,0:T(1,128)S(1)} %get-tuple-element.45.leak_ref, bf16[64,2048]{1,0:T(8,128)(2,1)S(1)} %collective-permute-done.13.refs_0_.refs_10_, ...), custom_call_target="tpu_custom_call" | custom-call | tf_op jit(solution)/shard_map/step/pallas_call | solution.py:351
  60.3 0.4 partials.6
  60.7 0.3 collective-permute-done.15.refs_4_
  61.1 1.4 %collective-permute-start.16 = (s16[2,64,384]{2,1,0:T(8,128)(2,1)S(1)}, s16[2,64,384]{2,1,0:T(8,128)(2,1)S(1)}, u32[]{:S(2)}, u32[]{:S(2)}) collective-permute-start(s16[2,64,384]{2,1,0:T(8,128)(2,1)S(1)} %get-tuple-element.76), channel_id=1, source_target_pairs={{0,4},{2,6},{4,0},{6,2},{8,12},{10,14},{12,8},{14,10},{1,5},{3,7},... | collective-permute-start | bytes 294920 | tf_op jit(solution)/shard_map/ppermute | solution.py:31
  62.5 1.5 %collective-permute-start.17 = (s16[2,64,384]{2,1,0:T(8,128)(2,1)S(1)}, s16[2,64,384]{2,1,0:T(8,128)(2,1)S(1)}, u32[]{:S(2)}, u32[]{:S(2)}) collective-permute-start(s16[2,64,384]{2,1,0:T(8,128)(2,1)S(1)} %get-tuple-element.77), channel_id=1, source_target_pairs={{0,8},{2,10},{4,12},{6,14},{8,0},{10,2},{12,4},{14,6},{1,9},{3,11}... | collective-permute-start | bytes 294920 | tf_op jit(solution)/shard_map/ppermute | solution.py:31
  64.0 1.5 %collective-permute-start.18 = (s16[2,64,384]{2,1,0:T(8,128)(2,1)S(1)}, s16[2,64,384]{2,1,0:T(8,128)(2,1)S(1)}, u32[]{:S(2)}, u32[]{:S(2)}) collective-permute-start(s16[2,64,384]{2,1,0:T(8,128)(2,1)S(1)} %get-tuple-element.78), channel_id=1, source_target_pairs={{0,12},{2,14},{4,8},{6,10},{8,4},{10,6},{12,0},{14,2},{1,13},{3,15... | collective-permute-start | bytes 294920 | tf_op jit(solution)/shard_map/ppermute | solution.py:31
  65.6 1.7 %collective-permute-done.16.refs_0_ = s16[2,64,384]{2,1,0:T(8,128)(2,1)S(1)} collective-permute-done((s16[2,64,384]{2,1,0:T(8,128)(2,1)S(1)}, s16[2,64,384]{2,1,0:T(8,128)(2,1)S(1)}, u32[]{:S(2)}, u32[]{:S(2)}) %collective-permute-start.16) | collective-permute-done | bytes 98336 | tf_op jit(solution)/shard_map/ppermute | solution.py:31
  67.2 6.0 %collective-permute-done.17.refs_1_ = s16[2,64,384]{2,1,0:T(8,128)(2,1)S(1)} collective-permute-done((s16[2,64,384]{2,1,0:T(8,128)(2,1)S(1)}, s16[2,64,384]{2,1,0:T(8,128)(2,1)S(1)}, u32[]{:S(2)}, u32[]{:S(2)}) %collective-permute-start.17) | collective-permute-done | bytes 98336 | tf_op jit(solution)/shard_map/ppermute | solution.py:31
  73.4 0.5 half.5.refs_2_
  73.8 1.6 %own_part.8.sum_ref = f32[64,2048]{1,0:T(8,128)S(1)} custom-call(bf16[64,2048]{1,0:T(8,128)(2,1)S(1)} %get-tuple-element.69.rates_ref.refs_8_, bf16[2048,2048]{1,0:T(8,128)(2,1)S(1)} %get-tuple-element.42.own_ref.weight_ref, f32[64,2048]{1,0:T(8,128)S(1)} %get-tuple-element.55.extra_ref), custom_call_target="tpu_custom_call" | custom-call | tf_op jit(solution)/shard_map/own_part/pallas_call | solution.py:280
  75.5 2.0 %step.9 = (f32[64,2048]{1,0:T(8,128)S(1)}, bf16[64,2048]{1,0:T(8,128)(2,1)S(1)}, f32[64,2048]{1,0:T(8,128)S(1)}) custom-call(f32[64,2048]{1,0:T(8,128)S(1)} %own_part.8.sum_ref, f32[64,2048]{1,0:T(8,128)S(1)} %get-tuple-element.70.state_ref, f32[1,2048]{1,0:T(1,128)S(1)} %get-tuple-element.45.leak_ref, ...), custom_call_target="tpu_custom_call" | custom-call | tf_op jit(solution)/shard_map/step/pallas_call | solution.py:351
  77.5 0.5 collective-permute-start.20
  78.1 1.6 %own_part.9.sum_ref = f32[64,2048]{1,0:T(8,128)S(1)} custom-call(bf16[64,2048]{1,0:T(8,128)(2,1)S(1)} %get-tuple-element.79.rates_ref.refs_9_, bf16[2048,2048]{1,0:T(8,128)(2,1)S(1)} %get-tuple-element.42.own_ref.weight_ref, f32[64,2048]{1,0:T(8,128)S(1)} %get-tuple-element.55.extra_ref), custom_call_target="tpu_custom_call" | custom-call | tf_op jit(solution)/shard_map/own_part/pallas_call | solution.py:280
  79.7 2.9 %last_step.1 = (f32[64,2048]{1,0:T(8,128)}, bf16[6,64,384]{2,1,0:T(8,128)(2,1)}) custom-call(f32[64,2048]{1,0:T(8,128)S(1)} %own_part.9.sum_ref, f32[64,2048]{1,0:T(8,128)S(1)} %get-tuple-element.80.state_ref, f32[1,2048]{1,0:T(1,128)S(1)} %get-tuple-element.45.leak_ref, bf16[64,2048]{1,0:T(8,128)(2,1)S(1)} %collective-permute-done.20.refs_0_.refs_12_, ...), custom_call_target="tpu_custom_call" | custom-call | tf_op jit(solution)/shard_map/last_step/pallas_call | solution.py:366
  (23 shorter events, 1.0 us)
Async XLA Ops:
  0.6 10.3 %collective-permute-start.1 = (bf16[6,64,384]{2,1,0:T(8,128)(2,1)}, bf16[6,64,384]{2,1,0:T(8,128)(2,1)S(1)}, u32[]{:S(2)}, u32[]{:S(2)}) collective-permute-start(bf16[6,64,384]{2,1,0:T(8,128)(2,1)} %history_far.1), channel_id=1, source_target_pairs={{0,2},{2,0},{4,6},{6,4},{8,10},{10,8},{12,14},{14,12},{1,3},{3,1},... | collective-permute-start | bytes 884744 | tf_op jit(solution)/shard_map/ppermute | solution.py:31
  4.8 18.8 %collective-permute-start = (bf16[64,2048]{1,0:T(8,128)(2,1)S(1)}, bf16[64,2048]{1,0:T(8,128)(2,1)S(1)}, u32[]{:S(2)}, u32[]{:S(2)}) collective-permute-start(bf16[64,2048]{1,0:T(8,128)(2,1)S(1)} %tanh_convert_fusion.rates_ref.refs_0_), channel_id=1, source_target_pairs={{0,1},{1,0},{2,3},{3,2},{4,5},{5,4},{6,7},{7,6},{8,9},{9,8},{10,11... | collective-permute-start | bytes 786440 | tf_op jit(solution)/shard_map/ppermute | solution.py:31
  11.5 4.7 %collective-permute-start.2 = (s16[2,64,384]{2,1,0:T(8,128)(2,1)S(1)}, s16[2,64,384]{2,1,0:T(8,128)(2,1)S(1)}, u32[]{:S(2)}, u32[]{:S(2)}) collective-permute-start(s16[2,64,384]{2,1,0:T(8,128)(2,1)S(1)} %get-tuple-element.49), channel_id=1, source_target_pairs={{0,4},{2,6},{4,0},{6,2},{8,12},{10,14},{12,8},{14,10},{1,5},{3,7},... | collective-permute-start | bytes 294920 | tf_op jit(solution)/shard_map/ppermute | solution.py:31
  13.4 10.1 %collective-permute-start.3 = (s16[2,64,384]{2,1,0:T(8,128)(2,1)S(1)}, s16[2,64,384]{2,1,0:T(8,128)(2,1)S(1)}, u32[]{:S(2)}, u32[]{:S(2)}) collective-permute-start(s16[2,64,384]{2,1,0:T(8,128)(2,1)S(1)} %get-tuple-element.50), channel_id=1, source_target_pairs={{0,8},{2,10},{4,12},{6,14},{8,0},{10,2},{12,4},{14,6},{1,9},{3,11}... | collective-permute-start | bytes 294920 | tf_op jit(solution)/shard_map/ppermute | solution.py:31
  16.0 7.5 %collective-permute-start.4 = (s16[2,64,384]{2,1,0:T(8,128)(2,1)S(1)}, s16[2,64,384]{2,1,0:T(8,128)(2,1)S(1)}, u32[]{:S(2)}, u32[]{:S(2)}) collective-permute-start(s16[2,64,384]{2,1,0:T(8,128)(2,1)S(1)} %get-tuple-element.51), channel_id=1, source_target_pairs={{0,12},{2,14},{4,8},{6,10},{8,4},{10,6},{12,0},{14,2},{1,13},{3,15... | collective-permute-start | bytes 294920 | tf_op jit(solution)/shard_map/ppermute | solution.py:31
  23.5 5.0 %collective-permute-start.5 = (bf16[128,384]{1,0:T(8,128)(2,1)S(1)}, bf16[128,384]{1,0:T(8,128)(2,1)S(1)}, u32[]{:S(2)}, u32[]{:S(2)}) collective-permute-start(bf16[128,384]{1,0:T(8,128)(2,1)S(1)} %drive.3.drive_ref), channel_id=1, source_target_pairs={{0,1},{1,0},{2,3},{3,2},{4,5},{5,4},{6,7},{7,6},{8,9},{9,8},{10,11... | collective-permute-start | bytes 294920 | tf_op jit(solution)/shard_map/ppermute | solution.py:31
  29.0 2.2 %collective-permute-start.6 = (bf16[64,2048]{1,0:T(8,128)(2,1)S(1)}, bf16[64,2048]{1,0:T(8,128)(2,1)S(1)}, u32[]{:S(2)}, u32[]{:S(2)}) collective-permute-start(bf16[64,2048]{1,0:T(8,128)(2,1)S(1)} %get-tuple-element.54.rates_ref.refs_0_), channel_id=1, source_target_pairs={{0,1},{1,0},{2,3},{3,2},{4,5},{5,4},{6,7},{7,6},{8,9},{9,8},{10,11... | collective-permute-start | bytes 786440 | tf_op jit(solution)/shard_map/ppermute | solution.py:31
  32.8 20.0 %collective-permute-start.7 = (bf16[64,2048]{1,0:T(8,128)(2,1)S(1)}, bf16[64,2048]{1,0:T(8,128)(2,1)S(1)}, u32[]{:S(2)}, u32[]{:S(2)}) collective-permute-start(bf16[64,2048]{1,0:T(8,128)(2,1)S(1)} %get-tuple-element.59.rates_ref.refs_1_), channel_id=1, source_target_pairs={{0,1},{1,0},{2,3},{3,2},{4,5},{5,4},{6,7},{7,6},{8,9},{9,8},{10,11... | collective-permute-start | bytes 786440 | tf_op jit(solution)/shard_map/ppermute | solution.py:31
  33.7 4.2 %collective-permute-start.8 = (bf16[1,64,384]{2,1,0:T(8,128)(2,1)S(1)}, bf16[1,64,384]{2,1,0:T(8,128)(2,1)S(1)}, u32[]{:S(2)}, u32[]{:S(2)}) collective-permute-start(bf16[1,64,384]{2,1,0:T(8,128)(2,1)S(1)} %pick.2.refs_2_.refs_5_), channel_id=1, source_target_pairs={{0,2},{2,0},{4,6},{6,4},{8,10},{10,8},{12,14},{14,12},{1,3},{3,1},... | collective-permute-start | bytes 147464 | tf_op jit(solution)/shard_map/ppermute | solution.py:31
  38.5 10.6 %collective-permute-start.10 = (s16[2,64,384]{2,1,0:T(8,128)(2,1)S(1)}, s16[2,64,384]{2,1,0:T(8,128)(2,1)S(1)}, u32[]{:S(2)}, u32[]{:S(2)}) collective-permute-start(s16[2,64,384]{2,1,0:T(8,128)(2,1)S(1)} %get-tuple-element.65), channel_id=1, source_target_pairs={{0,8},{2,10},{4,12},{6,14},{8,0},{10,2},{12,4},{14,6},{1,9},{3,11}... | collective-permute-start | bytes 294920 | tf_op jit(solution)/shard_map/ppermute | solution.py:31
  41.2 7.9 %collective-permute-start.11 = (s16[2,64,384]{2,1,0:T(8,128)(2,1)S(1)}, s16[2,64,384]{2,1,0:T(8,128)(2,1)S(1)}, u32[]{:S(2)}, u32[]{:S(2)}) collective-permute-start(s16[2,64,384]{2,1,0:T(8,128)(2,1)S(1)} %get-tuple-element.66), channel_id=1, source_target_pairs={{0,12},{2,14},{4,8},{6,10},{8,4},{10,6},{12,0},{14,2},{1,13},{3,15... | collective-permute-start | bytes 294920 | tf_op jit(solution)/shard_map/ppermute | solution.py:31
  42.5 6.8 %collective-permute-start.9 = (s16[2,64,384]{2,1,0:T(8,128)(2,1)S(1)}, s16[2,64,384]{2,1,0:T(8,128)(2,1)S(1)}, u32[]{:S(2)}, u32[]{:S(2)}) collective-permute-start(s16[2,64,384]{2,1,0:T(8,128)(2,1)S(1)} %get-tuple-element.64), channel_id=1, source_target_pairs={{0,4},{2,6},{4,0},{6,2},{8,12},{10,14},{12,8},{14,10},{1,5},{3,7},... | collective-permute-start | bytes 294920 | tf_op jit(solution)/shard_map/ppermute | solution.py:31
  49.4 1.4 %collective-permute-start.12 = (bf16[128,384]{1,0:T(8,128)(2,1)S(1)}, bf16[128,384]{1,0:T(8,128)(2,1)S(1)}, u32[]{:S(2)}, u32[]{:S(2)}) collective-permute-start(bf16[128,384]{1,0:T(8,128)(2,1)S(1)} %drive.4.drive_ref), channel_id=1, source_target_pairs={{0,1},{1,0},{2,3},{3,2},{4,5},{5,4},{6,7},{7,6},{8,9},{9,8},{10,11... | collective-permute-start | bytes 294920 | tf_op jit(solution)/shard_map/ppermute | solution.py:31
  54.5 3.9 %collective-permute-start.13 = (bf16[64,2048]{1,0:T(8,128)(2,1)S(1)}, bf16[64,2048]{1,0:T(8,128)(2,1)S(1)}, u32[]{:S(2)}, u32[]{:S(2)}) collective-permute-start(bf16[64,2048]{1,0:T(8,128)(2,1)S(1)} %get-tuple-element.67.rates_ref.refs_7_), channel_id=1, source_target_pairs={{0,1},{1,0},{2,3},{3,2},{4,5},{5,4},{6,7},{7,6},{8,9},{9,8},{10,11... | collective-permute-start | bytes 786440 | tf_op jit(solution)/shard_map/ppermute | solution.py:31
  55.8 5.1 %collective-permute-start.15 = (bf16[2,64,384]{2,1,0:T(8,128)(2,1)S(1)}, bf16[2,64,384]{2,1,0:T(8,128)(2,1)S(1)}, u32[]{:S(2)}, u32[]{:S(2)}) collective-permute-start(bf16[2,64,384]{2,1,0:T(8,128)(2,1)S(1)} %pick.3.refs_4_.refs_6_), channel_id=1, source_target_pairs={{0,2},{2,0},{4,6},{6,4},{8,10},{10,8},{12,14},{14,12},{1,3},{3,1},... | collective-permute-start | bytes 294920 | tf_op jit(solution)/shard_map/ppermute | solution.py:31
  60.1 15.3 %collective-permute-start.14 = (bf16[64,2048]{1,0:T(8,128)(2,1)S(1)}, bf16[64,2048]{1,0:T(8,128)(2,1)S(1)}, u32[]{:S(2)}, u32[]{:S(2)}) collective-permute-start(bf16[64,2048]{1,0:T(8,128)(2,1)S(1)} %get-tuple-element.69.rates_ref.refs_8_), channel_id=1, source_target_pairs={{0,1},{1,0},{2,3},{3,2},{4,5},{5,4},{6,7},{7,6},{8,9},{9,8},{10,11... | collective-permute-start | bytes 786440 | tf_op jit(solution)/shard_map/ppermute | solution.py:31
  61.1 6.1 %collective-permute-start.16 = (s16[2,64,384]{2,1,0:T(8,128)(2,1)S(1)}, s16[2,64,384]{2,1,0:T(8,128)(2,1)S(1)}, u32[]{:S(2)}, u32[]{:S(2)}) collective-permute-start(s16[2,64,384]{2,1,0:T(8,128)(2,1)S(1)} %get-tuple-element.76), channel_id=1, source_target_pairs={{0,4},{2,6},{4,0},{6,2},{8,12},{10,14},{12,8},{14,10},{1,5},{3,7},... | collective-permute-start | bytes 294920 | tf_op jit(solution)/shard_map/ppermute | solution.py:31
  62.5 10.7 %collective-permute-start.17 = (s16[2,64,384]{2,1,0:T(8,128)(2,1)S(1)}, s16[2,64,384]{2,1,0:T(8,128)(2,1)S(1)}, u32[]{:S(2)}, u32[]{:S(2)}) collective-permute-start(s16[2,64,384]{2,1,0:T(8,128)(2,1)S(1)} %get-tuple-element.77), channel_id=1, source_target_pairs={{0,8},{2,10},{4,12},{6,14},{8,0},{10,2},{12,4},{14,6},{1,9},{3,11}... | collective-permute-start | bytes 294920 | tf_op jit(solution)/shard_map/ppermute | solution.py:31
  64.0 9.2 %collective-permute-start.18 = (s16[2,64,384]{2,1,0:T(8,128)(2,1)S(1)}, s16[2,64,384]{2,1,0:T(8,128)(2,1)S(1)}, u32[]{:S(2)}, u32[]{:S(2)}) collective-permute-start(s16[2,64,384]{2,1,0:T(8,128)(2,1)S(1)} %get-tuple-element.78), channel_id=1, source_target_pairs={{0,12},{2,14},{4,8},{6,10},{8,4},{10,6},{12,0},{14,2},{1,13},{3,15... | collective-permute-start | bytes 294920 | tf_op jit(solution)/shard_map/ppermute | solution.py:31
  73.3 2.1 %collective-permute-start.19 = (bf16[128,384]{1,0:T(8,128)(2,1)S(1)}, bf16[128,384]{1,0:T(8,128)(2,1)S(1)}, u32[]{:S(2)}, u32[]{:S(2)}) collective-permute-start(bf16[128,384]{1,0:T(8,128)(2,1)S(1)} %drive.5.drive_ref), channel_id=1, source_target_pairs={{0,1},{1,0},{2,3},{3,2},{4,5},{5,4},{6,7},{7,6},{8,9},{9,8},{10,11... | collective-permute-start | bytes 294920 | tf_op jit(solution)/shard_map/ppermute | solution.py:31
  77.5 2.2 %collective-permute-start.20 = (bf16[64,2048]{1,0:T(8,128)(2,1)S(1)}, bf16[64,2048]{1,0:T(8,128)(2,1)S(1)}, u32[]{:S(2)}, u32[]{:S(2)}) collective-permute-start(bf16[64,2048]{1,0:T(8,128)(2,1)S(1)} %get-tuple-element.79.rates_ref.refs_9_), channel_id=1, source_target_pairs={{0,1},{1,0},{2,3},{3,2},{4,5},{5,4},{6,7},{7,6},{8,9},{9,8},{10,11... | collective-permute-start | bytes 786440 | tf_op jit(solution)/shard_map/ppermute | solution.py:31

commit v4 on v3

--- a/solution.py
+++ b/solution.py
@@ -308,10 +308,10 @@
 
     if last:
         sems, state_buf, fresh, new_ref, all_ref = (refs.pop(index) for index in (-1, -1, -1, -2, -1))
-        pick_own_ref, pick_other_ref, first_ref, second_ref = (refs.pop(0) for _ in range(4))
+        pick_own_ref, pick_other_ref, *olds = (refs.pop(0) for _ in range(5))
         count = len(refs) // 2
         old = 0
-        for ref in (first_ref, second_ref):
+        for ref in olds:
             send(ref, all_ref.at[pl.ds(old, ref.shape[0])])
             old += ref.shape[0]
         picked = matmul(stacked(refs[:count]), pick_own_ref[...])
@@ -517,6 +517,11 @@
             row = 1
         if time == 0:
             sent = send((2, 3), known, None)
+        if time == 4:
+            owns, others = zip(*pairs)
+            half = pick_half(owns, select_own)
+            old.append(pick(others, half, select_other))
+            pairs = []
         state, rates, *more = step(total, state, leak_row, flow, drives, kept, row)
         kept = more[0] if more else kept
 

time: 82.9 us -> 85.1 us (1.027)
  waiting for transfers between devices: 26.9 us -> 27.9 us
    ppermute x21, waiting for transfers between devices: 26.9 us -> 27.9 us  [crossed(): return lax.ppermute(value, axis, pairs)]
where the time goes in v4:
time: 85.1 us; the launch traced here: 84.9 us
  Pallas kernels  34.5 us (41%)
  waiting for transfers between devices  27.9 us (33%)
  starting transfers between devices  20.3 us (24%)
  other arithmetic  1.12 us (1%)
  between operations  1.09 us (1%)
    ppermute x21, waiting for transfers between devices, crossed(): return lax.ppermute(value, axis, pairs)  27.9 us
    ppermute x21, starting transfers between devices, crossed(): return lax.ppermute(value, axis, pairs)  20.3 us
    pallas_call x5, Pallas kernels, own_part(): pl.pallas_call(own_kernel, out_shape=shaped(extra.shape, F32), in_specs=[...  8 us
    pallas_call x5, Pallas kernels, step(): pl.pallas_call(functools.partial(step_kernel, flow is not None, drives is...  7.47 us
    pallas_call x1, Pallas kernels, stage(): pl.pallas_call(functools.partial(stage_kernel, lines), out_shape=(pltpu.V...  5.25 us
    pallas_call x1, Pallas kernels, opening(): pl.pallas_call(opening_kernel, out_shape=(pltpu.VMEM(own.shape, BF16), pl...  4.44 us
    pallas_call x1, Pallas kernels, last_step(): pl.pallas_call(functools.partial(step_kernel, True, False, 0, True), out_...  2.89 us
    pallas_call x4, Pallas kernels, partials(): pl.pallas_call(functools.partial(partial_kernel, times, lines, [field[:2]...  1.73 us
  transfers between devices with their start and end apart: 21, of which 10 were waited for; matrix products, arithmetic and copies ran while one was open for 1% of the time, Pallas kernels for 30%

profile of v4, /device:TPU:0, one launch (start us, length us, event | category | flops | bytes accessed | tf_op | source)
XLA Modules:
  0.0 84.9 jit_solution(3173119347346866207)
XLA Ops:
  0.6 3.0 %collective-permute-start.1 = (bf16[6,64,384]{2,1,0:T(8,128)(2,1)}, bf16[6,64,384]{2,1,0:T(8,128)(2,1)S(1)}, u32[]{:S(2)}, u32[]{:S(2)}) collective-permute-start(bf16[6,64,384]{2,1,0:T(8,128)(2,1)} %history_far.1), channel_id=1, source_target_pairs={{0,2},{2,0},{4,6},{6,4},{8,10},{10,8},{12,14},{14,12},{1,3},{3,1},... | collective-permute-start | bytes 884744 | tf_op jit(solution)/shard_map/ppermute | solution.py:31
  3.7 1.1 %tanh_convert_fusion.rates_ref.refs_0_ = bf16[64,2048]{1,0:T(8,128)(2,1)S(1)} fusion(f32[64,2048]{1,0:T(8,128)} %state_far.1), kind=kLoop, calls=%fused_computation | loop fusion | flops 131072 | bytes 786432 | tf_op jit(solution)/shard_map/convert_element_type | solution.py:462
  4.9 5.3 %stage.1 = (bf16[6,64,384]{2,1,0:T(8,128)(2,1)S(1)}, bf16[2048,2048]{1,0:T(8,128)(2,1)S(1)}, bf16[384,2048]{1,0:T(8,128)(2,1)S(1)}, bf16[384,2048]{1,0:T(8,128)(...) custom-call(s32[1]{0:T(128)} %bitcast.1.area_ref, s32[1]{0:T(128)} %bitcast.unit_ref, ...), custom_call_target="tpu_custom_call" | custom-call | tf_op jit(solution)/shard_map/stage/pallas_call | solution.py:127
  10.1 0.8 collective-permute-done.1.refs_1_
  10.9 0.6 partials.4
  11.5 1.9 %collective-permute-start.2 = (s16[2,64,384]{2,1,0:T(8,128)(2,1)S(1)}, s16[2,64,384]{2,1,0:T(8,128)(2,1)S(1)}, u32[]{:S(2)}, u32[]{:S(2)}) collective-permute-start(s16[2,64,384]{2,1,0:T(8,128)(2,1)S(1)} %get-tuple-element.49), channel_id=1, source_target_pairs={{0,4},{2,6},{4,0},{6,2},{8,12},{10,14},{12,8},{14,10},{1,5},{3,7},... | collective-permute-start | bytes 294920 | tf_op jit(solution)/shard_map/ppermute | solution.py:31
  13.4 2.6 %collective-permute-start.3 = (s16[2,64,384]{2,1,0:T(8,128)(2,1)S(1)}, s16[2,64,384]{2,1,0:T(8,128)(2,1)S(1)}, u32[]{:S(2)}, u32[]{:S(2)}) collective-permute-start(s16[2,64,384]{2,1,0:T(8,128)(2,1)S(1)} %get-tuple-element.50), channel_id=1, source_target_pairs={{0,8},{2,10},{4,12},{6,14},{8,0},{10,2},{12,4},{14,6},{1,9},{3,11}... | collective-permute-start | bytes 294920 | tf_op jit(solution)/shard_map/ppermute | solution.py:31
  16.2 7.3 %collective-permute-done.3.refs_1_ = s16[2,64,384]{2,1,0:T(8,128)(2,1)S(1)} collective-permute-done((s16[2,64,384]{2,1,0:T(8,128)(2,1)S(1)}, s16[2,64,384]{2,1,0:T(8,128)(2,1)S(1)}, u32[]{:S(2)}, u32[]{:S(2)}) %collective-permute-start.3) | collective-permute-done | bytes 98336 | tf_op jit(solution)/shard_map/ppermute | solution.py:31
  23.6 4.4 %opening.1 = (bf16[2048,2048]{1,0:T(8,128)(2,1)S(1)}, f32[64,2048]{1,0:T(8,128)S(1)}, f32[64,2048]{1,0:T(8,128)S(1)}, f32[1,2048]{1,0:T(1,128)S(1)}, f32[64,2048]{1,0:T(8,128)S(1)}) custom-call(s32[1]{0:T(128)} %bitcast.unit_ref, bf16[64,2048]{1,0:T(8,128)(2,1)S(1)} %tanh_convert_fusion.rates_ref.refs_0_, ...), custom_call_target="tpu_custom_call" | custom-call | tf_op jit(solution)/shard_map/opening/pallas_call | solution.py:188
  28.1 0.5 half.3.refs_0_
  28.5 0.5 step.5
  29.0 0.5 collective-permute-start.6
  29.5 1.6 %own_part.5.sum_ref = f32[64,2048]{1,0:T(8,128)S(1)} custom-call(bf16[64,2048]{1,0:T(8,128)(2,1)S(1)} %get-tuple-element.54.rates_ref.refs_0_, bf16[2048,2048]{1,0:T(8,128)(2,1)S(1)} %get-tuple-element.42.own_ref.weight_ref, f32[64,2048]{1,0:T(8,128)S(1)} %get-tuple-element.55.extra_ref), custom_call_target="tpu_custom_call" | custom-call | tf_op jit(solution)/shard_map/own_part/pallas_call | solution.py:280
  31.2 1.7 %step.6 = (f32[64,2048]{1,0:T(8,128)S(1)}, bf16[64,2048]{1,0:T(8,128)(2,1)S(1)}) custom-call(f32[64,2048]{1,0:T(8,128)S(1)} %own_part.5.sum_ref, f32[64,2048]{1,0:T(8,128)S(1)} %get-tuple-element.56.state_ref, f32[1,2048]{1,0:T(1,128)S(1)} %get-tuple-element.45.leak_ref, bf16[64,2048]{1,0:T(8,128)(2,1)S(1)} %collective-permute-done.6.refs_0_, ...), custom_call_target="tpu_custom_call" | custom-call | tf_op jit(solution)/shard_map/step/pallas_call | solution.py:351
  32.9 0.4 pick_half.3.refs_1_
  33.3 0.4 pick.3.refs_2_.refs_5_
  33.7 1.0 %collective-permute-start.8 = (bf16[1,64,384]{2,1,0:T(8,128)(2,1)S(1)}, bf16[1,64,384]{2,1,0:T(8,128)(2,1)S(1)}, u32[]{:S(2)}, u32[]{:S(2)}) collective-permute-start(bf16[1,64,384]{2,1,0:T(8,128)(2,1)S(1)} %pick.3.refs_2_.refs_5_), channel_id=1, source_target_pairs={{0,2},{2,0},{4,6},{6,4},{8,10},{10,8},{12,14},{14,12},{1,3},{3,1},... | collective-permute-start | bytes 147464 | tf_op jit(solution)/shard_map/ppermute | solution.py:31
  34.7 3.1 %collective-permute-done.8.refs_3_ = bf16[1,64,384]{2,1,0:T(8,128)(2,1)S(1)} collective-permute-done((bf16[1,64,384]{2,1,0:T(8,128)(2,1)S(1)}, bf16[1,64,384]{2,1,0:T(8,128)(2,1)S(1)}, u32[]{:S(2)}, u32[]{:S(2)}) %collective-permute-start.8) | collective-permute-done | bytes 49184 | tf_op jit(solution)/shard_map/ppermute | solution.py:31
  37.9 0.6 partials.5
  38.5 1.7 %collective-permute-start.9 = (s16[2,64,384]{2,1,0:T(8,128)(2,1)S(1)}, s16[2,64,384]{2,1,0:T(8,128)(2,1)S(1)}, u32[]{:S(2)}, u32[]{:S(2)}) collective-permute-start(s16[2,64,384]{2,1,0:T(8,128)(2,1)S(1)} %get-tuple-element.64), channel_id=1, source_target_pairs={{0,4},{2,6},{4,0},{6,2},{8,12},{10,14},{12,8},{14,10},{1,5},{3,7},... | collective-permute-start | bytes 294920 | tf_op jit(solution)/shard_map/ppermute | solution.py:31
  40.2 1.4 %collective-permute-start.10 = (s16[2,64,384]{2,1,0:T(8,128)(2,1)S(1)}, s16[2,64,384]{2,1,0:T(8,128)(2,1)S(1)}, u32[]{:S(2)}, u32[]{:S(2)}) collective-permute-start(s16[2,64,384]{2,1,0:T(8,128)(2,1)S(1)} %get-tuple-element.65), channel_id=1, source_target_pairs={{0,8},{2,10},{4,12},{6,14},{8,0},{10,2},{12,4},{14,6},{1,9},{3,11}... | collective-permute-start | bytes 294920 | tf_op jit(solution)/shard_map/ppermute | solution.py:31
  41.6 1.3 %collective-permute-start.11 = (s16[2,64,384]{2,1,0:T(8,128)(2,1)S(1)}, s16[2,64,384]{2,1,0:T(8,128)(2,1)S(1)}, u32[]{:S(2)}, u32[]{:S(2)}) collective-permute-start(s16[2,64,384]{2,1,0:T(8,128)(2,1)S(1)} %get-tuple-element.66), channel_id=1, source_target_pairs={{0,12},{2,14},{4,8},{6,10},{8,4},{10,6},{12,0},{14,2},{1,13},{3,15... | collective-permute-start | bytes 294920 | tf_op jit(solution)/shard_map/ppermute | solution.py:31
  42.9 1.2 %collective-permute-done.9.refs_0_ = s16[2,64,384]{2,1,0:T(8,128)(2,1)S(1)} collective-permute-done((s16[2,64,384]{2,1,0:T(8,128)(2,1)S(1)}, s16[2,64,384]{2,1,0:T(8,128)(2,1)S(1)}, u32[]{:S(2)}, u32[]{:S(2)}) %collective-permute-start.9) | collective-permute-done | bytes 98336 | tf_op jit(solution)/shard_map/ppermute | solution.py:31
  44.1 6.3 %collective-permute-done.10.refs_1_ = s16[2,64,384]{2,1,0:T(8,128)(2,1)S(1)} collective-permute-done((s16[2,64,384]{2,1,0:T(8,128)(2,1)S(1)}, s16[2,64,384]{2,1,0:T(8,128)(2,1)S(1)}, u32[]{:S(2)}, u32[]{:S(2)}) %collective-permute-start.10) | collective-permute-done | bytes 98336 | tf_op jit(solution)/shard_map/ppermute | solution.py:31
  50.6 0.4 half.4.half_ref
  51.0 0.8 collective-permute-done.12.drive_ref
  51.8 0.4 full.1.refs_2_
  52.3 1.6 %own_part.6.sum_ref = f32[64,2048]{1,0:T(8,128)S(1)} custom-call(bf16[64,2048]{1,0:T(8,128)(2,1)S(1)} %get-tuple-element.59.rates_ref.refs_1_, bf16[2048,2048]{1,0:T(8,128)(2,1)S(1)} %get-tuple-element.42.own_ref.weight_ref, f32[64,2048]{1,0:T(8,128)S(1)} %get-tuple-element.55.extra_ref), custom_call_target="tpu_custom_call" | custom-call | tf_op jit(solution)/shard_map/own_part/pallas_call | solution.py:280
  53.9 1.7 %step.7 = (f32[64,2048]{1,0:T(8,128)S(1)}, bf16[64,2048]{1,0:T(8,128)(2,1)S(1)}) custom-call(f32[64,2048]{1,0:T(8,128)S(1)} %own_part.6.sum_ref, f32[64,2048]{1,0:T(8,128)S(1)} %get-tuple-element.60.state_ref, f32[1,2048]{1,0:T(1,128)S(1)} %get-tuple-element.45.leak_ref, bf16[64,2048]{1,0:T(8,128)(2,1)S(1)} %collective-permute-done.7.refs_0_.refs_1_, ...), custom_call_target="tpu_custom_call" | custom-call | tf_op jit(solution)/shard_map/step/pallas_call | solution.py:351
  55.8 0.6 pick_half.4.refs_2_
  56.4 0.4 pick.4.refs_4_.refs_6_
  56.8 1.0 %collective-permute-start.15 = (bf16[2,64,384]{2,1,0:T(8,128)(2,1)S(1)}, bf16[2,64,384]{2,1,0:T(8,128)(2,1)S(1)}, u32[]{:S(2)}, u32[]{:S(2)}) collective-permute-start(bf16[2,64,384]{2,1,0:T(8,128)(2,1)S(1)} %pick.4.refs_4_.refs_6_), channel_id=1, source_target_pairs={{0,2},{2,0},{4,6},{6,4},{8,10},{10,8},{12,14},{14,12},{1,3},{3,1},... | collective-permute-start | bytes 294920 | tf_op jit(solution)/shard_map/ppermute | solution.py:31
  57.9 1.6 %own_part.7.sum_ref = f32[64,2048]{1,0:T(8,128)S(1)} custom-call(bf16[64,2048]{1,0:T(8,128)(2,1)S(1)} %get-tuple-element.67.rates_ref.refs_0_, bf16[2048,2048]{1,0:T(8,128)(2,1)S(1)} %get-tuple-element.42.own_ref.weight_ref, f32[64,2048]{1,0:T(8,128)S(1)} %get-tuple-element.55.extra_ref), custom_call_target="tpu_custom_call" | custom-call | tf_op jit(solution)/shard_map/own_part/pallas_call | solution.py:280
  59.5 1.7 %step.8 = (f32[64,2048]{1,0:T(8,128)S(1)}, bf16[64,2048]{1,0:T(8,128)(2,1)S(1)}) custom-call(f32[64,2048]{1,0:T(8,128)S(1)} %own_part.7.sum_ref, f32[64,2048]{1,0:T(8,128)S(1)} %get-tuple-element.68.state_ref, f32[1,2048]{1,0:T(1,128)S(1)} %get-tuple-element.45.leak_ref, bf16[64,2048]{1,0:T(8,128)(2,1)S(1)} %collective-permute-done.13.refs_0_, ...), custom_call_target="tpu_custom_call" | custom-call | tf_op jit(solution)/shard_map/step/pallas_call | solution.py:351
  61.3 0.4 partials.6
  62.1 1.7 %collective-permute-start.16 = (s16[2,64,384]{2,1,0:T(8,128)(2,1)S(1)}, s16[2,64,384]{2,1,0:T(8,128)(2,1)S(1)}, u32[]{:S(2)}, u32[]{:S(2)}) collective-permute-start(s16[2,64,384]{2,1,0:T(8,128)(2,1)S(1)} %get-tuple-element.76), channel_id=1, source_target_pairs={{0,4},{2,6},{4,0},{6,2},{8,12},{10,14},{12,8},{14,10},{1,5},{3,7},... | collective-permute-start | bytes 294920 | tf_op jit(solution)/shard_map/ppermute | solution.py:31
  63.8 1.0 %collective-permute-start.17 = (s16[2,64,384]{2,1,0:T(8,128)(2,1)S(1)}, s16[2,64,384]{2,1,0:T(8,128)(2,1)S(1)}, u32[]{:S(2)}, u32[]{:S(2)}) collective-permute-start(s16[2,64,384]{2,1,0:T(8,128)(2,1)S(1)} %get-tuple-element.77), channel_id=1, source_target_pairs={{0,8},{2,10},{4,12},{6,14},{8,0},{10,2},{12,4},{14,6},{1,9},{3,11}... | collective-permute-start | bytes 294920 | tf_op jit(solution)/shard_map/ppermute | solution.py:31
  64.8 1.8 %collective-permute-start.18 = (s16[2,64,384]{2,1,0:T(8,128)(2,1)S(1)}, s16[2,64,384]{2,1,0:T(8,128)(2,1)S(1)}, u32[]{:S(2)}, u32[]{:S(2)}) collective-permute-start(s16[2,64,384]{2,1,0:T(8,128)(2,1)S(1)} %get-tuple-element.78), channel_id=1, source_target_pairs={{0,12},{2,14},{4,8},{6,10},{8,4},{10,6},{12,0},{14,2},{1,13},{3,15... | collective-permute-start | bytes 294920 | tf_op jit(solution)/shard_map/ppermute | solution.py:31
  66.6 0.5 collective-permute-done.16.refs_0_
  67.1 7.4 %collective-permute-done.17.refs_1_ = s16[2,64,384]{2,1,0:T(8,128)(2,1)S(1)} collective-permute-done((s16[2,64,384]{2,1,0:T(8,128)(2,1)S(1)}, s16[2,64,384]{2,1,0:T(8,128)(2,1)S(1)}, u32[]{:S(2)}, u32[]{:S(2)}) %collective-permute-start.17) | collective-permute-done | bytes 98336 | tf_op jit(solution)/shard_map/ppermute | solution.py:31
  74.7 0.5 half.5.refs_2_
  75.1 1.6 %own_part.8.sum_ref = f32[64,2048]{1,0:T(8,128)S(1)} custom-call(bf16[64,2048]{1,0:T(8,128)(2,1)S(1)} %get-tuple-element.69.rates_ref.refs_1_, bf16[2048,2048]{1,0:T(8,128)(2,1)S(1)} %get-tuple-element.42.own_ref.weight_ref, f32[64,2048]{1,0:T(8,128)S(1)} %get-tuple-element.55.extra_ref), custom_call_target="tpu_custom_call" | custom-call | tf_op jit(solution)/shard_map/own_part/pallas_call | solution.py:280
  76.8 2.0 %step.9 = (f32[64,2048]{1,0:T(8,128)S(1)}, bf16[64,2048]{1,0:T(8,128)(2,1)S(1)}, f32[64,2048]{1,0:T(8,128)S(1)}) custom-call(f32[64,2048]{1,0:T(8,128)S(1)} %own_part.8.sum_ref, f32[64,2048]{1,0:T(8,128)S(1)} %get-tuple-element.70.state_ref, f32[1,2048]{1,0:T(1,128)S(1)} %get-tuple-element.45.leak_ref, ...), custom_call_target="tpu_custom_call" | custom-call | tf_op jit(solution)/shard_map/step/pallas_call | solution.py:351
  78.8 0.5 collective-permute-start.20
  79.4 0.4 pick_half.5.refs_2_
  79.8 1.6 %own_part.9.sum_ref = f32[64,2048]{1,0:T(8,128)S(1)} custom-call(bf16[64,2048]{1,0:T(8,128)(2,1)S(1)} %get-tuple-element.79.rates_ref.refs_8_, bf16[2048,2048]{1,0:T(8,128)(2,1)S(1)} %get-tuple-element.42.own_ref.weight_ref, f32[64,2048]{1,0:T(8,128)S(1)} %get-tuple-element.55.extra_ref), custom_call_target="tpu_custom_call" | custom-call | tf_op jit(solution)/shard_map/own_part/pallas_call | solution.py:280
  81.4 0.4 pick.5.refs_7_
  81.9 2.9 %last_step.1 = (f32[64,2048]{1,0:T(8,128)}, bf16[6,64,384]{2,1,0:T(8,128)(2,1)}) custom-call(f32[64,2048]{1,0:T(8,128)S(1)} %own_part.9.sum_ref, f32[64,2048]{1,0:T(8,128)S(1)} %get-tuple-element.80.state_ref, f32[1,2048]{1,0:T(1,128)S(1)} %get-tuple-element.45.leak_ref, bf16[64,2048]{1,0:T(8,128)(2,1)S(1)} %collective-permute-done.20.refs_0_.refs_9_, ...), custom_call_target="tpu_custom_call" | custom-call | tf_op jit(solution)/shard_map/last_step/pallas_call | solution.py:366
  (25 shorter events, 1.7 us)
Async XLA Ops:
  0.6 10.3 %collective-permute-start.1 = (bf16[6,64,384]{2,1,0:T(8,128)(2,1)}, bf16[6,64,384]{2,1,0:T(8,128)(2,1)S(1)}, u32[]{:S(2)}, u32[]{:S(2)}) collective-permute-start(bf16[6,64,384]{2,1,0:T(8,128)(2,1)} %history_far.1), channel_id=1, source_target_pairs={{0,2},{2,0},{4,6},{6,4},{8,10},{10,8},{12,14},{14,12},{1,3},{3,1},... | collective-permute-start | bytes 884744 | tf_op jit(solution)/shard_map/ppermute | solution.py:31
  4.8 18.8 %collective-permute-start = (bf16[64,2048]{1,0:T(8,128)(2,1)S(1)}, bf16[64,2048]{1,0:T(8,128)(2,1)S(1)}, u32[]{:S(2)}, u32[]{:S(2)}) collective-permute-start(bf16[64,2048]{1,0:T(8,128)(2,1)S(1)} %tanh_convert_fusion.rates_ref.refs_0_), channel_id=1, source_target_pairs={{0,1},{1,0},{2,3},{3,2},{4,5},{5,4},{6,7},{7,6},{8,9},{9,8},{10,11... | collective-permute-start | bytes 786440 | tf_op jit(solution)/shard_map/ppermute | solution.py:31
  11.5 4.7 %collective-permute-start.2 = (s16[2,64,384]{2,1,0:T(8,128)(2,1)S(1)}, s16[2,64,384]{2,1,0:T(8,128)(2,1)S(1)}, u32[]{:S(2)}, u32[]{:S(2)}) collective-permute-start(s16[2,64,384]{2,1,0:T(8,128)(2,1)S(1)} %get-tuple-element.49), channel_id=1, source_target_pairs={{0,4},{2,6},{4,0},{6,2},{8,12},{10,14},{12,8},{14,10},{1,5},{3,7},... | collective-permute-start | bytes 294920 | tf_op jit(solution)/shard_map/ppermute | solution.py:31
  13.4 10.1 %collective-permute-start.3 = (s16[2,64,384]{2,1,0:T(8,128)(2,1)S(1)}, s16[2,64,384]{2,1,0:T(8,128)(2,1)S(1)}, u32[]{:S(2)}, u32[]{:S(2)}) collective-permute-start(s16[2,64,384]{2,1,0:T(8,128)(2,1)S(1)} %get-tuple-element.50), channel_id=1, source_target_pairs={{0,8},{2,10},{4,12},{6,14},{8,0},{10,2},{12,4},{14,6},{1,9},{3,11}... | collective-permute-start | bytes 294920 | tf_op jit(solution)/shard_map/ppermute | solution.py:31
  16.0 7.5 %collective-permute-start.4 = (s16[2,64,384]{2,1,0:T(8,128)(2,1)S(1)}, s16[2,64,384]{2,1,0:T(8,128)(2,1)S(1)}, u32[]{:S(2)}, u32[]{:S(2)}) collective-permute-start(s16[2,64,384]{2,1,0:T(8,128)(2,1)S(1)} %get-tuple-element.51), channel_id=1, source_target_pairs={{0,12},{2,14},{4,8},{6,10},{8,4},{10,6},{12,0},{14,2},{1,13},{3,15... | collective-permute-start | bytes 294920 | tf_op jit(solution)/shard_map/ppermute | solution.py:31
  23.5 5.0 %collective-permute-start.5 = (bf16[128,384]{1,0:T(8,128)(2,1)S(1)}, bf16[128,384]{1,0:T(8,128)(2,1)S(1)}, u32[]{:S(2)}, u32[]{:S(2)}) collective-permute-start(bf16[128,384]{1,0:T(8,128)(2,1)S(1)} %drive.3.drive_ref), channel_id=1, source_target_pairs={{0,1},{1,0},{2,3},{3,2},{4,5},{5,4},{6,7},{7,6},{8,9},{9,8},{10,11... | collective-permute-start | bytes 294920 | tf_op jit(solution)/shard_map/ppermute | solution.py:31
  29.0 2.1 %collective-permute-start.6 = (bf16[64,2048]{1,0:T(8,128)(2,1)S(1)}, bf16[64,2048]{1,0:T(8,128)(2,1)S(1)}, u32[]{:S(2)}, u32[]{:S(2)}) collective-permute-start(bf16[64,2048]{1,0:T(8,128)(2,1)S(1)} %get-tuple-element.54.rates_ref.refs_0_), channel_id=1, source_target_pairs={{0,1},{1,0},{2,3},{3,2},{4,5},{5,4},{6,7},{7,6},{8,9},{9,8},{10,11... | collective-permute-start | bytes 786440 | tf_op jit(solution)/shard_map/ppermute | solution.py:31
  32.8 21.1 %collective-permute-start.7 = (bf16[64,2048]{1,0:T(8,128)(2,1)S(1)}, bf16[64,2048]{1,0:T(8,128)(2,1)S(1)}, u32[]{:S(2)}, u32[]{:S(2)}) collective-permute-start(bf16[64,2048]{1,0:T(8,128)(2,1)S(1)} %get-tuple-element.59.rates_ref.refs_1_), channel_id=1, source_target_pairs={{0,1},{1,0},{2,3},{3,2},{4,5},{5,4},{6,7},{7,6},{8,9},{9,8},{10,11... | collective-permute-start | bytes 786440 | tf_op jit(solution)/shard_map/ppermute | solution.py:31
  33.7 4.2 %collective-permute-start.8 = (bf16[1,64,384]{2,1,0:T(8,128)(2,1)S(1)}, bf16[1,64,384]{2,1,0:T(8,128)(2,1)S(1)}, u32[]{:S(2)}, u32[]{:S(2)}) collective-permute-start(bf16[1,64,384]{2,1,0:T(8,128)(2,1)S(1)} %pick.3.refs_2_.refs_5_), channel_id=1, source_target_pairs={{0,2},{2,0},{4,6},{6,4},{8,10},{10,8},{12,14},{14,12},{1,3},{3,1},... | collective-permute-start | bytes 147464 | tf_op jit(solution)/shard_map/ppermute | solution.py:31
  38.5 5.6 %collective-permute-start.9 = (s16[2,64,384]{2,1,0:T(8,128)(2,1)S(1)}, s16[2,64,384]{2,1,0:T(8,128)(2,1)S(1)}, u32[]{:S(2)}, u32[]{:S(2)}) collective-permute-start(s16[2,64,384]{2,1,0:T(8,128)(2,1)S(1)} %get-tuple-element.64), channel_id=1, source_target_pairs={{0,4},{2,6},{4,0},{6,2},{8,12},{10,14},{12,8},{14,10},{1,5},{3,7},... | collective-permute-start | bytes 294920 | tf_op jit(solution)/shard_map/ppermute | solution.py:31
  40.2 10.2 %collective-permute-start.10 = (s16[2,64,384]{2,1,0:T(8,128)(2,1)S(1)}, s16[2,64,384]{2,1,0:T(8,128)(2,1)S(1)}, u32[]{:S(2)}, u32[]{:S(2)}) collective-permute-start(s16[2,64,384]{2,1,0:T(8,128)(2,1)S(1)} %get-tuple-element.65), channel_id=1, source_target_pairs={{0,8},{2,10},{4,12},{6,14},{8,0},{10,2},{12,4},{14,6},{1,9},{3,11}... | collective-permute-start | bytes 294920 | tf_op jit(solution)/shard_map/ppermute | solution.py:31
  41.6 8.8 %collective-permute-start.11 = (s16[2,64,384]{2,1,0:T(8,128)(2,1)S(1)}, s16[2,64,384]{2,1,0:T(8,128)(2,1)S(1)}, u32[]{:S(2)}, u32[]{:S(2)}) collective-permute-start(s16[2,64,384]{2,1,0:T(8,128)(2,1)S(1)} %get-tuple-element.66), channel_id=1, source_target_pairs={{0,12},{2,14},{4,8},{6,10},{8,4},{10,6},{12,0},{14,2},{1,13},{3,15... | collective-permute-start | bytes 294920 | tf_op jit(solution)/shard_map/ppermute | solution.py:31
  50.5 1.4 %collective-permute-start.12 = (bf16[128,384]{1,0:T(8,128)(2,1)S(1)}, bf16[128,384]{1,0:T(8,128)(2,1)S(1)}, u32[]{:S(2)}, u32[]{:S(2)}) collective-permute-start(bf16[128,384]{1,0:T(8,128)(2,1)S(1)} %drive.4.drive_ref), channel_id=1, source_target_pairs={{0,1},{1,0},{2,3},{3,2},{4,5},{5,4},{6,7},{7,6},{8,9},{9,8},{10,11... | collective-permute-start | bytes 294920 | tf_op jit(solution)/shard_map/ppermute | solution.py:31
  55.6 3.9 %collective-permute-start.13 = (bf16[64,2048]{1,0:T(8,128)(2,1)S(1)}, bf16[64,2048]{1,0:T(8,128)(2,1)S(1)}, u32[]{:S(2)}, u32[]{:S(2)}) collective-permute-start(bf16[64,2048]{1,0:T(8,128)(2,1)S(1)} %get-tuple-element.67.rates_ref.refs_0_), channel_id=1, source_target_pairs={{0,1},{1,0},{2,3},{3,2},{4,5},{5,4},{6,7},{7,6},{8,9},{9,8},{10,11... | collective-permute-start | bytes 786440 | tf_op jit(solution)/shard_map/ppermute | solution.py:31
  56.8 5.1 %collective-permute-start.15 = (bf16[2,64,384]{2,1,0:T(8,128)(2,1)S(1)}, bf16[2,64,384]{2,1,0:T(8,128)(2,1)S(1)}, u32[]{:S(2)}, u32[]{:S(2)}) collective-permute-start(bf16[2,64,384]{2,1,0:T(8,128)(2,1)S(1)} %pick.4.refs_4_.refs_6_), channel_id=1, source_target_pairs={{0,2},{2,0},{4,6},{6,4},{8,10},{10,8},{12,14},{14,12},{1,3},{3,1},... | collective-permute-start | bytes 294920 | tf_op jit(solution)/shard_map/ppermute | solution.py:31
  61.2 15.6 %collective-permute-start.14 = (bf16[64,2048]{1,0:T(8,128)(2,1)S(1)}, bf16[64,2048]{1,0:T(8,128)(2,1)S(1)}, u32[]{:S(2)}, u32[]{:S(2)}) collective-permute-start(bf16[64,2048]{1,0:T(8,128)(2,1)S(1)} %get-tuple-element.69.rates_ref.refs_1_), channel_id=1, source_target_pairs={{0,1},{1,0},{2,3},{3,2},{4,5},{5,4},{6,7},{7,6},{8,9},{9,8},{10,11... | collective-permute-start | bytes 786440 | tf_op jit(solution)/shard_map/ppermute | solution.py:31
  62.1 5.0 %collective-permute-start.16 = (s16[2,64,384]{2,1,0:T(8,128)(2,1)S(1)}, s16[2,64,384]{2,1,0:T(8,128)(2,1)S(1)}, u32[]{:S(2)}, u32[]{:S(2)}) collective-permute-start(s16[2,64,384]{2,1,0:T(8,128)(2,1)S(1)} %get-tuple-element.76), channel_id=1, source_target_pairs={{0,4},{2,6},{4,0},{6,2},{8,12},{10,14},{12,8},{14,10},{1,5},{3,7},... | collective-permute-start | bytes 294920 | tf_op jit(solution)/shard_map/ppermute | solution.py:31
  63.8 10.7 %collective-permute-start.17 = (s16[2,64,384]{2,1,0:T(8,128)(2,1)S(1)}, s16[2,64,384]{2,1,0:T(8,128)(2,1)S(1)}, u32[]{:S(2)}, u32[]{:S(2)}) collective-permute-start(s16[2,64,384]{2,1,0:T(8,128)(2,1)S(1)} %get-tuple-element.77), channel_id=1, source_target_pairs={{0,8},{2,10},{4,12},{6,14},{8,0},{10,2},{12,4},{14,6},{1,9},{3,11}... | collective-permute-start | bytes 294920 | tf_op jit(solution)/shard_map/ppermute | solution.py:31
  64.8 9.7 %collective-permute-start.18 = (s16[2,64,384]{2,1,0:T(8,128)(2,1)S(1)}, s16[2,64,384]{2,1,0:T(8,128)(2,1)S(1)}, u32[]{:S(2)}, u32[]{:S(2)}) collective-permute-start(s16[2,64,384]{2,1,0:T(8,128)(2,1)S(1)} %get-tuple-element.78), channel_id=1, source_target_pairs={{0,12},{2,14},{4,8},{6,10},{8,4},{10,6},{12,0},{14,2},{1,13},{3,15... | collective-permute-start | bytes 294920 | tf_op jit(solution)/shard_map/ppermute | solution.py:31
  74.6 2.1 %collective-permute-start.19 = (bf16[128,384]{1,0:T(8,128)(2,1)S(1)}, bf16[128,384]{1,0:T(8,128)(2,1)S(1)}, u32[]{:S(2)}, u32[]{:S(2)}) collective-permute-start(bf16[128,384]{1,0:T(8,128)(2,1)S(1)} %drive.5.drive_ref), channel_id=1, source_target_pairs={{0,1},{1,0},{2,3},{3,2},{4,5},{5,4},{6,7},{7,6},{8,9},{9,8},{10,11... | collective-permute-start | bytes 294920 | tf_op jit(solution)/shard_map/ppermute | solution.py:31
  78.8 3.0 %collective-permute-start.20 = (bf16[64,2048]{1,0:T(8,128)(2,1)S(1)}, bf16[64,2048]{1,0:T(8,128)(2,1)S(1)}, u32[]{:S(2)}, u32[]{:S(2)}) collective-permute-start(bf16[64,2048]{1,0:T(8,128)(2,1)S(1)} %get-tuple-element.79.rates_ref.refs_8_), channel_id=1, source_target_pairs={{0,1},{1,0},{2,3},{3,2},{4,5},{5,4},{6,7},{7,6},{8,9},{9,8},{10,11... | collective-permute-start | bytes 786440 | tf_op jit(solution)/shard_map/ppermute | solution.py:31
